TPU v7x, 512 devices: a whole 4x8x8 slice. The times are simulated.
512 devices in a mesh: section: 2 (over z_lo), batch: 16 (over z_hi, x), tensor: 16 (over y, core).
Axes of the slice: x: 4, y: 8, z: 8 (z_hi: 4, z_lo: 2; z = z_hi * 2 + z_lo), core: 2. Of those that a mesh axis runs over, the one named last changes fastest.
Arguments:
- tokens: bfloat16 [4096, 4096], P('batch', ('section', 'tensor')), may hold values from -950 to 950, as said below
- nb_ids: int32 [128, 128], P('batch'), may hold values from 0 to 15999
- nb_index: int32 [64, 2], P('batch'), may hold values from 0 to 7
- table: bfloat16 [16000, 4096], P('batch', ('section', 'tensor')), may hold values from -950 to 950, as said below
- norm_gains: float32 [2, 4096], replicated, may hold values from 0.1 to 1.9
- projections: bfloat16 [2, 2, 4096, 4096], P(None, None, None, ('section', 'tensor')), may hold values from -0.5 to 0.5
Outputs:
- mixed: bfloat16 [4096, 4096], P('batch', ('section', 'tensor'))
Inputs may be any that keep to these rules, and one draw needn't show every extreme that they name: tokens: entries of order one to some hundreds, of both signs. table: entries of order one to some hundreds, of both signs.
All inputs are finite; a program needn't handle non-finite values.
Results may differ from a plain program's by a relative error of at most 0.019.
Values may be sent and summed in bfloat16 or wider, within the bound.
No kernel may reach another device: no remote copies, remote signals or barrier semaphores. Data moves between devices by JAX's collectives and lax.ppermute only.
A program may use at most 64 MiB of HBM per device.

v0:
```python
import functools
import math

import jax
import jax.numpy as jnp
from jax import lax
from jax.experimental import pallas as pl
from jax.experimental.pallas import tpu as pltpu
from jax.sharding import Mesh
from jax.sharding import PartitionSpec as P

HEAD_DIM = 128
SPAN = 64
ROWS = 72
SHARD = 1000
HALF = 512
ROWS_IN = HALF + 128
EPS = 1e-06
SCALE = math.log2(math.e) / math.sqrt(HEAD_DIM)
F32 = jnp.float32
BF16 = jnp.bfloat16


def dot(a, b, dims):
    return lax.dot_general(a, b, (dims, ((), ())), preferred_element_type=F32)


def diagonal(shape):
    row = lax.broadcasted_iota(jnp.int32, shape, len(shape) - 2)
    lane = lax.broadcasted_iota(jnp.int32, shape, len(shape) - 1)
    return row == lane % SPAN


def sums_to_row(column):
    row = jnp.sum(jnp.where(diagonal((SPAN, 128)), column, 0.0), axis=0, keepdims=True)
    upper = row.astype(BF16).astype(F32)
    lane = lax.broadcasted_iota(jnp.int32, (1, 128), 1)
    return jnp.where(lane < SPAN, upper, row - upper)


def row_to_sums(row):
    return jnp.sum(jnp.where(diagonal((SPAN, 128)), row, 0.0), axis=1, keepdims=True)


def column_to_row(column):
    square = (128, 128)
    same = lax.broadcasted_iota(jnp.int32, square, 0) == lax.broadcasted_iota(jnp.int32, square, 1)
    return jnp.sum(jnp.where(same, column, 0.0), axis=0, keepdims=True)


def row_to_column(row):
    square = (128, 128)
    same = lax.broadcasted_iota(jnp.int32, square, 0) == lax.broadcasted_iota(jnp.int32, square, 1)
    return jnp.sum(jnp.where(same, row, 0.0), axis=1, keepdims=True)


def far_kernel(source_ref, b0_ref, b1_ref, b2_ref, b3_ref, b4_ref, gain_ref, w0_ref, w1_ref, lhs_ref, squares_ref, send_ref):
    square = jnp.zeros((ROWS_IN, 128), F32)
    pieces = [b0_ref, b1_ref]
    for ref in (b2_ref, b3_ref, b4_ref):
        pieces += [ref.at[0], ref.at[1]]
    for k, ref in enumerate(pieces):
        source = source_ref[k]
        for i in range(2):
            wide = ref[i].astype(F32)
            square = square + wide * wide
            gain = gain_ref[source, i]
            lanes = slice(i * 128, (i + 1) * 128)
            lhs_ref[source, :HALF, lanes] = (wide[:HALF] * gain[0:1]).astype(BF16)
            lhs_ref[source, HALF:, lanes] = (wide[HALF:] * gain[1:2]).astype(BF16)
    sums = jnp.sum(square, axis=1, keepdims=True)
    tail = [column_to_row(sums[k * 128 : (k + 1) * 128]) for k in range(5)]
    squares = jnp.concatenate(tail + [jnp.zeros((3, 128), F32)], axis=0)
    squares_ref[...] = squares
    upper = squares.astype(BF16)
    lower = (squares - upper.astype(F32)).astype(BF16)
    for i in range(4):
        send_ref[i, HALF + 64 :, :] = lower if i == 1 else upper
    lhs = jnp.concatenate([lhs_ref[y] for y in range(8)], axis=1)
    for m, ref in enumerate((w0_ref, w1_ref)):
        pair = jnp.concatenate([ref[0], ref[1]], axis=1)
        both = dot(lhs[:HALF], pair, ((1,), (0,)))
        query = dot(lhs[HALF:], ref[2], ((1,), (0,)))
        for i in range(2):
            send_ref[2 * m + i, :HALF, :] = both[:, i * 128 : (i + 1) * 128].astype(BF16)
            send_ref[2 * m + i, HALF : HALF + 64, :] = query[i * 64 : (i + 1) * 64].astype(BF16)


def project_far(source, blocks, gains, weights):
    vmem = pl.BlockSpec(memory_space=pltpu.VMEM)
    return pl.pallas_call(
        far_kernel,
        in_specs=[pl.BlockSpec(memory_space=pltpu.SMEM)] + [vmem] * 8,
        out_specs=[vmem] * 3,
        out_shape=[
            jax.ShapeDtypeStruct((8, ROWS_IN, 256), BF16),
            jax.ShapeDtypeStruct((8, 128), F32),
            jax.ShapeDtypeStruct((4, HALF + 72, 128), BF16),
        ],
        name="project_far",
    )(source, *blocks, gains, *weights)


def near_kernel(lhs_ref, w0_ref, w1_ref, keep_ref, keep_q_ref):
    lhs = jnp.concatenate([lhs_ref[y] for y in range(8)], axis=1)
    for m, ref in enumerate((w0_ref, w1_ref)):
        pair = jnp.concatenate([ref[0], ref[1]], axis=1)
        both = dot(lhs[:HALF], pair, ((1,), (0,)))
        keep_ref[m, 0] = both[:, :128]
        keep_ref[m, 1] = both[:, 128:]
        keep_q_ref[m] = dot(lhs[HALF:], ref[2], ((1,), (0,)))


def project_near(lhs, weights):
    vmem = pl.BlockSpec(memory_space=pltpu.VMEM)
    return pl.pallas_call(
        near_kernel,
        in_specs=[vmem] * 3,
        out_specs=[vmem] * 2,
        out_shape=[
            jax.ShapeDtypeStruct((2, 2, HALF, 128), F32),
            jax.ShapeDtypeStruct((2, 128, 128), F32),
        ],
        name="project_near",
    )(lhs, *weights)


def finish_kernel(source_ref, keep_ref, keep_q_ref, squares_ref, other_ref, count_ref, own_ref, give_ref, q_ref):
    core = source_ref[8]
    ours = squares_ref[...]
    theirs = other_ref[0, HALF + 64 :, :].astype(F32) + other_ref[1, HALF + 64 :, :].astype(F32)
    rate = lax.rsqrt((ours + theirs) * (1.0 / 4096) + EPS)
    for m, ref in enumerate((own_ref, give_ref)):
        head = core ^ m
        for k in range(4):
            rows = slice(k * 128, (k + 1) * 128)
            column = row_to_column(rate[k : k + 1])
            for i in range(2):
                total = keep_ref[m, i, rows] + other_ref[2 * m + i, rows, :].astype(F32)
                ref[i, rows] = (total * column).astype(BF16)
        column = row_to_column(rate[4:5])
        for i in range(2):
            rows = slice(i * 64, (i + 1) * 64)
            total = keep_q_ref[m, rows] + other_ref[2 * m + i, HALF : HALF + 64, :].astype(F32)
            value = (total * column[rows]).astype(BF16)
            for z in range(4):
                q_ref[z, head, rows] = value
        for z in range(4):
            q_ref[z, m, 128:] = count_ref[z]


def finish(source, keep, keep_q, squares, other, counts):
    vmem = pl.BlockSpec(memory_space=pltpu.VMEM)
    half = jax.ShapeDtypeStruct((2, HALF, 128), BF16)
    return pl.pallas_call(
        finish_kernel,
        in_specs=[pl.BlockSpec(memory_space=pltpu.SMEM)] + [vmem] * 5,
        out_specs=[vmem] * 3,
        out_shape=[half, half, jax.ShapeDtypeStruct((4, 2, 192, 128), BF16)],
        name="finish",
    )(source, keep, keep_q, squares, other, counts)


def partial(order_ref, first, queries, blocks, count_ref, expo_ref):
    total = jnp.zeros((4 * SPAN, 128), F32)
    for k, block in enumerate(blocks):
        lanes = slice(k * HALF, (k + 1) * HALF)
        bias = jnp.log2(count_ref[0, order_ref[first + k]].astype(F32))
        spread = jnp.broadcast_to(bias[:, None, :], (4, SPAN, HALF)).reshape(4 * SPAN, HALF)
        scores = dot(queries, block[0], ((1,), (1,)))
        expo = jnp.exp2(scores * SCALE + spread)
        expo_ref[:, lanes] = expo
        for i in range(HALF // 128):
            total = total + expo[:, i * 128 : (i + 1) * 128]
    total = jnp.sum(total, axis=1, keepdims=True)
    inverse = jnp.where(total > 0.0, 1.0 / total, 0.0)
    weights = (expo_ref[...] * inverse).astype(BF16)
    values = jnp.concatenate([block[1] for block in blocks], axis=0)
    return dot(weights, values, ((1,), (0,))), total


def near_attend_kernel(order_ref, q_ref, near_ref, next_ref, count_ref, part_ref, total_ref, expo_ref):
    queries = jnp.concatenate([q_ref[0, 0], q_ref[0, 1]], axis=0)
    blocks = [near_ref.at[0], near_ref.at[1], next_ref.at[0], next_ref.at[1]]
    part, total = partial(order_ref, 0, queries, blocks, count_ref, expo_ref)
    part_ref[...] = part
    total_ref[...] = jnp.broadcast_to(total, (4 * SPAN, 128))


def far_attend_kernel(order_ref, q_ref, far_ref, count_ref, part_ref, total_ref, out_ref, expo_ref):
    queries = jnp.concatenate([q_ref[0, 0], q_ref[0, 1]], axis=0)
    blocks = [far_ref.at[k, i] for k in range(2) for i in range(2)]
    part, total = partial(order_ref, 4, queries, blocks, count_ref, expo_ref)
    before = total_ref[:, 0:1]
    both = total + before
    inverse = jnp.where(both > 0.0, 1.0 / both, 0.0)
    part = (part * (total * inverse) + part_ref[...] * (before * inverse)).astype(BF16)
    for j in range(4):
        rows = slice(j * SPAN, (j + 1) * SPAN)
        out_ref[j // 2, 0, j % 2, :SPAN, :] = part[rows]
        tail = jnp.broadcast_to(sums_to_row(both[rows]), (ROWS - SPAN, 128))
        out_ref[j // 2, 0, j % 2, SPAN:, :] = tail.astype(BF16)


QUERY_SPEC = pl.BlockSpec((1, 2, 128, HEAD_DIM), lambda i, *_: (i, 0, 0, 0))
COUNT_SPEC = pl.BlockSpec((1, 8, 4, HALF), lambda i, *_: (i, 0, 0, 0))
PART_SPEC = pl.BlockSpec((4 * SPAN, HEAD_DIM), lambda i, *_: (i, 0))


def attend_near(order, queries, near, following, counts):
    block = pl.BlockSpec((2, 2, HALF, HEAD_DIM), lambda i, *_: (0, 0, 0, 0))
    return pl.pallas_call(
        near_attend_kernel,
        grid_spec=pltpu.PrefetchScalarGridSpec(
            num_scalar_prefetch=1,
            grid=(4,),
            in_specs=[QUERY_SPEC, block, block, COUNT_SPEC],
            out_specs=[PART_SPEC, PART_SPEC],
            scratch_shapes=[pltpu.VMEM((4 * SPAN, 4 * HALF), F32)],
        ),
        out_shape=[jax.ShapeDtypeStruct((16 * SPAN, HEAD_DIM), F32)] * 2,
        name="attend_near",
    )(order, queries, near, following, counts)


def attend_far(order, queries, beyond, counts, part, total):
    return pl.pallas_call(
        far_attend_kernel,
        grid_spec=pltpu.PrefetchScalarGridSpec(
            num_scalar_prefetch=1,
            grid=(4,),
            in_specs=[
                QUERY_SPEC,
                pl.BlockSpec((2, 2, 2, HALF, HEAD_DIM), lambda i, *_: (0, 0, 0, 0, 0)),
                COUNT_SPEC,
                PART_SPEC,
                PART_SPEC,
            ],
            out_specs=pl.BlockSpec((2, 1, 2, ROWS, HEAD_DIM), lambda i, *_: (0, i, 0, 0, 0)),
            scratch_shapes=[pltpu.VMEM((4 * SPAN, 4 * HALF), F32)],
        ),
        out_shape=jax.ShapeDtypeStruct((2, 4, 2, ROWS, HEAD_DIM), BF16),
        name="attend_far",
    )(order, queries, beyond, counts, part, total)


def merge(parts):
    sums = [row_to_sums(p[SPAN : SPAN + 1, :].astype(F32)) for p in parts]
    total = functools.reduce(jnp.add, sums)
    mixed = functools.reduce(
        jnp.add, [p[:SPAN, :].astype(F32) * (s / total) for p, s in zip(parts, sums)]
    )
    return mixed, total


def mix_kernel(place_ref, parts_ref, w0_ref, w1_ref, w2_ref, w3_ref, out_ref, att_ref):
    @pl.when(pl.program_id(0) == 0)
    def _():
        for s in range(2):
            for c in range(2):
                mixed, _ = merge([parts_ref[s, z, c] for z in range(4)])
                att_ref[2 * s + c] = mixed.astype(BF16)

    place = place_ref[0]
    acc = None
    for k, ref in enumerate((w0_ref, w1_ref, w2_ref, w3_ref)):
        term = dot(att_ref[place ^ k], ref[...], ((1,), (1,)))
        acc = term if acc is None else acc + term
    for d in range(out_ref.shape[0]):
        out_ref[d] = acc[:, d * HEAD_DIM : (d + 1) * HEAD_DIM].astype(BF16)


def mix(place, parts, weights):
    step = 8
    weight = pl.BlockSpec((step * HEAD_DIM, HEAD_DIM), lambda i, *_: (i, 0))
    return pl.pallas_call(
        mix_kernel,
        grid_spec=pltpu.PrefetchScalarGridSpec(
            num_scalar_prefetch=1,
            grid=(32 // step,),
            in_specs=[
                pl.BlockSpec((2, 4, 2, ROWS, HEAD_DIM), lambda i, *_: (0, 0, 0, 0, 0)),
                weight,
                weight,
                weight,
                weight,
            ],
            out_specs=pl.BlockSpec((step, SPAN, HEAD_DIM), lambda i, *_: (i, 0, 0)),
            scratch_shapes=[pltpu.VMEM((4, SPAN, HEAD_DIM), BF16)],
        ),
        out_shape=jax.ShapeDtypeStruct((32, SPAN, HEAD_DIM), BF16),
        name="mix",
    )(place, parts, *weights)


def swap(value, axis):
    return lax.ppermute(value, axis, [(0, 1), (1, 0)])


def multiplicities(nb_ids, nb_index):
    place = nb_ids % SHARD
    place = jnp.where(place < HALF, place, place + (2 * HALF - SHARD))
    upper = (nb_ids // SHARD) * 32 + place // 32
    one_upper = (upper[:, :, None] == jnp.arange(512)).astype(BF16)
    one_lower = ((place % 32)[:, :, None] == jnp.arange(32)).astype(BF16)
    per_block = jnp.einsum("nip,niq->npq", one_upper, one_lower, preferred_element_type=F32)
    pick = jnp.sum((nb_index[:, :, None] == jnp.arange(8)).astype(F32), axis=1)
    counts = jnp.einsum(
        "gn,npq->gpq", pick.astype(BF16), per_block.astype(BF16), preferred_element_type=F32
    )
    return counts.astype(BF16)


def half_of(table, tokens, core):
    rows = lax.dynamic_slice_in_dim(table, core * (SHARD - HALF), HALF)
    return jnp.concatenate([rows, lax.dynamic_slice_in_dim(tokens, core * 128, 128)], axis=0)


def pairs(size, turn):
    out = []
    for place in range(size):
        for core in range(2):
            spot = (place - core) % size
            other = spot ^ 1 if turn == 0 else spot + (1 if spot % 2 else -1)
            out.append((2 * place + core, 2 * ((other + core) % size) + core))
    return out


def exchange(value, axis, size, turn):
    return lax.ppermute(value, (axis, "c"), pairs(size, turn))


def after(value, *others):
    return lax.optimization_barrier((value, *others))[0]


def feature_rows(projections, section):
    start = section * 2048
    encoder = lax.dynamic_slice(projections, (0, 0, start, 0), (1, 2, 2048, 128))
    decoder = lax.dynamic_slice(projections, (1, 0, start, 0), (1, 1, 2048, 128))
    return jnp.concatenate([encoder[0], decoder[0]], axis=0)


def step(tokens, nb_ids, nb_index, table, norm_gains, projections):
    core, section, here = lax.axis_index("c"), lax.axis_index("s"), lax.axis_index("y")
    column = lax.axis_index("x")

    own = half_of(table, tokens, core)
    got = swap(half_of(table, tokens, 1 - core), "c")
    across = swap(feature_rows(projections, 1 - section), "s")
    chunk = jnp.where(core == 0, jnp.stack([own, got]), jnp.stack([got, own]))
    first = exchange(chunk, "y", 8, 0)
    second = exchange(jnp.stack([chunk, first]), "y", 8, 1)
    mine = after(feature_rows(projections, section), first)
    beside = swap(mine, "c")

    gains = lax.dynamic_slice_in_dim(norm_gains, section * 2048, 2048, axis=1)
    gains = gains.reshape(2, 8, 2, 128).transpose(1, 2, 0, 3)
    counts = multiplicities(nb_ids, nb_index).reshape(2, 2, 4, 4 * 1024)
    counts = lax.dynamic_index_in_dim(counts, core, 0, keepdims=False)
    counts = counts.transpose(1, 0, 2).reshape(4, 64, 128)
    sign = 1 - 2 * ((here + core) % 2)
    offsets = jnp.array([0, 1, -1, -2, 2, 3, -3, -4], jnp.int32)
    source = jnp.concatenate([(here + sign * offsets) % 8, core.reshape(1)]).astype(jnp.int32)
    sign = 1 - 2 * ((column + core) % 2)
    origin = (column + sign * offsets[:4]) % 4
    order = (2 * origin[:, None] + jnp.stack([core, 1 - core])[None]).reshape(8).astype(jnp.int32)

    third = exchange(second, "y", 8, 0)
    third, gains, counts, source, order = lax.optimization_barrier(
        (third, gains, counts, source, order)
    )
    fourth = exchange(third, "y", 8, 1)
    diagonal = swap(after(across, third), "c")

    lhs, squares, send = project_far(
        source, (chunk, first, second, third, fourth), gains, (across, diagonal)
    )
    other = swap(send, "s")
    keep, keep_q = project_near(lhs, (mine, beside))
    near, give, queries = finish(source, keep, keep_q, squares, other, counts)
    queries = queries.reshape(8, 192, 128)
    queries = lax.all_to_all(queries, ("zh", "c"), 0, 0)
    near = jnp.stack([near, swap(give, "c")])
    following = exchange(near, "x", 4, 0)
    following = after(following, queries)
    beyond = exchange(jnp.stack([near, following]), "x", 4, 1)
    queries = queries.reshape(4, 2, 192, 128)
    counts = queries[:, :, 128:].reshape(4, 2, 2, 8, HALF).transpose(0, 3, 1, 2, 4)
    counts = counts.reshape(4, 8, 4, HALF)

    wo = after(projections[1, 1], queries)
    wo_section = swap(wo, "s")
    wo_beside = swap(wo, "c")

    part, total = attend_near(order, queries, near, following, counts)
    parts = attend_far(order, queries, beyond, counts, part, total)
    wo_diagonal = swap(after(wo_section, parts), "c")
    parts = lax.all_to_all(parts.reshape(16, ROWS, HEAD_DIM), ("s", "zh", "c"), 0, 0)
    place = (section * 2 + core).astype(jnp.int32).reshape(1)
    weights = (wo, wo_beside, wo_section, wo_diagonal)
    out = mix(place, parts.reshape(2, 4, 2, ROWS, HEAD_DIM), weights)
    out = lax.all_to_all(out, ("s", "y", "c"), 0, 0)
    out = jnp.sum(out.reshape(2, 8, 2, SPAN, HEAD_DIM).astype(F32), axis=1)
    return out.astype(BF16).reshape(4 * SPAN, HEAD_DIM)


def solution(mesh):
    fine = Mesh(mesh.devices.reshape(2, 4, 4, 8, 2), ("s", "zh", "x", "y", "c"))
    batch, cols = ("zh", "x"), ("s", "y", "c")
    return jax.shard_map(
        step,
        mesh=fine,
        in_specs=(
            P(batch, cols),
            P(batch, None),
            P(batch, None),
            P(batch, cols),
            P(),
            P(None, None, None, cols),
        ),
        out_specs=P(batch, cols),
        check_vma=False,
    )
```

profile of v0, /device:TPU:1, one launch (start us, length us, event | category | flops | bytes accessed | tf_op | source)
XLA Modules:
  0.0 199.0 jit_solution(408830091065492670)
XLA Ops:
  0.0 0.8 constant_dynamic-slice_fusion.3
  0.8 1.0 constant_dynamic-slice_fusion.4
  1.8 8.7 %collective-permute-start = (bf16[640,128]{1,0:T(8,128)(2,1)S(1)}, bf16[640,128]{1,0:T(8,128)(2,1)S(1)}, u32[]{:S(2)}, u32[]{:S(2)}) collective-permute-start(bf16[640,128]{1,0:T(8,128)(2,1)S(1)} %pad_maximum_fusion.6), channel_id=1, source_target_pairs={{0,1},{1,0},{2,3},{3,2},{4,5},{5,4},{6,7},{7,6},{8,9},{9,8},{10,11... | collective-permute-start | bytes 491528 | tf_op jit(solution)/shard_map/ppermute | solution.py:297
  10.6 1.3 dynamic-slice_bitcast_fusion.2
  11.9 1.7 dynamic-slice_bitcast_fusion
  13.5 0.0 copy-start.13
  13.6 1.3 pad_maximum_fusion
  14.9 1.9 collective-permute-start.5
  16.8 0.5 fusion.1
  17.4 0.1 convert_reduce_fusion
  17.6 1.9 collective-permute-start.1
  19.5 0.3 convolution_convert_fusion
  19.8 0.0 copy-start.16
  19.8 0.3 copy.19
  20.1 0.0 copy-start.15
  20.1 1.2 reshape.110
  21.3 0.1 pad_add_fusion.1
  21.4 5.2 %collective-permute-done.1.b1_ref = bf16[2,640,128]{2,1,0:T(8,128)(2,1)S(1)} collective-permute-done((bf16[2,640,128]{2,1,0:T(8,128)(2,1)S(1)}, bf16[2,640,128]{2,1,0:T(8,128)(2,1)S(1)}, u32[]{:S(2)}, u32[]{:S(2)}) %collective-permute-start.1) | collective-permute-done | bytes 327712 | tf_op jit(solution)/shard_map/ppermute | solution.py:330
  26.6 0.1 pad_maximum_fusion.3
  26.7 1.9 collective-permute-start.2
  28.7 9.7 %collective-permute-done.2.b2_ref = bf16[2,2,640,128]{3,2,1,0:T(8,128)(2,1)S(1)} collective-permute-done((bf16[2,2,640,128]{3,2,1,0:T(8,128)(2,1)S(1)}, bf16[2,2,640,128]{3,2,1,0:T(8,128)(2,1)S(1)}, u32[]{:S(2)}, u32[]{:S(2)}) %collective-permute-start.2) | collective-permute-done | bytes 655392 | tf_op jit(solution)/shard_map/ppermute | solution.py:330
  38.4 1.9 collective-permute-start.3
  40.3 0.1 broadcast_add_fusion
  40.4 0.1 copy.20
  40.5 0.7 reshape.111.count_ref
  41.1 0.6 add.128.order_ref
  41.8 0.6 pad_add_fusion.source_ref
  42.3 0.6 constant_dynamic-slice_fusion
  42.9 8.1 %collective-permute-done.3.b3_ref = bf16[2,2,640,128]{3,2,1,0:T(8,128)(2,1)} collective-permute-done((bf16[2,2,640,128]{3,2,1,0:T(8,128)(2,1)S(1)}, bf16[2,2,640,128]{3,2,1,0:T(8,128)(2,1)}, u32[]{:S(2)}, u32[]{:S(2)}) %collective-permute-start.3) | collective-permute-done | bytes 655392 | tf_op jit(solution)/shard_map/ppermute | solution.py:330
  51.0 2.0 %collective-permute-done.5.w0_ref = bf16[3,2048,128]{2,1,0:T(8,128)(2,1)} collective-permute-done((bf16[3,2048,128]{2,1,0:T(8,128)(2,1)}, bf16[3,2048,128]{2,1,0:T(8,128)(2,1)}, u32[]{:S(2)}, u32[]{:S(2)}) %collective-permute-start.5) | collective-permute-done | bytes 1572896 | tf_op jit(solution)/shard_map/ppermute | solution.py:297
  53.0 2.8 %collective-permute-start.6 = (bf16[3,2048,128]{2,1,0:T(8,128)(2,1)}, bf16[3,2048,128]{2,1,0:T(8,128)(2,1)}, u32[]{:S(2)}, u32[]{:S(2)}) collective-permute-start(bf16[3,2048,128]{2,1,0:T(8,128)(2,1)} %collective-permute-done.5.w0_ref), channel_id=1, source_target_pairs={{0,1},{1,0},{2,3},{3,2},{4,5},{5,4},{6,7},{7,6},{8,9},{9,8},{10,11... | collective-permute-start | bytes 4718600 | tf_op jit(solution)/shard_map/ppermute | solution.py:297
  55.8 0.1 pad_maximum_fusion.1.w0_ref
  56.0 1.9 collective-permute-start.7
  57.9 1.9 collective-permute-start.4
  59.8 10.0 %collective-permute-done.4.b4_ref = bf16[2,2,640,128]{3,2,1,0:T(8,128)(2,1)} collective-permute-done((bf16[2,2,640,128]{3,2,1,0:T(8,128)(2,1)}, bf16[2,2,640,128]{3,2,1,0:T(8,128)(2,1)}, u32[]{:S(2)}, u32[]{:S(2)}) %collective-permute-start.4) | collective-permute-done | bytes 655392 | tf_op jit(solution)/shard_map/ppermute | solution.py:330
  69.9 6.0 %project_far.1 = (bf16[8,640,256]{2,1,0:T(8,128)(2,1)}, f32[8,128]{1,0:T(8,128)}, bf16[4,584,128]{2,1,0:T(8,128)(2,1)}) custom-call(s32[9]{0:T(128)} %pad_add_fusion.source_ref, bf16[2,640,128]{2,1,0:T(8,128)(2,1)} %copy-done.8, bf16[2,640,128]{2,1,0:T(8,128)(2,1)} %copy-done.7, bf16[2,2,640,128]{3,2,1,0:T(8,128)(2,1)} %copy-done.11, ...), custom_call_target="tpu_custom_call" | custom-call | tf_op jit(solution)/shard_map/project_far/pallas_call | solution.py:91
  75.8 2.6 %collective-permute-start.8 = (bf16[4,584,128]{2,1,0:T(8,128)(2,1)}, bf16[4,584,128]{2,1,0:T(8,128)(2,1)}, u32[]{:S(2)}, u32[]{:S(2)}) collective-permute-start(bf16[4,584,128]{2,1,0:T(8,128)(2,1)} %get-tuple-element.35), channel_id=1, source_target_pairs={{0,256},{256,0},{1,257},{257,1},{2,258},{258,2},{3,259},{259,3},{4... | collective-permute-start | bytes 1794056 | tf_op jit(solution)/shard_map/ppermute | solution.py:297
  78.5 1.1 copy-done.6
  79.6 5.2 %project_near.1 = (f32[2,2,512,128]{3,2,1,0:T(8,128)}, f32[2,128,128]{2,1,0:T(8,128)}) custom-call(bf16[8,640,256]{2,1,0:T(8,128)(2,1)} %get-tuple-element.30.lhs_ref, bf16[3,2048,128]{2,1,0:T(8,128)(2,1)} %copy-done.1, bf16[3,2048,128]{2,1,0:T(8,128)(2,1)} %copy-done.6), custom_call_target="tpu_custom_call" | custom-call | tf_op jit(solution)/shard_map/project_near/pallas_call | solution.py:116
  84.8 5.7 %collective-permute-done.8.other_ref = bf16[4,584,128]{2,1,0:T(8,128)(2,1)} collective-permute-done((bf16[4,584,128]{2,1,0:T(8,128)(2,1)}, bf16[4,584,128]{2,1,0:T(8,128)(2,1)}, u32[]{:S(2)}, u32[]{:S(2)}) %collective-permute-start.8) | collective-permute-done | bytes 598048 | tf_op jit(solution)/shard_map/ppermute | solution.py:297
  90.5 2.7 %finish.1 = (bf16[2,512,128]{2,1,0:T(8,128)(2,1)}, bf16[2,512,128]{2,1,0:T(8,128)(2,1)}, bf16[4,2,192,128]{3,2,1,0:T(8,128)(2,1)}) custom-call(s32[9]{0:T(128)} %pad_add_fusion.source_ref, f32[2,2,512,128]{3,2,1,0:T(8,128)} %get-tuple-element.32.keep_ref, f32[2,128,128]{2,1,0:T(8,128)} %get-tuple-element.33.keep_q_ref, ...), custom_call_target="tpu_custom_call" | custom-call | tf_op jit(solution)/shard_map/finish/pallas_call | solution.py:155
  93.2 5.3 %collective-permute-start.9 = (bf16[2,512,128]{2,1,0:T(8,128)(2,1)}, bf16[2,512,128]{2,1,0:T(8,128)(2,1)S(1)}, u32[]{:S(2)}, u32[]{:S(2)}) collective-permute-start(bf16[2,512,128]{2,1,0:T(8,128)(2,1)} %get-tuple-element.39), channel_id=1, source_target_pairs={{0,1},{1,0},{2,3},{3,2},{4,5},{5,4},{6,7},{7,6},{8,9},{9,8},{10,11... | collective-permute-start | bytes 786440 | tf_op jit(solution)/shard_map/ppermute | solution.py:297
  98.5 5.8 %all-to-all-start = ((bf16[8,192,128]{2,1,0:T(8,128)(2,1)}), bf16[8,192,128]{2,1,0:T(8,128)(2,1)S(1)}, u32[]{:S(2)}, u32[]{:S(2)}) async-start(bf16[8,192,128]{2,1,0:T(8,128)(2,1)} %bitcast.57), calls=%async_computation | async-start | bytes 786432 | tf_op jit(solution)/shard_map/all_to_all | solution.py:383
  104.3 1.0 fusion.16
  105.3 4.4 %collective-permute-start.10 = (bf16[2,2,512,128]{3,2,1,0:T(8,128)(2,1)S(1)}, bf16[2,2,512,128]{3,2,1,0:T(8,128)(2,1)S(1)}, u32[]{:S(2)}, u32[]{:S(2)}) collective-permute-start(bf16[2,2,512,128]{3,2,1,0:T(8,128)(2,1)S(1)} %get-tuple-element.50.near_ref), channel_id=1, source_target_pairs={{0,16},{1,49},{16,0},{17,33},{32,48},{33,17},{48,32},{49,1},{2,18}... | collective-permute-start | bytes 1572872 | tf_op jit(solution)/shard_map/ppermute | solution.py:330
  109.7 1.3 slice_bitcast_fusion.w0_ref
  111.0 5.9 %all-to-all-done = bf16[8,192,128]{2,1,0:T(8,128)(2,1)S(1)} async-done(((bf16[8,192,128]{2,1,0:T(8,128)(2,1)}), bf16[8,192,128]{2,1,0:T(8,128)(2,1)S(1)}, u32[]{:S(2)}, u32[]{:S(2)}) %all-to-all-start) | async-done | bytes 393248 | tf_op jit(solution)/shard_map/all_to_all | solution.py:383
  117.0 1.2 pad_maximum_fusion.2
  118.2 3.1 %collective-permute-start.11 = (bf16[2,2,2,512,128]{4,3,2,1,0:T(8,128)(2,1)}, bf16[2,2,2,512,128]{4,3,2,1,0:T(8,128)(2,1)}, u32[]{:S(2)}, u32[]{:S(2)}) collective-permute-start(bf16[2,2,2,512,128]{4,3,2,1,0:T(8,128)(2,1)} %pad_maximum_fusion.2), channel_id=1, source_target_pairs={{0,48},{1,17},{16,32},{17,1},{32,16},{33,49},{48,0},{49,33},{2,50}... | collective-permute-start | bytes 3145736 | tf_op jit(solution)/shard_map/ppermute | solution.py:330
  121.3 1.9 collective-permute-start.13
  123.2 6.9 %collective-permute-start.12 = (bf16[4096,128]{1,0:T(8,128)(2,1)S(1)}, bf16[4096,128]{1,0:T(8,128)(2,1)}, u32[]{:S(2)}, u32[]{:S(2)}) collective-permute-start(bf16[4096,128]{1,0:T(8,128)(2,1)S(1)} %slice_bitcast_fusion.w0_ref), channel_id=1, source_target_pairs={{0,1},{1,0},{2,3},{3,2},{4,5},{5,4},{6,7},{7,6},{8,9},{9,8},{10,11... | collective-permute-start | bytes 3145736 | tf_op jit(solution)/shard_map/ppermute | solution.py:297
  130.2 0.1 reshape.115
  130.3 0.1 copy.25
  130.4 0.7 reshape.116.count_ref
  131.1 6.3 %attend_near.1 = (f32[1024,128]{1,0:T(8,128)}, f32[1024,128]{1,0:T(8,128)}) custom-call(s32[8]{0:T(128)} %add.128.order_ref, bf16[4,2,192,128]{3,2,1,0:T(8,128)(2,1)} %bitcast.47, bf16[2,2,512,128]{3,2,1,0:T(8,128)(2,1)} %copy-done.4, bf16[2,2,512,128]{3,2,1,0:T(8,128)(2,1)} %copy-done.5, bf16[4,8,4,512]{3,2,1,0:T(4,128)(2,1)} %reshape.116.count_ref), custom_call_target="tpu_custom_call" | custom-call | tf_op jit(solution)/shard_map/attend_near/pallas_call | solution.py:212
  137.4 6.6 %attend_far.1 = bf16[2,4,2,72,128]{4,3,2,1,0:T(8,128)(2,1)} custom-call(s32[8]{0:T(128)} %add.128.order_ref, bf16[4,2,192,128]{3,2,1,0:T(8,128)(2,1)} %bitcast.48, bf16[2,2,2,512,128]{4,3,2,1,0:T(8,128)(2,1)} %collective-permute-done.11.far_ref, bf16[4,8,4,512]{3,2,1,0:T(4,128)(2,1)} %reshape.116.count_ref, f32[1024,128]{1,0:T(8,128)} %get-tuple-element.41.part_ref, ...), custom_call_target="tpu_custom_call" | custom-call | tf_op jit(solution)/shard_map/attend_far/pallas_call | solution.py:227
  144.0 0.1 collective-permute-done.13.w2_ref
  144.1 6.6 %collective-permute-start.14 = (bf16[4096,128]{1,0:T(8,128)(2,1)S(1)}, bf16[4096,128]{1,0:T(8,128)(2,1)}, u32[]{:S(2)}, u32[]{:S(2)}) collective-permute-start(bf16[4096,128]{1,0:T(8,128)(2,1)S(1)} %collective-permute-done.13.w2_ref), channel_id=1, source_target_pairs={{0,1},{1,0},{2,3},{3,2},{4,5},{5,4},{6,7},{7,6},{8,9},{9,8},{10,11... | collective-permute-start | bytes 3145736 | tf_op jit(solution)/shard_map/ppermute | solution.py:297
  150.7 5.5 %all-to-all-start.1 = ((bf16[16,72,128]{2,1,0:T(8,128)(2,1)}), bf16[16,72,128]{2,1,0:T(8,128)(2,1)S(1)}, u32[]{:S(2)}, u32[]{:S(2)}) async-start(bf16[16,72,128]{2,1,0:T(8,128)(2,1)} %bitcast.52), calls=%async_computation.1 | async-start | bytes 589824 | tf_op jit(solution)/shard_map/all_to_all | solution.py:399
  156.2 12.5 %all-to-all-done.1 = bf16[16,72,128]{2,1,0:T(8,128)(2,1)S(1)} async-done(((bf16[16,72,128]{2,1,0:T(8,128)(2,1)}), bf16[16,72,128]{2,1,0:T(8,128)(2,1)S(1)}, u32[]{:S(2)}, u32[]{:S(2)}) %all-to-all-start.1) | async-done | bytes 294944 | tf_op jit(solution)/shard_map/all_to_all | solution.py:399
  168.7 0.7 copy-done.9
  169.4 5.1 %mix.1 = bf16[32,64,128]{2,1,0:T(8,128)(2,1)} custom-call(s32[1]{0:T(128)} %bitcast.place_ref, bf16[2,4,2,72,128]{4,3,2,1,0:T(8,128)(2,1)} %bitcast.53, bf16[4096,128]{1,0:T(8,128)(2,1)} %copy-done.3, bf16[4096,128]{1,0:T(8,128)(2,1)} %collective-permute-done.12.w1_ref, bf16[4096,128]{1,0:T(8,128)(2,1)} %copy-done.10, ...), custom_call_target="tpu_custom_call" | custom-call | tf_op jit(solution)/shard_map/mix/pallas_call | solution.py:276
  174.5 23.7 %all_to_all.15 = bf16[32,64,128]{2,1,0:T(8,128)(2,1)S(1)} all-to-all(bf16[32,64,128]{2,1,0:T(8,128)(2,1)} %mix.1), channel_id=1, replica_groups=mesh['s'=2,'zh'=4,'x'=4,'y'=8,'c'=2] {'s','y','c'}, dimensions={0} | all-to-all | bytes 1048576 | tf_op jit(solution)/shard_map/all_to_all | solution.py:403
  198.2 0.7 reduce_sum.22
  (46 shorter events, 0.3 us)
Async XLA Ops:
  0.0 42.3 %copy-start = (f32[2,4096]{1,0:T(2,128)S(1)}, f32[2,4096]{1,0:T(2,128)}, u32[]{:S(2)}) copy-start(f32[2,4096]{1,0:T(2,128)} %param.11) | copy-start | bytes 98308
  1.8 15.7 %collective-permute-start = (bf16[640,128]{1,0:T(8,128)(2,1)S(1)}, bf16[640,128]{1,0:T(8,128)(2,1)S(1)}, u32[]{:S(2)}, u32[]{:S(2)}) collective-permute-start(bf16[640,128]{1,0:T(8,128)(2,1)S(1)} %pad_maximum_fusion.6), channel_id=1, source_target_pairs={{0,1},{1,0},{2,3},{3,2},{4,5},{5,4},{6,7},{7,6},{8,9},{9,8},{10,11... | collective-permute-start | bytes 491528 | tf_op jit(solution)/shard_map/ppermute | solution.py:297
  13.5 3.3 %copy-start.13 = (s32[8,128]{1,0:T(8,128)S(1)}, s32[8,128]{1,0:T(8,128)}, u32[]{:S(2)}) copy-start(s32[8,128]{1,0:T(8,128)} %param.8) | copy-start | bytes 12292
  13.6 3.8 %copy-start.14 = (s32[4,2]{0,1:T(2,128)S(1)}, s32[4,2]{0,1:T(2,128)}, u32[]{:S(2)}) copy-start(s32[4,2]{0,1:T(2,128)} %param.9) | copy-start | bytes 100
  14.9 38.1 %collective-permute-start.5 = (bf16[3,2048,128]{2,1,0:T(8,128)(2,1)}, bf16[3,2048,128]{2,1,0:T(8,128)(2,1)}, u32[]{:S(2)}, u32[]{:S(2)}) collective-permute-start(bf16[3,2048,128]{2,1,0:T(8,128)(2,1)} %pad_maximum_fusion), channel_id=1, source_target_pairs={{0,256},{256,0},{1,257},{257,1},{2,258},{258,2},{3,259},{259,3},{4... | collective-permute-start | bytes 4718600 | tf_op jit(solution)/shard_map/ppermute | solution.py:297
  17.5 9.1 %copy-start.8 = (bf16[2,640,128]{2,1,0:T(8,128)(2,1)}, bf16[2,640,128]{2,1,0:T(8,128)(2,1)S(1)}, u32[]{:S(2)}) copy-start(bf16[2,640,128]{2,1,0:T(8,128)(2,1)S(1)} %maximum_select_fusion.1.b0_ref) | copy-start | bytes 983044
  17.6 9.0 %collective-permute-start.1 = (bf16[2,640,128]{2,1,0:T(8,128)(2,1)S(1)}, bf16[2,640,128]{2,1,0:T(8,128)(2,1)S(1)}, u32[]{:S(2)}, u32[]{:S(2)}) collective-permute-start(bf16[2,640,128]{2,1,0:T(8,128)(2,1)S(1)} %maximum_select_fusion.1.b0_ref), channel_id=1, source_target_pairs={{0,2},{1,15},{2,0},{3,5},{4,6},{5,3},{6,4},{7,9},{8,10},{9,7},{10,... | collective-permute-start | bytes 983048 | tf_op jit(solution)/shard_map/ppermute | solution.py:330
  19.8 8.8 %copy-start.16 = (s32[4]{0:T(128)S(1)}, s32[4]{0:T(128)}, u32[]{:S(2)}) copy-start(s32[4]{0:T(128)} %constant.133) | copy-start | bytes 52
  20.1 21.7 %copy-start.15 = (s32[8]{0:T(128)S(1)}, s32[8]{0:T(128)}, u32[]{:S(2)}) copy-start(s32[8]{0:T(128)} %constant.129.clone) | copy-start | bytes 100
  21.3 7.3 %copy-start.12 = (bf16[2,2,4,4096]{3,2,1,0:T(4,128)(2,1)S(1)}, bf16[2,2,4,4096]{3,2,1,0:T(4,128)(2,1)}, u32[]{:S(2)}) copy-start(bf16[2,2,4,4096]{3,2,1,0:T(4,128)(2,1)} %reshape.110) | copy-start | bytes 393220
  26.6 29.4 %copy-start.7 = (bf16[2,640,128]{2,1,0:T(8,128)(2,1)}, bf16[2,640,128]{2,1,0:T(8,128)(2,1)S(1)}, u32[]{:S(2)}) copy-start(bf16[2,640,128]{2,1,0:T(8,128)(2,1)S(1)} %collective-permute-done.1.b1_ref) | copy-start | bytes 983044
  26.7 11.7 %collective-permute-start.2 = (bf16[2,2,640,128]{3,2,1,0:T(8,128)(2,1)S(1)}, bf16[2,2,640,128]{3,2,1,0:T(8,128)(2,1)S(1)}, u32[]{:S(2)}, u32[]{:S(2)}) collective-permute-start(bf16[2,2,640,128]{3,2,1,0:T(8,128)(2,1)S(1)} %pad_maximum_fusion.3), channel_id=1, source_target_pairs={{0,14},{1,3},{2,4},{3,1},{4,2},{5,7},{6,8},{7,5},{8,6},{9,11},{10,... | collective-permute-start | bytes 1966088 | tf_op jit(solution)/shard_map/ppermute | solution.py:330
  38.4 17.4 %copy-start.11 = (bf16[2,2,640,128]{3,2,1,0:T(8,128)(2,1)}, bf16[2,2,640,128]{3,2,1,0:T(8,128)(2,1)S(1)}, u32[]{:S(2)}) copy-start(bf16[2,2,640,128]{3,2,1,0:T(8,128)(2,1)S(1)} %collective-permute-done.2.b2_ref) | copy-start | bytes 1966084
  38.4 12.6 %collective-permute-start.3 = (bf16[2,2,640,128]{3,2,1,0:T(8,128)(2,1)S(1)}, bf16[2,2,640,128]{3,2,1,0:T(8,128)(2,1)}, u32[]{:S(2)}, u32[]{:S(2)}) collective-permute-start(bf16[2,2,640,128]{3,2,1,0:T(8,128)(2,1)S(1)} %collective-permute-done.2.b2_ref), channel_id=1, source_target_pairs={{0,2},{1,15},{2,0},{3,5},{4,6},{5,3},{6,4},{7,9},{8,10},{9,7},{10,... | collective-permute-start | bytes 1966088 | tf_op jit(solution)/shard_map/ppermute | solution.py:330
  53.0 16.8 %collective-permute-start.6 = (bf16[3,2048,128]{2,1,0:T(8,128)(2,1)}, bf16[3,2048,128]{2,1,0:T(8,128)(2,1)}, u32[]{:S(2)}, u32[]{:S(2)}) collective-permute-start(bf16[3,2048,128]{2,1,0:T(8,128)(2,1)} %collective-permute-done.5.w0_ref), channel_id=1, source_target_pairs={{0,1},{1,0},{2,3},{3,2},{4,5},{5,4},{6,7},{7,6},{8,9},{9,8},{10,11... | collective-permute-start | bytes 4718600 | tf_op jit(solution)/shard_map/ppermute | solution.py:297
  56.0 19.9 %copy-start.1 = (bf16[3,2048,128]{2,1,0:T(8,128)(2,1)}, bf16[3,2048,128]{2,1,0:T(8,128)(2,1)S(1)}, u32[]{:S(2)}) copy-start(bf16[3,2048,128]{2,1,0:T(8,128)(2,1)S(1)} %pad_maximum_fusion.1.w0_ref) | copy-start | bytes 4718596
  56.0 22.5 %collective-permute-start.7 = (bf16[3,2048,128]{2,1,0:T(8,128)(2,1)S(1)}, bf16[3,2048,128]{2,1,0:T(8,128)(2,1)S(1)}, u32[]{:S(2)}, u32[]{:S(2)}) collective-permute-start(bf16[3,2048,128]{2,1,0:T(8,128)(2,1)S(1)} %pad_maximum_fusion.1.w0_ref), channel_id=1, source_target_pairs={{0,1},{1,0},{2,3},{3,2},{4,5},{5,4},{6,7},{7,6},{8,9},{9,8},{10,11... | collective-permute-start | bytes 4718600 | tf_op jit(solution)/shard_map/ppermute | solution.py:297
  57.9 11.9 %collective-permute-start.4 = (bf16[2,2,640,128]{3,2,1,0:T(8,128)(2,1)}, bf16[2,2,640,128]{3,2,1,0:T(8,128)(2,1)}, u32[]{:S(2)}, u32[]{:S(2)}) collective-permute-start(bf16[2,2,640,128]{3,2,1,0:T(8,128)(2,1)} %collective-permute-done.3.b3_ref), channel_id=1, source_target_pairs={{0,14},{1,3},{2,4},{3,1},{4,2},{5,7},{6,8},{7,5},{8,6},{9,11},{10,... | collective-permute-start | bytes 1966088 | tf_op jit(solution)/shard_map/ppermute | solution.py:330
  75.8 14.7 %collective-permute-start.8 = (bf16[4,584,128]{2,1,0:T(8,128)(2,1)}, bf16[4,584,128]{2,1,0:T(8,128)(2,1)}, u32[]{:S(2)}, u32[]{:S(2)}) collective-permute-start(bf16[4,584,128]{2,1,0:T(8,128)(2,1)} %get-tuple-element.35), channel_id=1, source_target_pairs={{0,256},{256,0},{1,257},{257,1},{2,258},{258,2},{3,259},{259,3},{4... | collective-permute-start | bytes 1794056 | tf_op jit(solution)/shard_map/ppermute | solution.py:297
  78.5 1.2 copy-start.6
  93.2 11.1 %collective-permute-start.9 = (bf16[2,512,128]{2,1,0:T(8,128)(2,1)}, bf16[2,512,128]{2,1,0:T(8,128)(2,1)S(1)}, u32[]{:S(2)}, u32[]{:S(2)}) collective-permute-start(bf16[2,512,128]{2,1,0:T(8,128)(2,1)} %get-tuple-element.39), channel_id=1, source_target_pairs={{0,1},{1,0},{2,3},{3,2},{4,5},{5,4},{6,7},{7,6},{8,9},{9,8},{10,11... | collective-permute-start | bytes 786440 | tf_op jit(solution)/shard_map/ppermute | solution.py:297
  98.5 18.5 %all-to-all-start = ((bf16[8,192,128]{2,1,0:T(8,128)(2,1)}), bf16[8,192,128]{2,1,0:T(8,128)(2,1)S(1)}, u32[]{:S(2)}, u32[]{:S(2)}) async-start(bf16[8,192,128]{2,1,0:T(8,128)(2,1)} %bitcast.57), calls=%async_computation | async-start | bytes 786432 | tf_op jit(solution)/shard_map/all_to_all | solution.py:383
  105.3 12.9 %copy-start.4 = (bf16[2,2,512,128]{3,2,1,0:T(8,128)(2,1)}, bf16[2,2,512,128]{3,2,1,0:T(8,128)(2,1)S(1)}, u32[]{:S(2)}) copy-start(bf16[2,2,512,128]{3,2,1,0:T(8,128)(2,1)S(1)} %get-tuple-element.50.near_ref) | copy-start | bytes 1572868
  105.3 11.7 %collective-permute-start.10 = (bf16[2,2,512,128]{3,2,1,0:T(8,128)(2,1)S(1)}, bf16[2,2,512,128]{3,2,1,0:T(8,128)(2,1)S(1)}, u32[]{:S(2)}, u32[]{:S(2)}) collective-permute-start(bf16[2,2,512,128]{3,2,1,0:T(8,128)(2,1)S(1)} %get-tuple-element.50.near_ref), channel_id=1, source_target_pairs={{0,16},{1,49},{16,0},{17,33},{32,48},{33,17},{48,32},{49,1},{2,18}... | collective-permute-start | bytes 1572872 | tf_op jit(solution)/shard_map/ppermute | solution.py:330
  111.0 20.1 %copy-start.3 = (bf16[4096,128]{1,0:T(8,128)(2,1)}, bf16[4096,128]{1,0:T(8,128)(2,1)S(1)}, u32[]{:S(2)}) copy-start(bf16[4096,128]{1,0:T(8,128)(2,1)S(1)} %slice_bitcast_fusion.w0_ref) | copy-start | bytes 3145732
  117.0 14.1 %copy-start.2 = (bf16[8,192,128]{2,1,0:T(8,128)(2,1)}, bf16[8,192,128]{2,1,0:T(8,128)(2,1)S(1)}, u32[]{:S(2)}) copy-start(bf16[8,192,128]{2,1,0:T(8,128)(2,1)S(1)} %all-to-all-done) | copy-start | bytes 1179652
  117.0 14.1 %copy-start.5 = (bf16[2,2,512,128]{3,2,1,0:T(8,128)(2,1)}, bf16[2,2,512,128]{3,2,1,0:T(8,128)(2,1)S(1)}, u32[]{:S(2)}) copy-start(bf16[2,2,512,128]{3,2,1,0:T(8,128)(2,1)S(1)} %collective-permute-done.10.next_ref) | copy-start | bytes 1572868
  118.2 19.2 %collective-permute-start.11 = (bf16[2,2,2,512,128]{4,3,2,1,0:T(8,128)(2,1)}, bf16[2,2,2,512,128]{4,3,2,1,0:T(8,128)(2,1)}, u32[]{:S(2)}, u32[]{:S(2)}) collective-permute-start(bf16[2,2,2,512,128]{4,3,2,1,0:T(8,128)(2,1)} %pad_maximum_fusion.2), channel_id=1, source_target_pairs={{0,48},{1,17},{16,32},{17,1},{32,16},{33,49},{48,0},{49,33},{2,50}... | collective-permute-start | bytes 3145736 | tf_op jit(solution)/shard_map/ppermute | solution.py:330
  121.3 22.8 %collective-permute-start.13 = (bf16[4096,128]{1,0:T(8,128)(2,1)S(1)}, bf16[4096,128]{1,0:T(8,128)(2,1)S(1)}, u32[]{:S(2)}, u32[]{:S(2)}) collective-permute-start(bf16[4096,128]{1,0:T(8,128)(2,1)S(1)} %slice_bitcast_fusion.w0_ref), channel_id=1, source_target_pairs={{0,256},{256,0},{1,257},{257,1},{2,258},{258,2},{3,259},{259,3},{4... | collective-permute-start | bytes 3145736 | tf_op jit(solution)/shard_map/ppermute | solution.py:297
  123.2 32.9 %collective-permute-start.12 = (bf16[4096,128]{1,0:T(8,128)(2,1)S(1)}, bf16[4096,128]{1,0:T(8,128)(2,1)}, u32[]{:S(2)}, u32[]{:S(2)}) collective-permute-start(bf16[4096,128]{1,0:T(8,128)(2,1)S(1)} %slice_bitcast_fusion.w0_ref), channel_id=1, source_target_pairs={{0,1},{1,0},{2,3},{3,2},{4,5},{5,4},{6,7},{7,6},{8,9},{9,8},{10,11... | collective-permute-start | bytes 3145736 | tf_op jit(solution)/shard_map/ppermute | solution.py:297
  144.1 24.6 %copy-start.10 = (bf16[4096,128]{1,0:T(8,128)(2,1)}, bf16[4096,128]{1,0:T(8,128)(2,1)S(1)}, u32[]{:S(2)}) copy-start(bf16[4096,128]{1,0:T(8,128)(2,1)S(1)} %collective-permute-done.13.w2_ref) | copy-start | bytes 3145732
  144.1 24.6 %collective-permute-start.14 = (bf16[4096,128]{1,0:T(8,128)(2,1)S(1)}, bf16[4096,128]{1,0:T(8,128)(2,1)}, u32[]{:S(2)}, u32[]{:S(2)}) collective-permute-start(bf16[4096,128]{1,0:T(8,128)(2,1)S(1)} %collective-permute-done.13.w2_ref), channel_id=1, source_target_pairs={{0,1},{1,0},{2,3},{3,2},{4,5},{5,4},{6,7},{7,6},{8,9},{9,8},{10,11... | collective-permute-start | bytes 3145736 | tf_op jit(solution)/shard_map/ppermute | solution.py:297
  150.7 18.0 %all-to-all-start.1 = ((bf16[16,72,128]{2,1,0:T(8,128)(2,1)}), bf16[16,72,128]{2,1,0:T(8,128)(2,1)S(1)}, u32[]{:S(2)}, u32[]{:S(2)}) async-start(bf16[16,72,128]{2,1,0:T(8,128)(2,1)} %bitcast.52), calls=%async_computation.1 | async-start | bytes 589824 | tf_op jit(solution)/shard_map/all_to_all | solution.py:399
  168.7 0.7 copy-start.9
where the time goes:
time: 201 us; the launch traced here: 199 us
  starting transfers between devices  65.1 us (32%)
  waiting for transfers between devices  59.2 us (29%)
  Pallas kernels  31.9 us (16%)
  blocking collectives  23.7 us (12%)
  local copies, waits for them, and re-layouts  12.4 us (6%)
  other arithmetic  5.39 us (3%)
    ppermute x9, starting transfers between devices, swap(): return lax.ppermute(value, axis, [(0, 1), (1, 0)])  38.7 us
    ppermute x6, waiting for transfers between devices, exchange(): return lax.ppermute(value, (axis, 'c'), pairs(size, turn))  33 us
    all_to_all x1, blocking collectives, step(): out = lax.all_to_all(out, ('s', 'y', 'c'), 0, 0)  23.7 us
    ppermute x6, starting transfers between devices, exchange(): return lax.ppermute(value, (axis, 'c'), pairs(size, turn))  15.2 us
    all_to_all x1, waiting for transfers between devices, step(): lax.all_to_all(parts.reshape(16, ROWS, HEAD_DIM), ('s', 'zh', 'c'), 0, 0)  12.5 us
    ppermute x9, waiting for transfers between devices, swap(): return lax.ppermute(value, axis, [(0, 1), (1, 0)])  7.76 us
    pallas_call x1, Pallas kernels, attend_far(): pl.pallas_call(far_attend_kernel, grid_spec=pltpu.PrefetchScalarGridSpec(...  6.63 us
    pallas_call x1, Pallas kernels, attend_near(): pl.pallas_call(near_attend_kernel, grid_spec=pltpu.PrefetchScalarGridSpec...  6.29 us
  transfers between devices with their start and end apart: 17, of which 9 were waited for; matrix products, arithmetic and copies ran while one was open for 6% of the time, Pallas kernels for 12%

commit v1 on v0

--- a/solution.py
+++ b/solution.py
@@ -351,16 +351,16 @@
     chunk = jnp.where(core == 0, jnp.stack([own, got]), jnp.stack([got, own]))
     first = exchange(chunk, "y", 8, 0)
     second = exchange(jnp.stack([chunk, first]), "y", 8, 1)
-    mine = after(feature_rows(projections, section), first)
+    mine = feature_rows(after(projections, first), section)
     beside = swap(mine, "c")
 
     gains = lax.dynamic_slice_in_dim(norm_gains, section * 2048, 2048, axis=1)
     gains = gains.reshape(2, 8, 2, 128).transpose(1, 2, 0, 3)
-    counts = multiplicities(nb_ids, nb_index).reshape(2, 2, 4, 4 * 1024)
+    counts = multiplicities(after(nb_ids, first), nb_index).reshape(2, 2, 4, 4 * 1024)
     counts = lax.dynamic_index_in_dim(counts, core, 0, keepdims=False)
     counts = counts.transpose(1, 0, 2).reshape(4, 64, 128)
     sign = 1 - 2 * ((here + core) % 2)
-    offsets = jnp.array([0, 1, -1, -2, 2, 3, -3, -4], jnp.int32)
+    offsets = after(jnp.array([0, 1, -1, -2, 2, 3, -3, -4], jnp.int32), first)
     source = jnp.concatenate([(here + sign * offsets) % 8, core.reshape(1)]).astype(jnp.int32)
     sign = 1 - 2 * ((column + core) % 2)
     origin = (column + sign * offsets[:4]) % 4
@@ -376,6 +376,8 @@
     lhs, squares, send = project_far(
         source, (chunk, first, second, third, fourth), gains, (across, diagonal)
     )
+    wo = after(projections[1, 1], third)
+    wo_section = swap(wo, "s")
     other = swap(send, "s")
     keep, keep_q = project_near(lhs, (mine, beside))
     near, give, queries = finish(source, keep, keep_q, squares, other, counts)
@@ -383,19 +385,16 @@
     queries = lax.all_to_all(queries, ("zh", "c"), 0, 0)
     near = jnp.stack([near, swap(give, "c")])
     following = exchange(near, "x", 4, 0)
-    following = after(following, queries)
     beyond = exchange(jnp.stack([near, following]), "x", 4, 1)
     queries = queries.reshape(4, 2, 192, 128)
     counts = queries[:, :, 128:].reshape(4, 2, 2, 8, HALF).transpose(0, 3, 1, 2, 4)
     counts = counts.reshape(4, 8, 4, HALF)
 
-    wo = after(projections[1, 1], queries)
-    wo_section = swap(wo, "s")
     wo_beside = swap(wo, "c")
+    wo_diagonal = swap(wo_section, "c")
 
     part, total = attend_near(order, queries, near, following, counts)
     parts = attend_far(order, queries, beyond, counts, part, total)
-    wo_diagonal = swap(after(wo_section, parts), "c")
     parts = lax.all_to_all(parts.reshape(16, ROWS, HEAD_DIM), ("s", "zh", "c"), 0, 0)
     place = (section * 2 + core).astype(jnp.int32).reshape(1)
     weights = (wo, wo_beside, wo_section, wo_diagonal)

time: 201 us -> 211 us (1.050)
  waiting for transfers between devices: 59.2 us -> 70.9 us
  starting transfers between devices: 65.1 us -> 59.4 us
  local copies, waits for them, and re-layouts: 12.4 us -> 16.4 us
    ppermute x9, waiting for transfers between devices: 7.76 us -> 13.6 us  [swap(): return lax.ppermute(value, axis, [(0, 1), (1, 0)])]
    ppermute x9, starting transfers between devices: 38.7 us -> 33.4 us  [swap(): return lax.ppermute(value, axis, [(0, 1), (1, 0)])]
    all_to_all x1, starting transfers between devices: 5.77 us -> 9.46 us  [step(): queries = lax.all_to_all(queries, ('zh', 'c'), 0, 0)]
    ppermute x6, starting transfers between devices: 15.2 us -> 11.6 us  [exchange(): return lax.ppermute(value, (axis, 'c'), pairs(size, turn))]
    all_to_all x1, waiting for transfers between devices: 5.95 us -> 8.85 us  [step(): queries = lax.all_to_all(queries, ('zh', 'c'), 0, 0)]
    ppermute x6, waiting for transfers between devices: 33 us -> 35.9 us  [exchange(): return lax.ppermute(value, (axis, 'c'), pairs(size, turn))]
    squeeze x2 -> x4, local copies, waits for them, and re-layouts: 2.97 us -> 4.77 us  [feature_rows(): return jnp.concatenate([encoder[0], decoder[0]], axis=0)]
  transfers between devices with their start and end apart: 17 -> 17, of which waited for: 9 -> 11; matrix products, arithmetic and copies ran while one was open for 6% -> 7% of each run, Pallas kernels for 12% -> 12%
where the time goes in v1:
time: 211 us; the launch traced here: 209 us
  waiting for transfers between devices  70.9 us (34%)
  starting transfers between devices  59.4 us (28%)
  Pallas kernels  31.9 us (15%)
  blocking collectives  23.7 us (11%)
  local copies, waits for them, and re-layouts  16.4 us (8%)
  other arithmetic  5.15 us (2%)
    ppermute x6, waiting for transfers between devices, exchange(): return lax.ppermute(value, (axis, 'c'), pairs(size, turn))  35.9 us
    ppermute x9, starting transfers between devices, swap(): return lax.ppermute(value, axis, [(0, 1), (1, 0)])  33.4 us
    all_to_all x1, blocking collectives, step(): out = lax.all_to_all(out, ('s', 'y', 'c'), 0, 0)  23.7 us
    ppermute x9, waiting for transfers between devices, swap(): return lax.ppermute(value, axis, [(0, 1), (1, 0)])  13.6 us
    all_to_all x1, waiting for transfers between devices, step(): lax.all_to_all(parts.reshape(16, ROWS, HEAD_DIM), ('s', 'zh', 'c'), 0, 0)  12.5 us
    ppermute x6, starting transfers between devices, exchange(): return lax.ppermute(value, (axis, 'c'), pairs(size, turn))  11.6 us
    all_to_all x1, starting transfers between devices, step(): queries = lax.all_to_all(queries, ('zh', 'c'), 0, 0)  9.46 us
    all_to_all x1, waiting for transfers between devices, step(): queries = lax.all_to_all(queries, ('zh', 'c'), 0, 0)  8.85 us
  transfers between devices with their start and end apart: 17, of which 11 were waited for; matrix products, arithmetic and copies ran while one was open for 7% of the time, Pallas kernels for 12%

profile of v1, /device:TPU:1, one launch (start us, length us, event | category | flops | bytes accessed | tf_op | source)
XLA Modules:
  0.0 209.3 jit_solution(12717034712069971250)
XLA Ops:
  0.0 0.8 constant_dynamic-slice_fusion.3
  0.8 1.0 constant_dynamic-slice_fusion.4
  1.8 8.7 %collective-permute-start = (bf16[640,128]{1,0:T(8,128)(2,1)S(1)}, bf16[640,128]{1,0:T(8,128)(2,1)S(1)}, u32[]{:S(2)}, u32[]{:S(2)}) collective-permute-start(bf16[640,128]{1,0:T(8,128)(2,1)S(1)} %pad_maximum_fusion.6), channel_id=1, source_target_pairs={{0,1},{1,0},{2,3},{3,2},{4,5},{5,4},{6,7},{7,6},{8,9},{9,8},{10,11... | collective-permute-start | bytes 491528 | tf_op jit(solution)/shard_map/ppermute | solution.py:297
  10.6 1.1 dynamic-slice_bitcast_fusion.3
  11.7 1.3 dynamic-slice_bitcast_fusion.1
  13.0 0.1 pad_maximum_fusion
  13.1 1.9 collective-permute-start.5
  15.1 0.1 convert_reduce_fusion
  15.3 1.9 collective-permute-start.1
  17.3 0.6 constant_dynamic-slice_fusion
  17.9 6.4 %collective-permute-done.1.b1_ref = bf16[2,640,128]{2,1,0:T(8,128)(2,1)S(1)} collective-permute-done((bf16[2,640,128]{2,1,0:T(8,128)(2,1)S(1)}, bf16[2,640,128]{2,1,0:T(8,128)(2,1)S(1)}, u32[]{:S(2)}, u32[]{:S(2)}) %collective-permute-start.1) | collective-permute-done | bytes 327712 | tf_op jit(solution)/shard_map/ppermute | solution.py:330
  24.3 1.0 pad_maximum_fusion.3
  25.3 2.0 collective-permute-start.2
  27.4 0.5 fusion.1
  27.9 0.9 convolution_convert_fusion
  28.9 1.2 copy.19
  30.1 0.5 reshape.110
  30.7 6.7 %collective-permute-done.2.b2_ref = bf16[2,2,640,128]{3,2,1,0:T(8,128)(2,1)S(1)} collective-permute-done((bf16[2,2,640,128]{3,2,1,0:T(8,128)(2,1)}, bf16[2,2,640,128]{3,2,1,0:T(8,128)(2,1)S(1)}, u32[]{:S(2)}, u32[]{:S(2)}) %collective-permute-start.2) | collective-permute-done | bytes 655392 | tf_op jit(solution)/shard_map/ppermute | solution.py:330
  37.4 1.9 collective-permute-start.3
  39.4 0.7 reshape.111.count_ref
  40.2 0.7 add.128.order_ref
  40.8 0.6 pad_add_fusion.source_ref
  41.4 8.5 %collective-permute-done.3.b3_ref = bf16[2,2,640,128]{3,2,1,0:T(8,128)(2,1)S(1)} collective-permute-done((bf16[2,2,640,128]{3,2,1,0:T(8,128)(2,1)S(1)}, bf16[2,2,640,128]{3,2,1,0:T(8,128)(2,1)S(1)}, u32[]{:S(2)}, u32[]{:S(2)}) %collective-permute-start.3) | collective-permute-done | bytes 655392 | tf_op jit(solution)/shard_map/ppermute | solution.py:330
  49.9 1.1 collective-permute-done.5.w0_ref
  51.1 2.8 %collective-permute-start.6 = (bf16[3,2048,128]{2,1,0:T(8,128)(2,1)}, bf16[3,2048,128]{2,1,0:T(8,128)(2,1)}, u32[]{:S(2)}, u32[]{:S(2)}) collective-permute-start(bf16[3,2048,128]{2,1,0:T(8,128)(2,1)} %collective-permute-done.5.w0_ref), channel_id=1, source_target_pairs={{0,1},{1,0},{2,3},{3,2},{4,5},{5,4},{6,7},{7,6},{8,9},{9,8},{10,11... | collective-permute-start | bytes 4718600 | tf_op jit(solution)/shard_map/ppermute | solution.py:297
  53.8 1.1 dynamic-slice_bitcast_fusion.2
  54.9 1.3 dynamic-slice_bitcast_fusion
  56.3 0.1 pad_maximum_fusion.1.w0_ref
  56.4 2.1 collective-permute-start.7
  58.5 1.9 collective-permute-start.4
  60.4 9.7 %collective-permute-done.4.b4_ref = bf16[2,2,640,128]{3,2,1,0:T(8,128)(2,1)S(1)} collective-permute-done((bf16[2,2,640,128]{3,2,1,0:T(8,128)(2,1)S(1)}, bf16[2,2,640,128]{3,2,1,0:T(8,128)(2,1)S(1)}, u32[]{:S(2)}, u32[]{:S(2)}) %collective-permute-start.4) | collective-permute-done | bytes 655392 | tf_op jit(solution)/shard_map/ppermute | solution.py:330
  70.1 0.8 copy-done.14
  71.0 6.0 %project_far.1 = (bf16[8,640,256]{2,1,0:T(8,128)(2,1)}, f32[8,128]{1,0:T(8,128)}, bf16[4,584,128]{2,1,0:T(8,128)(2,1)}) custom-call(s32[9]{0:T(128)} %pad_add_fusion.source_ref, bf16[2,640,128]{2,1,0:T(8,128)(2,1)} %copy-done.8, bf16[2,640,128]{2,1,0:T(8,128)(2,1)} %copy-done.7, bf16[2,2,640,128]{3,2,1,0:T(8,128)(2,1)} %copy-done.11, ...), custom_call_target="tpu_custom_call" | custom-call | tf_op jit(solution)/shard_map/project_far/pallas_call | solution.py:91
  76.9 3.5 %collective-permute-start.8 = (bf16[4,584,128]{2,1,0:T(8,128)(2,1)}, bf16[4,584,128]{2,1,0:T(8,128)(2,1)}, u32[]{:S(2)}, u32[]{:S(2)}) collective-permute-start(bf16[4,584,128]{2,1,0:T(8,128)(2,1)} %get-tuple-element.37), channel_id=1, source_target_pairs={{0,256},{256,0},{1,257},{257,1},{2,258},{258,2},{3,259},{259,3},{4... | collective-permute-start | bytes 1794056 | tf_op jit(solution)/shard_map/ppermute | solution.py:297
  80.4 1.2 copy-done.6
  81.6 5.2 %project_near.1 = (f32[2,2,512,128]{3,2,1,0:T(8,128)}, f32[2,128,128]{2,1,0:T(8,128)}) custom-call(bf16[8,640,256]{2,1,0:T(8,128)(2,1)} %get-tuple-element.32.lhs_ref, bf16[3,2048,128]{2,1,0:T(8,128)(2,1)} %copy-done.1, bf16[3,2048,128]{2,1,0:T(8,128)(2,1)} %copy-done.6), custom_call_target="tpu_custom_call" | custom-call | tf_op jit(solution)/shard_map/project_near/pallas_call | solution.py:116
  86.8 5.1 %collective-permute-done.8.other_ref = bf16[4,584,128]{2,1,0:T(8,128)(2,1)} collective-permute-done((bf16[4,584,128]{2,1,0:T(8,128)(2,1)}, bf16[4,584,128]{2,1,0:T(8,128)(2,1)}, u32[]{:S(2)}, u32[]{:S(2)}) %collective-permute-start.8) | collective-permute-done | bytes 598048 | tf_op jit(solution)/shard_map/ppermute | solution.py:297
  91.9 2.7 %finish.1 = (bf16[2,512,128]{2,1,0:T(8,128)(2,1)}, bf16[2,512,128]{2,1,0:T(8,128)(2,1)}, bf16[4,2,192,128]{3,2,1,0:T(8,128)(2,1)}) custom-call(s32[9]{0:T(128)} %pad_add_fusion.source_ref, f32[2,2,512,128]{3,2,1,0:T(8,128)} %get-tuple-element.34.keep_ref, f32[2,128,128]{2,1,0:T(8,128)} %get-tuple-element.35.keep_q_ref, ...), custom_call_target="tpu_custom_call" | custom-call | tf_op jit(solution)/shard_map/finish/pallas_call | solution.py:155
  94.5 5.2 %collective-permute-start.9 = (bf16[2,512,128]{2,1,0:T(8,128)(2,1)}, bf16[2,512,128]{2,1,0:T(8,128)(2,1)S(1)}, u32[]{:S(2)}, u32[]{:S(2)}) collective-permute-start(bf16[2,512,128]{2,1,0:T(8,128)(2,1)} %get-tuple-element.41), channel_id=1, source_target_pairs={{0,1},{1,0},{2,3},{3,2},{4,5},{5,4},{6,7},{7,6},{8,9},{9,8},{10,11... | collective-permute-start | bytes 786440 | tf_op jit(solution)/shard_map/ppermute | solution.py:297
  99.7 1.4 collective-permute-done.9
  101.1 1.0 fusion.16
  102.1 1.9 collective-permute-start.10
  104.1 1.3 slice_bitcast_fusion.w0_ref
  105.4 3.4 %collective-permute-start.13 = (bf16[4096,128]{1,0:T(8,128)(2,1)S(1)}, bf16[4096,128]{1,0:T(8,128)(2,1)}, u32[]{:S(2)}, u32[]{:S(2)}) collective-permute-start(bf16[4096,128]{1,0:T(8,128)(2,1)S(1)} %slice_bitcast_fusion.w0_ref), channel_id=1, source_target_pairs={{0,256},{256,0},{1,257},{257,1},{2,258},{258,2},{3,259},{259,3},{4... | collective-permute-start | bytes 3145736 | tf_op jit(solution)/shard_map/ppermute | solution.py:297
  108.7 4.5 %collective-permute-done.10.next_ref = bf16[2,2,512,128]{3,2,1,0:T(8,128)(2,1)S(1)} collective-permute-done((bf16[2,2,512,128]{3,2,1,0:T(8,128)(2,1)S(1)}, bf16[2,2,512,128]{3,2,1,0:T(8,128)(2,1)S(1)}, u32[]{:S(2)}, u32[]{:S(2)}) %collective-permute-start.10) | collective-permute-done | bytes 524320 | tf_op jit(solution)/shard_map/ppermute | solution.py:330
  113.3 1.2 pad_maximum_fusion.2
  114.5 1.9 collective-permute-start.11
  116.4 9.5 %all-to-all-start = ((bf16[8,192,128]{2,1,0:T(8,128)(2,1)}), bf16[8,192,128]{2,1,0:T(8,128)(2,1)S(1)}, u32[]{:S(2)}, u32[]{:S(2)}) async-start(bf16[8,192,128]{2,1,0:T(8,128)(2,1)} %bitcast.17), calls=%async_computation | async-start | bytes 786432 | tf_op jit(solution)/shard_map/all_to_all | solution.py:385
  125.8 1.9 collective-permute-start.12
  127.8 6.1 %collective-permute-done.13.w2_ref = bf16[4096,128]{1,0:T(8,128)(2,1)} collective-permute-done((bf16[4096,128]{1,0:T(8,128)(2,1)S(1)}, bf16[4096,128]{1,0:T(8,128)(2,1)}, u32[]{:S(2)}, u32[]{:S(2)}) %collective-permute-start.13) | collective-permute-done | bytes 1048608 | tf_op jit(solution)/shard_map/ppermute | solution.py:297
  133.8 4.0 %collective-permute-start.14 = (bf16[4096,128]{1,0:T(8,128)(2,1)}, bf16[4096,128]{1,0:T(8,128)(2,1)}, u32[]{:S(2)}, u32[]{:S(2)}) collective-permute-start(bf16[4096,128]{1,0:T(8,128)(2,1)} %collective-permute-done.13.w2_ref), channel_id=1, source_target_pairs={{0,1},{1,0},{2,3},{3,2},{4,5},{5,4},{6,7},{7,6},{8,9},{9,8},{10,11... | collective-permute-start | bytes 3145736 | tf_op jit(solution)/shard_map/ppermute | solution.py:297
  137.8 8.8 %all-to-all-done = bf16[8,192,128]{2,1,0:T(8,128)(2,1)S(1)} async-done(((bf16[8,192,128]{2,1,0:T(8,128)(2,1)}), bf16[8,192,128]{2,1,0:T(8,128)(2,1)S(1)}, u32[]{:S(2)}, u32[]{:S(2)}) %all-to-all-start) | async-done | bytes 393248 | tf_op jit(solution)/shard_map/all_to_all | solution.py:385
  146.7 0.1 reshape.115
  146.8 0.1 copy.25
  146.9 0.7 reshape.116.count_ref
  147.6 6.3 %attend_near.1 = (f32[1024,128]{1,0:T(8,128)}, f32[1024,128]{1,0:T(8,128)}) custom-call(s32[8]{0:T(128)} %add.128.order_ref, bf16[4,2,192,128]{3,2,1,0:T(8,128)(2,1)} %bitcast.47, bf16[2,2,512,128]{3,2,1,0:T(8,128)(2,1)} %copy-done.4, bf16[2,2,512,128]{3,2,1,0:T(8,128)(2,1)} %copy-done.5, bf16[4,8,4,512]{3,2,1,0:T(4,128)(2,1)} %reshape.116.count_ref), custom_call_target="tpu_custom_call" | custom-call | tf_op jit(solution)/shard_map/attend_near/pallas_call | solution.py:212
  153.9 1.0 copy-done.10
  154.9 6.6 %attend_far.1 = bf16[2,4,2,72,128]{4,3,2,1,0:T(8,128)(2,1)} custom-call(s32[8]{0:T(128)} %add.128.order_ref, bf16[4,2,192,128]{3,2,1,0:T(8,128)(2,1)} %bitcast.48, bf16[2,2,2,512,128]{4,3,2,1,0:T(8,128)(2,1)} %copy-done.10, bf16[4,8,4,512]{3,2,1,0:T(4,128)(2,1)} %reshape.116.count_ref, f32[1024,128]{1,0:T(8,128)} %get-tuple-element.42.part_ref, ...), custom_call_target="tpu_custom_call" | custom-call | tf_op jit(solution)/shard_map/attend_far/pallas_call | solution.py:227
  161.5 5.0 %all-to-all-start.1 = ((bf16[16,72,128]{2,1,0:T(8,128)(2,1)}), bf16[16,72,128]{2,1,0:T(8,128)(2,1)S(1)}, u32[]{:S(2)}, u32[]{:S(2)}) async-start(bf16[16,72,128]{2,1,0:T(8,128)(2,1)} %bitcast.52), calls=%async_computation.1 | async-start | bytes 589824 | tf_op jit(solution)/shard_map/all_to_all | solution.py:398
  166.5 12.5 %all-to-all-done.1 = bf16[16,72,128]{2,1,0:T(8,128)(2,1)S(1)} async-done(((bf16[16,72,128]{2,1,0:T(8,128)(2,1)}), bf16[16,72,128]{2,1,0:T(8,128)(2,1)S(1)}, u32[]{:S(2)}, u32[]{:S(2)}) %all-to-all-start.1) | async-done | bytes 294944 | tf_op jit(solution)/shard_map/all_to_all | solution.py:398
  179.1 0.7 copy-done.9
  179.8 5.1 %mix.1 = bf16[32,64,128]{2,1,0:T(8,128)(2,1)} custom-call(s32[1]{0:T(128)} %bitcast.place_ref, bf16[2,4,2,72,128]{4,3,2,1,0:T(8,128)(2,1)} %bitcast.53, bf16[4096,128]{1,0:T(8,128)(2,1)} %copy-done.3, bf16[4096,128]{1,0:T(8,128)(2,1)} %collective-permute-done.12.w1_ref, bf16[4096,128]{1,0:T(8,128)(2,1)} %collective-permute-done.13.w2_ref, ...), custom_call_target="tpu_custom_call" | custom-call | tf_op jit(solution)/shard_map/mix/pallas_call | solution.py:276
  184.9 23.7 %all_to_all.15 = bf16[32,64,128]{2,1,0:T(8,128)(2,1)S(1)} all-to-all(bf16[32,64,128]{2,1,0:T(8,128)(2,1)} %mix.1), channel_id=1, replica_groups=mesh['s'=2,'zh'=4,'x'=4,'y'=8,'c'=2] {'s','y','c'}, dimensions={0} | all-to-all | bytes 1048576 | tf_op jit(solution)/shard_map/all_to_all | solution.py:402
  208.6 0.7 reduce_sum.22
  (50 shorter events, 0.5 us)
Async XLA Ops:
  0.0 17.2 %copy-start = (f32[2,4096]{1,0:T(2,128)S(1)}, f32[2,4096]{1,0:T(2,128)}, u32[]{:S(2)}) copy-start(f32[2,4096]{1,0:T(2,128)} %param.11) | copy-start | bytes 98308
  1.8 13.4 %collective-permute-start = (bf16[640,128]{1,0:T(8,128)(2,1)S(1)}, bf16[640,128]{1,0:T(8,128)(2,1)S(1)}, u32[]{:S(2)}, u32[]{:S(2)}) collective-permute-start(bf16[640,128]{1,0:T(8,128)(2,1)S(1)} %pad_maximum_fusion.6), channel_id=1, source_target_pairs={{0,1},{1,0},{2,3},{3,2},{4,5},{5,4},{6,7},{7,6},{8,9},{9,8},{10,11... | collective-permute-start | bytes 491528 | tf_op jit(solution)/shard_map/ppermute | solution.py:297
  13.0 2.1 copy-start.17
  13.1 37.9 %collective-permute-start.5 = (bf16[3,2048,128]{2,1,0:T(8,128)(2,1)S(1)}, bf16[3,2048,128]{2,1,0:T(8,128)(2,1)}, u32[]{:S(2)}, u32[]{:S(2)}) collective-permute-start(bf16[3,2048,128]{2,1,0:T(8,128)(2,1)S(1)} %pad_maximum_fusion), channel_id=1, source_target_pairs={{0,256},{256,0},{1,257},{257,1},{2,258},{258,2},{3,259},{259,3},{4... | collective-permute-start | bytes 4718600 | tf_op jit(solution)/shard_map/ppermute | solution.py:297
  15.2 12.2 %copy-start.15 = (s32[8,128]{1,0:T(8,128)S(1)}, s32[8,128]{1,0:T(8,128)}, u32[]{:S(2)}) copy-start(s32[8,128]{1,0:T(8,128)} %param.8) | copy-start | bytes 12292
  15.3 13.6 %copy-start.8 = (bf16[2,640,128]{2,1,0:T(8,128)(2,1)}, bf16[2,640,128]{2,1,0:T(8,128)(2,1)S(1)}, u32[]{:S(2)}) copy-start(bf16[2,640,128]{2,1,0:T(8,128)(2,1)S(1)} %maximum_select_fusion.1.b0_ref) | copy-start | bytes 983044
  15.3 9.0 %collective-permute-start.1 = (bf16[2,640,128]{2,1,0:T(8,128)(2,1)S(1)}, bf16[2,640,128]{2,1,0:T(8,128)(2,1)S(1)}, u32[]{:S(2)}, u32[]{:S(2)}) collective-permute-start(bf16[2,640,128]{2,1,0:T(8,128)(2,1)S(1)} %maximum_select_fusion.1.b0_ref), channel_id=1, source_target_pairs={{0,2},{1,15},{2,0},{3,5},{4,6},{5,3},{6,4},{7,9},{8,10},{9,7},{10,... | collective-permute-start | bytes 983048 | tf_op jit(solution)/shard_map/ppermute | solution.py:330
  24.3 5.7 %copy-start.7 = (bf16[2,640,128]{2,1,0:T(8,128)(2,1)}, bf16[2,640,128]{2,1,0:T(8,128)(2,1)S(1)}, u32[]{:S(2)}) copy-start(bf16[2,640,128]{2,1,0:T(8,128)(2,1)S(1)} %collective-permute-done.1.b1_ref) | copy-start | bytes 983044
  25.3 14.0 %copy-start.16 = (s32[8]{0:T(128)S(1)}, s32[8]{0:T(128)}, u32[]{:S(2)}) copy-start(s32[8]{0:T(128)} %constant.129.clone) | copy-start | bytes 100
  25.3 12.1 %collective-permute-start.2 = (bf16[2,2,640,128]{3,2,1,0:T(8,128)(2,1)}, bf16[2,2,640,128]{3,2,1,0:T(8,128)(2,1)S(1)}, u32[]{:S(2)}, u32[]{:S(2)}) collective-permute-start(bf16[2,2,640,128]{3,2,1,0:T(8,128)(2,1)} %pad_maximum_fusion.3), channel_id=1, source_target_pairs={{0,14},{1,3},{2,4},{3,1},{4,2},{5,7},{6,8},{7,5},{8,6},{9,11},{10,... | collective-permute-start | bytes 1966088 | tf_op jit(solution)/shard_map/ppermute | solution.py:330
  37.4 17.5 %copy-start.11 = (bf16[2,2,640,128]{3,2,1,0:T(8,128)(2,1)}, bf16[2,2,640,128]{3,2,1,0:T(8,128)(2,1)S(1)}, u32[]{:S(2)}) copy-start(bf16[2,2,640,128]{3,2,1,0:T(8,128)(2,1)S(1)} %collective-permute-done.2.b2_ref) | copy-start | bytes 1966084
  37.4 12.5 %collective-permute-start.3 = (bf16[2,2,640,128]{3,2,1,0:T(8,128)(2,1)S(1)}, bf16[2,2,640,128]{3,2,1,0:T(8,128)(2,1)S(1)}, u32[]{:S(2)}, u32[]{:S(2)}) collective-permute-start(bf16[2,2,640,128]{3,2,1,0:T(8,128)(2,1)S(1)} %collective-permute-done.2.b2_ref), channel_id=1, source_target_pairs={{0,2},{1,15},{2,0},{3,5},{4,6},{5,3},{6,4},{7,9},{8,10},{9,7},{10,... | collective-permute-start | bytes 1966088 | tf_op jit(solution)/shard_map/ppermute | solution.py:330
  49.9 5.0 %copy-start.12 = (bf16[2,2,640,128]{3,2,1,0:T(8,128)(2,1)}, bf16[2,2,640,128]{3,2,1,0:T(8,128)(2,1)S(1)}, u32[]{:S(2)}) copy-start(bf16[2,2,640,128]{3,2,1,0:T(8,128)(2,1)S(1)} %collective-permute-done.3.b3_ref) | copy-start | bytes 1966084
  51.1 19.9 %collective-permute-start.6 = (bf16[3,2048,128]{2,1,0:T(8,128)(2,1)}, bf16[3,2048,128]{2,1,0:T(8,128)(2,1)}, u32[]{:S(2)}, u32[]{:S(2)}) collective-permute-start(bf16[3,2048,128]{2,1,0:T(8,128)(2,1)} %collective-permute-done.5.w0_ref), channel_id=1, source_target_pairs={{0,1},{1,0},{2,3},{3,2},{4,5},{5,4},{6,7},{7,6},{8,9},{9,8},{10,11... | collective-permute-start | bytes 4718600 | tf_op jit(solution)/shard_map/ppermute | solution.py:297
  56.3 2.2 %copy-start.13 = (bf16[2,2,640,128]{3,2,1,0:T(8,128)(2,1)S(1)}, bf16[2,2,640,128]{3,2,1,0:T(8,128)(2,1)}, u32[]{:S(2)}) copy-start(bf16[2,2,640,128]{3,2,1,0:T(8,128)(2,1)} %copy-done.12) | copy-start | bytes 1966084
  56.4 20.5 %copy-start.1 = (bf16[3,2048,128]{2,1,0:T(8,128)(2,1)}, bf16[3,2048,128]{2,1,0:T(8,128)(2,1)S(1)}, u32[]{:S(2)}) copy-start(bf16[3,2048,128]{2,1,0:T(8,128)(2,1)S(1)} %pad_maximum_fusion.1.w0_ref) | copy-start | bytes 4718596
  56.4 24.0 %collective-permute-start.7 = (bf16[3,2048,128]{2,1,0:T(8,128)(2,1)S(1)}, bf16[3,2048,128]{2,1,0:T(8,128)(2,1)S(1)}, u32[]{:S(2)}, u32[]{:S(2)}) collective-permute-start(bf16[3,2048,128]{2,1,0:T(8,128)(2,1)S(1)} %pad_maximum_fusion.1.w0_ref), channel_id=1, source_target_pairs={{0,1},{1,0},{2,3},{3,2},{4,5},{5,4},{6,7},{7,6},{8,9},{9,8},{10,11... | collective-permute-start | bytes 4718600 | tf_op jit(solution)/shard_map/ppermute | solution.py:297
  58.5 11.6 %collective-permute-start.4 = (bf16[2,2,640,128]{3,2,1,0:T(8,128)(2,1)S(1)}, bf16[2,2,640,128]{3,2,1,0:T(8,128)(2,1)S(1)}, u32[]{:S(2)}, u32[]{:S(2)}) collective-permute-start(bf16[2,2,640,128]{3,2,1,0:T(8,128)(2,1)S(1)} %copy-done.13), channel_id=1, source_target_pairs={{0,14},{1,3},{2,4},{3,1},{4,2},{5,7},{6,8},{7,5},{8,6},{9,11},{10,... | collective-permute-start | bytes 1966088 | tf_op jit(solution)/shard_map/ppermute | solution.py:330
  70.1 0.8 copy-start.14
  76.9 14.9 %collective-permute-start.8 = (bf16[4,584,128]{2,1,0:T(8,128)(2,1)}, bf16[4,584,128]{2,1,0:T(8,128)(2,1)}, u32[]{:S(2)}, u32[]{:S(2)}) collective-permute-start(bf16[4,584,128]{2,1,0:T(8,128)(2,1)} %get-tuple-element.37), channel_id=1, source_target_pairs={{0,256},{256,0},{1,257},{257,1},{2,258},{258,2},{3,259},{259,3},{4... | collective-permute-start | bytes 1794056 | tf_op jit(solution)/shard_map/ppermute | solution.py:297
  80.4 1.2 copy-start.6
  94.5 6.6 %collective-permute-start.9 = (bf16[2,512,128]{2,1,0:T(8,128)(2,1)}, bf16[2,512,128]{2,1,0:T(8,128)(2,1)S(1)}, u32[]{:S(2)}, u32[]{:S(2)}) collective-permute-start(bf16[2,512,128]{2,1,0:T(8,128)(2,1)} %get-tuple-element.41), channel_id=1, source_target_pairs={{0,1},{1,0},{2,3},{3,2},{4,5},{5,4},{6,7},{7,6},{8,9},{9,8},{10,11... | collective-permute-start | bytes 786440 | tf_op jit(solution)/shard_map/ppermute | solution.py:297
  102.1 12.3 %copy-start.4 = (bf16[2,2,512,128]{3,2,1,0:T(8,128)(2,1)}, bf16[2,2,512,128]{3,2,1,0:T(8,128)(2,1)S(1)}, u32[]{:S(2)}) copy-start(bf16[2,2,512,128]{3,2,1,0:T(8,128)(2,1)S(1)} %get-tuple-element.46.near_ref) | copy-start | bytes 1572868
  102.1 11.1 %collective-permute-start.10 = (bf16[2,2,512,128]{3,2,1,0:T(8,128)(2,1)S(1)}, bf16[2,2,512,128]{3,2,1,0:T(8,128)(2,1)S(1)}, u32[]{:S(2)}, u32[]{:S(2)}) collective-permute-start(bf16[2,2,512,128]{3,2,1,0:T(8,128)(2,1)S(1)} %get-tuple-element.46.near_ref), channel_id=1, source_target_pairs={{0,16},{1,49},{16,0},{17,33},{32,48},{33,17},{48,32},{49,1},{2,18}... | collective-permute-start | bytes 1572872 | tf_op jit(solution)/shard_map/ppermute | solution.py:330
  105.4 41.3 %copy-start.3 = (bf16[4096,128]{1,0:T(8,128)(2,1)}, bf16[4096,128]{1,0:T(8,128)(2,1)S(1)}, u32[]{:S(2)}) copy-start(bf16[4096,128]{1,0:T(8,128)(2,1)S(1)} %slice_bitcast_fusion.w0_ref) | copy-start | bytes 3145732
  105.4 28.5 %collective-permute-start.13 = (bf16[4096,128]{1,0:T(8,128)(2,1)S(1)}, bf16[4096,128]{1,0:T(8,128)(2,1)}, u32[]{:S(2)}, u32[]{:S(2)}) collective-permute-start(bf16[4096,128]{1,0:T(8,128)(2,1)S(1)} %slice_bitcast_fusion.w0_ref), channel_id=1, source_target_pairs={{0,256},{256,0},{1,257},{257,1},{2,258},{258,2},{3,259},{259,3},{4... | collective-permute-start | bytes 3145736 | tf_op jit(solution)/shard_map/ppermute | solution.py:297
  113.3 33.4 %copy-start.5 = (bf16[2,2,512,128]{3,2,1,0:T(8,128)(2,1)}, bf16[2,2,512,128]{3,2,1,0:T(8,128)(2,1)S(1)}, u32[]{:S(2)}) copy-start(bf16[2,2,512,128]{3,2,1,0:T(8,128)(2,1)S(1)} %collective-permute-done.10.next_ref) | copy-start | bytes 1572868
  114.5 39.4 %collective-permute-start.11 = (bf16[2,2,2,512,128]{4,3,2,1,0:T(8,128)(2,1)}, bf16[2,2,2,512,128]{4,3,2,1,0:T(8,128)(2,1)S(1)}, u32[]{:S(2)}, u32[]{:S(2)}) collective-permute-start(bf16[2,2,2,512,128]{4,3,2,1,0:T(8,128)(2,1)} %pad_maximum_fusion.2), channel_id=1, source_target_pairs={{0,48},{1,17},{16,32},{17,1},{32,16},{33,49},{48,0},{49,33},{2,50}... | collective-permute-start | bytes 3145736 | tf_op jit(solution)/shard_map/ppermute | solution.py:330
  116.4 30.3 %all-to-all-start = ((bf16[8,192,128]{2,1,0:T(8,128)(2,1)}), bf16[8,192,128]{2,1,0:T(8,128)(2,1)S(1)}, u32[]{:S(2)}, u32[]{:S(2)}) async-start(bf16[8,192,128]{2,1,0:T(8,128)(2,1)} %bitcast.17), calls=%async_computation | async-start | bytes 786432 | tf_op jit(solution)/shard_map/all_to_all | solution.py:385
  125.8 40.7 %collective-permute-start.12 = (bf16[4096,128]{1,0:T(8,128)(2,1)S(1)}, bf16[4096,128]{1,0:T(8,128)(2,1)}, u32[]{:S(2)}, u32[]{:S(2)}) collective-permute-start(bf16[4096,128]{1,0:T(8,128)(2,1)S(1)} %slice_bitcast_fusion.w0_ref), channel_id=1, source_target_pairs={{0,1},{1,0},{2,3},{3,2},{4,5},{5,4},{6,7},{7,6},{8,9},{9,8},{10,11... | collective-permute-start | bytes 3145736 | tf_op jit(solution)/shard_map/ppermute | solution.py:297
  133.8 32.7 %collective-permute-start.14 = (bf16[4096,128]{1,0:T(8,128)(2,1)}, bf16[4096,128]{1,0:T(8,128)(2,1)}, u32[]{:S(2)}, u32[]{:S(2)}) collective-permute-start(bf16[4096,128]{1,0:T(8,128)(2,1)} %collective-permute-done.13.w2_ref), channel_id=1, source_target_pairs={{0,1},{1,0},{2,3},{3,2},{4,5},{5,4},{6,7},{7,6},{8,9},{9,8},{10,11... | collective-permute-start | bytes 3145736 | tf_op jit(solution)/shard_map/ppermute | solution.py:297
  146.6 1.0 copy-start.2
  153.9 1.0 copy-start.10
  161.5 17.5 %all-to-all-start.1 = ((bf16[16,72,128]{2,1,0:T(8,128)(2,1)}), bf16[16,72,128]{2,1,0:T(8,128)(2,1)S(1)}, u32[]{:S(2)}, u32[]{:S(2)}) async-start(bf16[16,72,128]{2,1,0:T(8,128)(2,1)} %bitcast.52), calls=%async_computation.1 | async-start | bytes 589824 | tf_op jit(solution)/shard_map/all_to_all | solution.py:398
  179.0 0.7 copy-start.9

commit v2 on v1

--- a/solution.py
+++ b/solution.py
@@ -54,20 +54,60 @@
     return jnp.sum(jnp.where(same, row, 0.0), axis=1, keepdims=True)
 
 
-def far_kernel(source_ref, b0_ref, b1_ref, b2_ref, b3_ref, b4_ref, gain_ref, w0_ref, w1_ref, lhs_ref, squares_ref, send_ref):
+def normed(ref, gain, lhs_ref, slot, square):
+    for i in range(2):
+        wide = ref[i].astype(F32)
+        square = square + wide * wide
+        lanes = slice(i * 128, (i + 1) * 128)
+        lhs_ref[slot, :HALF, lanes] = (wide[:HALF] * gain[i, 0:1]).astype(BF16)
+        lhs_ref[slot, HALF:, lanes] = (wide[HALF:] * gain[i, 1:2]).astype(BF16)
+    return square
+
+
+def columns(pieces):
+    return jnp.concatenate(pieces, axis=1)
+
+
+def rows_of(ref, which, source_ref, slots):
+    picked = [
+        ref[which, pl.ds(pl.multiple_of(source_ref[k] * 256, 256), 256), :] for k in slots
+    ]
+    return jnp.concatenate(picked, axis=0)
+
+
+def early_kernel(source_ref, b0_ref, b1_ref, b2_ref, b3_ref, gain_ref, w0_ref, w1_ref, lhs_ref, square_ref, kv_ref, q_ref):
     square = jnp.zeros((ROWS_IN, 128), F32)
-    pieces = [b0_ref, b1_ref]
-    for ref in (b2_ref, b3_ref, b4_ref):
-        pieces += [ref.at[0], ref.at[1]]
+    pieces = [b0_ref, b1_ref, b2_ref.at[0], b2_ref.at[1], b3_ref.at[0], b3_ref.at[1]]
     for k, ref in enumerate(pieces):
-        source = source_ref[k]
-        for i in range(2):
-            wide = ref[i].astype(F32)
-            square = square + wide * wide
-            gain = gain_ref[source, i]
-            lanes = slice(i * 128, (i + 1) * 128)
-            lhs_ref[source, :HALF, lanes] = (wide[:HALF] * gain[0:1]).astype(BF16)
-            lhs_ref[source, HALF:, lanes] = (wide[HALF:] * gain[1:2]).astype(BF16)
+        square = normed(ref, gain_ref[source_ref[k]], lhs_ref, k, square)
+    square_ref[...] = square
+    lhs = columns([lhs_ref[k] for k in range(6)])
+    for m, ref in enumerate((w0_ref, w1_ref)):
+        pair = columns([rows_of(ref, i, source_ref, range(6)) for i in range(2)])
+        kv_ref[m] = dot(lhs[:HALF], pair, ((1,), (0,)))
+        q_ref[m] = dot(lhs[HALF:], rows_of(ref, 2, source_ref, range(6)), ((1,), (0,)))
+
+
+def project_early(source, blocks, gains, weights):
+    vmem = pl.BlockSpec(memory_space=pltpu.VMEM)
+    return pl.pallas_call(
+        early_kernel,
+        in_specs=[pl.BlockSpec(memory_space=pltpu.SMEM)] + [vmem] * 7,
+        out_specs=[vmem] * 4,
+        out_shape=[
+            jax.ShapeDtypeStruct((6, ROWS_IN, 256), BF16),
+            jax.ShapeDtypeStruct((ROWS_IN, 128), F32),
+            jax.ShapeDtypeStruct((2, HALF, 256), F32),
+            jax.ShapeDtypeStruct((2, 128, 128), F32),
+        ],
+        name="project_early",
+    )(source, *blocks, gains, *weights)
+
+
+def late_kernel(source_ref, b4_ref, gain_ref, w00_ref, w01_ref, w10_ref, w11_ref, square_ref, kv_ref, q_ref, lhs_ref, squares_ref, send_ref):
+    square = square_ref[...]
+    for k in range(2):
+        square = normed(b4_ref.at[k], gain_ref[source_ref[6 + k]], lhs_ref, k, square)
     sums = jnp.sum(square, axis=1, keepdims=True)
     tail = [column_to_row(sums[k * 128 : (k + 1) * 128]) for k in range(5)]
     squares = jnp.concatenate(tail + [jnp.zeros((3, 128), F32)], axis=0)
@@ -76,53 +116,73 @@
     lower = (squares - upper.astype(F32)).astype(BF16)
     for i in range(4):
         send_ref[i, HALF + 64 :, :] = lower if i == 1 else upper
-    lhs = jnp.concatenate([lhs_ref[y] for y in range(8)], axis=1)
-    for m, ref in enumerate((w0_ref, w1_ref)):
-        pair = jnp.concatenate([ref[0], ref[1]], axis=1)
-        both = dot(lhs[:HALF], pair, ((1,), (0,)))
-        query = dot(lhs[HALF:], ref[2], ((1,), (0,)))
+    lhs = columns([lhs_ref[k] for k in range(2)])
+    for m, (one, two) in enumerate(((w00_ref, w01_ref), (w10_ref, w11_ref))):
+        rows = [jnp.concatenate([one[i], two[i]], axis=0) for i in range(3)]
+        both = kv_ref[m] + dot(lhs[:HALF], columns(rows[:2]), ((1,), (0,)))
+        query = q_ref[m] + dot(lhs[HALF:], rows[2], ((1,), (0,)))
         for i in range(2):
             send_ref[2 * m + i, :HALF, :] = both[:, i * 128 : (i + 1) * 128].astype(BF16)
             send_ref[2 * m + i, HALF : HALF + 64, :] = query[i * 64 : (i + 1) * 64].astype(BF16)
 
 
-def project_far(source, blocks, gains, weights):
-    vmem = pl.BlockSpec(memory_space=pltpu.VMEM)
-    return pl.pallas_call(
-        far_kernel,
-        in_specs=[pl.BlockSpec(memory_space=pltpu.SMEM)] + [vmem] * 8,
-        out_specs=[vmem] * 3,
+def whole_spec(*shape):
+    return pl.BlockSpec(shape, lambda i, *_: (0,) * len(shape))
+
+
+def project_late(source, block, gains, weights, square, kv, query):
+    picked = [pl.BlockSpec((3, 256, 128), lambda i, s, k=k: (0, s[6 + k], 0)) for k in range(2)]
+    return pl.pallas_call(
+        late_kernel,
+        grid_spec=pltpu.PrefetchScalarGridSpec(
+            num_scalar_prefetch=1,
+            grid=(1,),
+            in_specs=[
+                whole_spec(2, 2, ROWS_IN, 128),
+                whole_spec(8, 2, 2, 128),
+                *picked,
+                *picked,
+                whole_spec(ROWS_IN, 128),
+                whole_spec(2, HALF, 256),
+                whole_spec(2, 128, 128),
+            ],
+            out_specs=[
+                whole_spec(2, ROWS_IN, 256),
+                whole_spec(8, 128),
+                whole_spec(4, HALF + 72, 128),
+            ],
+        ),
         out_shape=[
-            jax.ShapeDtypeStruct((8, ROWS_IN, 256), BF16),
+            jax.ShapeDtypeStruct((2, ROWS_IN, 256), BF16),
             jax.ShapeDtypeStruct((8, 128), F32),
             jax.ShapeDtypeStruct((4, HALF + 72, 128), BF16),
         ],
-        name="project_far",
-    )(source, *blocks, gains, *weights)
-
-
-def near_kernel(lhs_ref, w0_ref, w1_ref, keep_ref, keep_q_ref):
-    lhs = jnp.concatenate([lhs_ref[y] for y in range(8)], axis=1)
+        name="project_late",
+    )(source, block, gains, weights[0], weights[0], weights[1], weights[1], square, kv, query)
+
+
+def near_kernel(source_ref, early_ref, late_ref, w0_ref, w1_ref, keep_ref, keep_q_ref):
+    lhs = columns([early_ref[k] for k in range(6)] + [late_ref[k] for k in range(2)])
     for m, ref in enumerate((w0_ref, w1_ref)):
-        pair = jnp.concatenate([ref[0], ref[1]], axis=1)
+        pair = columns([rows_of(ref, i, source_ref, range(8)) for i in range(2)])
         both = dot(lhs[:HALF], pair, ((1,), (0,)))
         keep_ref[m, 0] = both[:, :128]
         keep_ref[m, 1] = both[:, 128:]
-        keep_q_ref[m] = dot(lhs[HALF:], ref[2], ((1,), (0,)))
-
-
-def project_near(lhs, weights):
+        keep_q_ref[m] = dot(lhs[HALF:], rows_of(ref, 2, source_ref, range(8)), ((1,), (0,)))
+
+
+def project_near(source, early, late, weights):
     vmem = pl.BlockSpec(memory_space=pltpu.VMEM)
     return pl.pallas_call(
         near_kernel,
-        in_specs=[vmem] * 3,
+        in_specs=[pl.BlockSpec(memory_space=pltpu.SMEM)] + [vmem] * 4,
         out_specs=[vmem] * 2,
         out_shape=[
             jax.ShapeDtypeStruct((2, 2, HALF, 128), F32),
             jax.ShapeDtypeStruct((2, 128, 128), F32),
         ],
         name="project_near",
-    )(lhs, *weights)
+    )(source, early, late, *weights)
 
 
 def finish_kernel(source_ref, keep_ref, keep_q_ref, squares_ref, other_ref, count_ref, own_ref, give_ref, q_ref):
@@ -373,29 +433,31 @@
     fourth = exchange(third, "y", 8, 1)
     diagonal = swap(after(across, third), "c")
 
-    lhs, squares, send = project_far(
-        source, (chunk, first, second, third, fourth), gains, (across, diagonal)
-    )
-    wo = after(projections[1, 1], third)
-    wo_section = swap(wo, "s")
+    far = (across, diagonal)
+    early, square, kv, query = project_early(source, (chunk, first, second, third), gains, far)
+    late, squares, send = project_late(source, fourth, gains, far, square, kv, query)
     other = swap(send, "s")
-    keep, keep_q = project_near(lhs, (mine, beside))
+    keep, keep_q = project_near(source, early, late, (mine, beside))
     near, give, queries = finish(source, keep, keep_q, squares, other, counts)
     queries = queries.reshape(8, 192, 128)
     queries = lax.all_to_all(queries, ("zh", "c"), 0, 0)
     near = jnp.stack([near, swap(give, "c")])
     following = exchange(near, "x", 4, 0)
+    following = after(following, queries)
     beyond = exchange(jnp.stack([near, following]), "x", 4, 1)
     queries = queries.reshape(4, 2, 192, 128)
     counts = queries[:, :, 128:].reshape(4, 2, 2, 8, HALF).transpose(0, 3, 1, 2, 4)
     counts = counts.reshape(4, 8, 4, HALF)
 
+    wo = after(projections[1, 1], first)
+    wo_section = swap(after(wo, queries), "s")
     wo_beside = swap(wo, "c")
     wo_diagonal = swap(wo_section, "c")
 
     part, total = attend_near(order, queries, near, following, counts)
     parts = attend_far(order, queries, beyond, counts, part, total)
-    parts = lax.all_to_all(parts.reshape(16, ROWS, HEAD_DIM), ("s", "zh", "c"), 0, 0)
+    parts = parts.reshape(16, ROWS, HEAD_DIM)
+    parts = lax.all_to_all(parts, ("s", "zh", "c"), 0, 0)
     place = (section * 2 + core).astype(jnp.int32).reshape(1)
     weights = (wo, wo_beside, wo_section, wo_diagonal)
     out = mix(place, parts.reshape(2, 4, 2, ROWS, HEAD_DIM), weights)

time: 211 us -> 210 us (level)
  waiting for transfers between devices: 70.9 us -> 65.5 us
  Pallas kernels: 31.9 us -> 35 us
  starting transfers between devices: 59.4 us -> 61.7 us
    ppermute x6, waiting for transfers between devices: 35.9 us -> 26.8 us  [exchange(): return lax.ppermute(value, (axis, 'c'), pairs(size, turn))]
    ppermute x9, waiting for transfers between devices: 13.6 us -> 20.2 us  [swap(): return lax.ppermute(value, axis, [(0, 1), (1, 0)])]
    ppermute x6, starting transfers between devices: 11.6 us -> 15.3 us  [exchange(): return lax.ppermute(value, (axis, 'c'), pairs(size, turn))]
    all_to_all x1, starting transfers between devices: 9.46 us -> 5.84 us  [step(): queries = lax.all_to_all(queries, ('zh', 'c'), 0, 0)]
    ppermute x9, starting transfers between devices: 33.4 us -> 37 us  [swap(): return lax.ppermute(value, axis, [(0, 1), (1, 0)])]
    pallas_call x2 -> x3, Pallas kernels: 11.2 us -> 14.3 us  [the longest x1 5.26 us: project_early(): pl.pallas_call(early_kernel, in_specs=[pl.BlockSpec(memory_space=pltpu.SM...]
    all_to_all x1, waiting for transfers between devices: 8.85 us -> 6 us  [step(): queries = lax.all_to_all(queries, ('zh', 'c'), 0, 0)]
    concatenate x2, other arithmetic: 0.28 us -> 2.61 us  [feature_rows(): return jnp.concatenate([encoder[0], decoder[0]], axis=0)]
  transfers between devices with their start and end apart: 17 -> 17, of which waited for: 11 -> 9; matrix products, arithmetic and copies ran while one was open for 7% -> 8% of each run, Pallas kernels for 12% -> 13%
where the time goes in v2:
time: 210 us; the launch traced here: 208 us
  waiting for transfers between devices  65.5 us (31%)
  starting transfers between devices  61.7 us (29%)
  Pallas kernels  35 us (17%)
  blocking collectives  23.7 us (11%)
  local copies, waits for them, and re-layouts  14.5 us (7%)
  other arithmetic  6.54 us (3%)
    ppermute x9, starting transfers between devices, swap(): return lax.ppermute(value, axis, [(0, 1), (1, 0)])  37 us
    ppermute x6, waiting for transfers between devices, exchange(): return lax.ppermute(value, (axis, 'c'), pairs(size, turn))  26.8 us
    all_to_all x1, blocking collectives, step(): out = lax.all_to_all(out, ('s', 'y', 'c'), 0, 0)  23.7 us
    ppermute x9, waiting for transfers between devices, swap(): return lax.ppermute(value, axis, [(0, 1), (1, 0)])  20.2 us
    ppermute x6, starting transfers between devices, exchange(): return lax.ppermute(value, (axis, 'c'), pairs(size, turn))  15.3 us
    all_to_all x1, waiting for transfers between devices, step(): parts = lax.all_to_all(parts, ('s', 'zh', 'c'), 0, 0)  12.5 us
    pallas_call x1, Pallas kernels, attend_far(): pl.pallas_call(far_attend_kernel, grid_spec=pltpu.PrefetchScalarGridSpec(...  6.62 us
    pallas_call x1, Pallas kernels, attend_near(): pl.pallas_call(near_attend_kernel, grid_spec=pltpu.PrefetchScalarGridSpec...  6.3 us
  transfers between devices with their start and end apart: 17, of which 9 were waited for; matrix products, arithmetic and copies ran while one was open for 8% of the time, Pallas kernels for 13%

profile of v2, /device:TPU:1, one launch (start us, length us, event | category | flops | bytes accessed | tf_op | source)
XLA Modules:
  0.0 208.2 jit_solution(8277904385638738522)
XLA Ops:
  0.0 0.8 constant_dynamic-slice_fusion.3
  0.8 1.0 constant_dynamic-slice_fusion.4
  1.8 8.7 %collective-permute-start = (bf16[640,128]{1,0:T(8,128)(2,1)S(1)}, bf16[640,128]{1,0:T(8,128)(2,1)S(1)}, u32[]{:S(2)}, u32[]{:S(2)}) collective-permute-start(bf16[640,128]{1,0:T(8,128)(2,1)S(1)} %pad_maximum_fusion.6), channel_id=1, source_target_pairs={{0,1},{1,0},{2,3},{3,2},{4,5},{5,4},{6,7},{7,6},{8,9},{9,8},{10,11... | collective-permute-start | bytes 491528 | tf_op jit(solution)/shard_map/ppermute | solution.py:357
  10.6 1.1 dynamic-slice_bitcast_fusion.3
  11.7 1.3 dynamic-slice_bitcast_fusion.1
  13.0 1.3 pad_maximum_fusion
  14.3 1.9 collective-permute-start.4
  16.2 0.1 convert_reduce_fusion
  16.3 0.1 pad_add_fusion.1
  16.5 1.9 collective-permute-start.1
  18.4 0.6 constant_dynamic-slice_fusion
  19.1 6.4 %collective-permute-done.1.b1_ref = bf16[2,640,128]{2,1,0:T(8,128)(2,1)S(1)} collective-permute-done((bf16[2,640,128]{2,1,0:T(8,128)(2,1)S(1)}, bf16[2,640,128]{2,1,0:T(8,128)(2,1)S(1)}, u32[]{:S(2)}, u32[]{:S(2)}) %collective-permute-start.1) | collective-permute-done | bytes 327712 | tf_op jit(solution)/shard_map/ppermute | solution.py:390
  25.6 2.1 collective-permute-start.2
  27.7 0.5 fusion.1
  28.2 0.3 convolution_convert_fusion
  28.5 0.3 copy.19
  28.8 0.5 reshape.110
  29.4 8.1 %collective-permute-done.2.b2_ref = bf16[2,2,640,128]{3,2,1,0:T(8,128)(2,1)} collective-permute-done((bf16[2,2,640,128]{3,2,1,0:T(8,128)(2,1)S(1)}, bf16[2,2,640,128]{3,2,1,0:T(8,128)(2,1)}, u32[]{:S(2)}, u32[]{:S(2)}) %collective-permute-start.2) | collective-permute-done | bytes 655392 | tf_op jit(solution)/shard_map/ppermute | solution.py:390
  37.5 1.9 collective-permute-start.3
  39.4 0.1 copy.20
  39.5 0.7 reshape.111.count_ref
  40.2 0.1 broadcast_add_fusion
  40.2 0.7 add.128.order_ref
  40.9 0.6 pad_add_fusion.source_ref
  41.5 8.8 %collective-permute-done.3.b3_ref = bf16[2,2,640,128]{3,2,1,0:T(8,128)(2,1)} collective-permute-done((bf16[2,2,640,128]{3,2,1,0:T(8,128)(2,1)}, bf16[2,2,640,128]{3,2,1,0:T(8,128)(2,1)}, u32[]{:S(2)}, u32[]{:S(2)}) %collective-permute-start.3) | collective-permute-done | bytes 655392 | tf_op jit(solution)/shard_map/ppermute | solution.py:390
  50.3 2.0 collective-permute-done.4.w0_ref.w00_ref.w01_ref
  52.3 2.8 %collective-permute-start.5 = (bf16[3,2048,128]{2,1,0:T(8,128)(2,1)S(1)}, bf16[3,2048,128]{2,1,0:T(8,128)(2,1)S(1)}, u32[]{:S(2)}, u32[]{:S(2)}) collective-permute-start(bf16[3,2048,128]{2,1,0:T(8,128)(2,1)S(1)} %collective-permute-done.4.w0_ref.w00_ref.w01_ref), channel_id=1, source_target_pairs={{0,1},{1,0},{2,3},{3,2},{4,5},{5,4},{6,7},{7,6},{8,9},{9,8},{10,11... | collective-permute-start | bytes 4718600 | tf_op jit(solution)/shard_map/ppermute | solution.py:357
  55.1 1.1 dynamic-slice_bitcast_fusion.2
  56.2 1.3 dynamic-slice_bitcast_fusion
  57.5 1.3 pad_maximum_fusion.1.w0_ref
  58.8 1.9 collective-permute-start.7
  60.7 1.9 collective-permute-start.6
  62.7 1.2 copy-done.2
  63.9 5.3 %project_early.1 = (bf16[6,640,256]{2,1,0:T(8,128)(2,1)}, f32[640,128]{1,0:T(8,128)}, f32[2,512,256]{2,1,0:T(8,128)}, f32[2,128,128]{2,1,0:T(8,128)}) custom-call(s32[9]{0:T(128)} %pad_add_fusion.source_ref, bf16[2,640,128]{2,1,0:T(8,128)(2,1)} %copy-done.8, bf16[2,640,128]{2,1,0:T(8,128)(2,1)} %copy-done.7, ...), custom_call_target="tpu_custom_call" | custom-call | tf_op jit(solution)/shard_map/project_early/pallas_call | solution.py:93
  69.2 3.5 %collective-permute-done.6.b4_ref = bf16[2,2,640,128]{3,2,1,0:T(8,128)(2,1)} collective-permute-done((bf16[2,2,640,128]{3,2,1,0:T(8,128)(2,1)}, bf16[2,2,640,128]{3,2,1,0:T(8,128)(2,1)}, u32[]{:S(2)}, u32[]{:S(2)}) %collective-permute-start.6) | collective-permute-done | bytes 655392 | tf_op jit(solution)/shard_map/ppermute | solution.py:390
  72.7 3.8 %project_late.1 = (bf16[2,640,256]{2,1,0:T(8,128)(2,1)}, f32[8,128]{1,0:T(8,128)}, bf16[4,584,128]{2,1,0:T(8,128)(2,1)}) custom-call(s32[9]{0:T(128)} %pad_add_fusion.source_ref, bf16[2,2,640,128]{3,2,1,0:T(8,128)(2,1)} %collective-permute-done.6.b4_ref, f32[8,2,2,128]{3,2,1,0:T(2,128)} %bitcast.61, bf16[3,2048,128]{2,1,0:T(8,128)(2,1)} %copy-done.1, ...), custom_call_target="tpu_custom_call" | custom-call | tf_op jit(solution)/shard_map/project_late/pallas_call | solution.py:135
  76.4 2.7 %collective-permute-start.8 = (bf16[4,584,128]{2,1,0:T(8,128)(2,1)}, bf16[4,584,128]{2,1,0:T(8,128)(2,1)S(1)}, u32[]{:S(2)}, u32[]{:S(2)}) collective-permute-start(bf16[4,584,128]{2,1,0:T(8,128)(2,1)} %get-tuple-element.47), channel_id=1, source_target_pairs={{0,256},{256,0},{1,257},{257,1},{2,258},{258,2},{3,259},{259,3},{4... | collective-permute-start | bytes 1794056 | tf_op jit(solution)/shard_map/ppermute | solution.py:357
  79.1 5.2 %project_near.1 = (f32[2,2,512,128]{3,2,1,0:T(8,128)}, f32[2,128,128]{2,1,0:T(8,128)}) custom-call(s32[9]{0:T(128)} %pad_add_fusion.source_ref, bf16[6,640,256]{2,1,0:T(8,128)(2,1)} %get-tuple-element.38.early_ref, bf16[2,640,256]{2,1,0:T(8,128)(2,1)} %get-tuple-element.42.late_ref, bf16[3,2048,128]{2,1,0:T(8,128)(2,1)} %pad_maximum_fusion.1.w0_ref, ...), custom_call_target="tpu_custom_call" | custom-call | tf_op jit(solution)/shard_map/project_near/pallas_call | solution.py:176
  84.4 6.6 %collective-permute-done.8.other_ref = bf16[4,584,128]{2,1,0:T(8,128)(2,1)S(1)} collective-permute-done((bf16[4,584,128]{2,1,0:T(8,128)(2,1)}, bf16[4,584,128]{2,1,0:T(8,128)(2,1)S(1)}, u32[]{:S(2)}, u32[]{:S(2)}) %collective-permute-start.8) | collective-permute-done | bytes 598048 | tf_op jit(solution)/shard_map/ppermute | solution.py:357
  91.0 0.8 copy-done.11
  91.9 2.7 %finish.1 = (bf16[2,512,128]{2,1,0:T(8,128)(2,1)}, bf16[2,512,128]{2,1,0:T(8,128)(2,1)}, bf16[4,2,192,128]{3,2,1,0:T(8,128)(2,1)}) custom-call(s32[9]{0:T(128)} %pad_add_fusion.source_ref, f32[2,2,512,128]{3,2,1,0:T(8,128)} %get-tuple-element.44.keep_ref, f32[2,128,128]{2,1,0:T(8,128)} %get-tuple-element.45.keep_q_ref, ...), custom_call_target="tpu_custom_call" | custom-call | tf_op jit(solution)/shard_map/finish/pallas_call | solution.py:215
  94.5 5.3 %collective-permute-start.9 = (bf16[2,512,128]{2,1,0:T(8,128)(2,1)}, bf16[2,512,128]{2,1,0:T(8,128)(2,1)S(1)}, u32[]{:S(2)}, u32[]{:S(2)}) collective-permute-start(bf16[2,512,128]{2,1,0:T(8,128)(2,1)} %get-tuple-element.51), channel_id=1, source_target_pairs={{0,1},{1,0},{2,3},{3,2},{4,5},{5,4},{6,7},{7,6},{8,9},{9,8},{10,11... | collective-permute-start | bytes 786440 | tf_op jit(solution)/shard_map/ppermute | solution.py:357
  99.8 5.8 %all-to-all-start = ((bf16[8,192,128]{2,1,0:T(8,128)(2,1)}), bf16[8,192,128]{2,1,0:T(8,128)(2,1)S(1)}, u32[]{:S(2)}, u32[]{:S(2)}) async-start(bf16[8,192,128]{2,1,0:T(8,128)(2,1)} %bitcast.57), calls=%async_computation | async-start | bytes 786432 | tf_op jit(solution)/shard_map/all_to_all | solution.py:443
  105.7 1.0 fusion.16
  106.7 4.4 %collective-permute-start.10 = (bf16[2,2,512,128]{3,2,1,0:T(8,128)(2,1)S(1)}, bf16[2,2,512,128]{3,2,1,0:T(8,128)(2,1)S(1)}, u32[]{:S(2)}, u32[]{:S(2)}) collective-permute-start(bf16[2,2,512,128]{3,2,1,0:T(8,128)(2,1)S(1)} %get-tuple-element.58.near_ref), channel_id=1, source_target_pairs={{0,16},{1,49},{16,0},{17,33},{32,48},{33,17},{48,32},{49,1},{2,18}... | collective-permute-start | bytes 1572872 | tf_op jit(solution)/shard_map/ppermute | solution.py:390
  111.1 1.3 slice_bitcast_fusion.w0_ref
  112.4 6.0 %all-to-all-done = bf16[8,192,128]{2,1,0:T(8,128)(2,1)S(1)} async-done(((bf16[8,192,128]{2,1,0:T(8,128)(2,1)}), bf16[8,192,128]{2,1,0:T(8,128)(2,1)S(1)}, u32[]{:S(2)}, u32[]{:S(2)}) %all-to-all-start) | async-done | bytes 393248 | tf_op jit(solution)/shard_map/all_to_all | solution.py:443
  118.4 1.9 collective-permute-start.13
  120.4 1.2 pad_maximum_fusion.2
  121.6 3.1 %collective-permute-start.11 = (bf16[2,2,2,512,128]{4,3,2,1,0:T(8,128)(2,1)}, bf16[2,2,2,512,128]{4,3,2,1,0:T(8,128)(2,1)}, u32[]{:S(2)}, u32[]{:S(2)}) collective-permute-start(bf16[2,2,2,512,128]{4,3,2,1,0:T(8,128)(2,1)} %pad_maximum_fusion.2), channel_id=1, source_target_pairs={{0,48},{1,17},{16,32},{17,1},{32,16},{33,49},{48,0},{49,33},{2,50}... | collective-permute-start | bytes 3145736 | tf_op jit(solution)/shard_map/ppermute | solution.py:390
  124.7 6.8 %collective-permute-start.12 = (bf16[4096,128]{1,0:T(8,128)(2,1)S(1)}, bf16[4096,128]{1,0:T(8,128)(2,1)S(1)}, u32[]{:S(2)}, u32[]{:S(2)}) collective-permute-start(bf16[4096,128]{1,0:T(8,128)(2,1)S(1)} %slice_bitcast_fusion.w0_ref), channel_id=1, source_target_pairs={{0,1},{1,0},{2,3},{3,2},{4,5},{5,4},{6,7},{7,6},{8,9},{9,8},{10,11... | collective-permute-start | bytes 3145736 | tf_op jit(solution)/shard_map/ppermute | solution.py:357
  131.5 11.5 %collective-permute-done.13.w2_ref = bf16[4096,128]{1,0:T(8,128)(2,1)} collective-permute-done((bf16[4096,128]{1,0:T(8,128)(2,1)S(1)}, bf16[4096,128]{1,0:T(8,128)(2,1)}, u32[]{:S(2)}, u32[]{:S(2)}) %collective-permute-start.13) | collective-permute-done | bytes 1048608 | tf_op jit(solution)/shard_map/ppermute | solution.py:357
  143.0 4.9 %collective-permute-start.14 = (bf16[4096,128]{1,0:T(8,128)(2,1)}, bf16[4096,128]{1,0:T(8,128)(2,1)}, u32[]{:S(2)}, u32[]{:S(2)}) collective-permute-start(bf16[4096,128]{1,0:T(8,128)(2,1)} %collective-permute-done.13.w2_ref), channel_id=1, source_target_pairs={{0,1},{1,0},{2,3},{3,2},{4,5},{5,4},{6,7},{7,6},{8,9},{9,8},{10,11... | collective-permute-start | bytes 3145736 | tf_op jit(solution)/shard_map/ppermute | solution.py:357
  147.9 0.1 reshape.115
  148.0 0.1 copy.25
  148.1 0.7 reshape.116.count_ref
  148.9 6.3 %attend_near.1 = (f32[1024,128]{1,0:T(8,128)}, f32[1024,128]{1,0:T(8,128)}) custom-call(s32[8]{0:T(128)} %add.128.order_ref, bf16[4,2,192,128]{3,2,1,0:T(8,128)(2,1)} %bitcast.47, bf16[2,2,512,128]{3,2,1,0:T(8,128)(2,1)} %copy-done.5, bf16[2,2,512,128]{3,2,1,0:T(8,128)(2,1)} %copy-done.6, bf16[4,8,4,512]{3,2,1,0:T(4,128)(2,1)} %reshape.116.count_ref), custom_call_target="tpu_custom_call" | custom-call | tf_op jit(solution)/shard_map/attend_near/pallas_call | solution.py:272
  155.2 6.6 %attend_far.1 = bf16[2,4,2,72,128]{4,3,2,1,0:T(8,128)(2,1)} custom-call(s32[8]{0:T(128)} %add.128.order_ref, bf16[4,2,192,128]{3,2,1,0:T(8,128)(2,1)} %bitcast.48, bf16[2,2,2,512,128]{4,3,2,1,0:T(8,128)(2,1)} %collective-permute-done.11.far_ref, bf16[4,8,4,512]{3,2,1,0:T(4,128)(2,1)} %reshape.116.count_ref, f32[1024,128]{1,0:T(8,128)} %get-tuple-element.53.part_ref, ...), custom_call_target="tpu_custom_call" | custom-call | tf_op jit(solution)/shard_map/attend_far/pallas_call | solution.py:287
  161.8 3.6 %all-to-all-start.1 = ((bf16[16,72,128]{2,1,0:T(8,128)(2,1)}), bf16[16,72,128]{2,1,0:T(8,128)(2,1)S(1)}, u32[]{:S(2)}, u32[]{:S(2)}) async-start(bf16[16,72,128]{2,1,0:T(8,128)(2,1)} %bitcast.52), calls=%async_computation.1 | async-start | bytes 589824 | tf_op jit(solution)/shard_map/all_to_all | solution.py:460
  165.4 12.5 %all-to-all-done.1 = bf16[16,72,128]{2,1,0:T(8,128)(2,1)S(1)} async-done(((bf16[16,72,128]{2,1,0:T(8,128)(2,1)}), bf16[16,72,128]{2,1,0:T(8,128)(2,1)S(1)}, u32[]{:S(2)}, u32[]{:S(2)}) %all-to-all-start.1) | async-done | bytes 294944 | tf_op jit(solution)/shard_map/all_to_all | solution.py:460
  177.9 0.7 copy-done.9
  178.7 5.1 %mix.1 = bf16[32,64,128]{2,1,0:T(8,128)(2,1)} custom-call(s32[1]{0:T(128)} %bitcast.place_ref, bf16[2,4,2,72,128]{4,3,2,1,0:T(8,128)(2,1)} %bitcast.53, bf16[4096,128]{1,0:T(8,128)(2,1)} %copy-done.4, bf16[4096,128]{1,0:T(8,128)(2,1)} %copy-done.10, bf16[4096,128]{1,0:T(8,128)(2,1)} %collective-permute-done.13.w2_ref, ...), custom_call_target="tpu_custom_call" | custom-call | tf_op jit(solution)/shard_map/mix/pallas_call | solution.py:336
  183.8 23.7 %all_to_all.15 = bf16[32,64,128]{2,1,0:T(8,128)(2,1)S(1)} all-to-all(bf16[32,64,128]{2,1,0:T(8,128)(2,1)} %mix.1), channel_id=1, replica_groups=mesh['s'=2,'zh'=4,'x'=4,'y'=8,'c'=2] {'s','y','c'}, dimensions={0} | all-to-all | bytes 1048576 | tf_op jit(solution)/shard_map/all_to_all | solution.py:464
  207.5 0.7 reduce_sum.22
  (45 shorter events, 0.3 us)
Async XLA Ops:
  0.0 18.4 %copy-start = (f32[2,4096]{1,0:T(2,128)S(1)}, f32[2,4096]{1,0:T(2,128)}, u32[]{:S(2)}) copy-start(f32[2,4096]{1,0:T(2,128)} %param.11) | copy-start | bytes 98308
  1.8 14.6 %collective-permute-start = (bf16[640,128]{1,0:T(8,128)(2,1)S(1)}, bf16[640,128]{1,0:T(8,128)(2,1)S(1)}, u32[]{:S(2)}, u32[]{:S(2)}) collective-permute-start(bf16[640,128]{1,0:T(8,128)(2,1)S(1)} %pad_maximum_fusion.6), channel_id=1, source_target_pairs={{0,1},{1,0},{2,3},{3,2},{4,5},{5,4},{6,7},{7,6},{8,9},{9,8},{10,11... | collective-permute-start | bytes 491528 | tf_op jit(solution)/shard_map/ppermute | solution.py:357
  13.0 3.3 %copy-start.14 = (s32[4,2]{0,1:T(2,128)S(1)}, s32[4,2]{0,1:T(2,128)}, u32[]{:S(2)}) copy-start(s32[4,2]{0,1:T(2,128)} %param.9) | copy-start | bytes 100
  14.3 38.0 %collective-permute-start.4 = (bf16[3,2048,128]{2,1,0:T(8,128)(2,1)}, bf16[3,2048,128]{2,1,0:T(8,128)(2,1)S(1)}, u32[]{:S(2)}, u32[]{:S(2)}) collective-permute-start(bf16[3,2048,128]{2,1,0:T(8,128)(2,1)} %pad_maximum_fusion), channel_id=1, source_target_pairs={{0,256},{256,0},{1,257},{257,1},{2,258},{258,2},{3,259},{259,3},{4... | collective-permute-start | bytes 4718600 | tf_op jit(solution)/shard_map/ppermute | solution.py:357
  16.4 11.3 %copy-start.12 = (s32[8,128]{1,0:T(8,128)S(1)}, s32[8,128]{1,0:T(8,128)}, u32[]{:S(2)}) copy-start(s32[8,128]{1,0:T(8,128)} %param.8) | copy-start | bytes 12292
  16.5 11.7 %copy-start.8 = (bf16[2,640,128]{2,1,0:T(8,128)(2,1)}, bf16[2,640,128]{2,1,0:T(8,128)(2,1)S(1)}, u32[]{:S(2)}) copy-start(bf16[2,640,128]{2,1,0:T(8,128)(2,1)S(1)} %maximum_select_fusion.1.b0_ref) | copy-start | bytes 983044
  16.5 9.0 %collective-permute-start.1 = (bf16[2,640,128]{2,1,0:T(8,128)(2,1)S(1)}, bf16[2,640,128]{2,1,0:T(8,128)(2,1)S(1)}, u32[]{:S(2)}, u32[]{:S(2)}) collective-permute-start(bf16[2,640,128]{2,1,0:T(8,128)(2,1)S(1)} %maximum_select_fusion.1.b0_ref), channel_id=1, source_target_pairs={{0,2},{1,15},{2,0},{3,5},{4,6},{5,3},{6,4},{7,9},{8,10},{9,7},{10,... | collective-permute-start | bytes 983048 | tf_op jit(solution)/shard_map/ppermute | solution.py:390
  25.5 3.3 %copy-start.7 = (bf16[2,640,128]{2,1,0:T(8,128)(2,1)}, bf16[2,640,128]{2,1,0:T(8,128)(2,1)S(1)}, u32[]{:S(2)}) copy-start(bf16[2,640,128]{2,1,0:T(8,128)(2,1)S(1)} %collective-permute-done.1.b1_ref) | copy-start | bytes 983044
  25.6 13.8 %copy-start.13 = (s32[8]{0:T(128)S(1)}, s32[8]{0:T(128)}, u32[]{:S(2)}) copy-start(s32[8]{0:T(128)} %constant.129.clone) | copy-start | bytes 100
  25.6 11.9 %collective-permute-start.2 = (bf16[2,2,640,128]{3,2,1,0:T(8,128)(2,1)S(1)}, bf16[2,2,640,128]{3,2,1,0:T(8,128)(2,1)}, u32[]{:S(2)}, u32[]{:S(2)}) collective-permute-start(bf16[2,2,640,128]{3,2,1,0:T(8,128)(2,1)S(1)} %pad_maximum_fusion.3), channel_id=1, source_target_pairs={{0,14},{1,3},{2,4},{3,1},{4,2},{5,7},{6,8},{7,5},{8,6},{9,11},{10,... | collective-permute-start | bytes 1966088 | tf_op jit(solution)/shard_map/ppermute | solution.py:390
  37.5 12.8 %collective-permute-start.3 = (bf16[2,2,640,128]{3,2,1,0:T(8,128)(2,1)}, bf16[2,2,640,128]{3,2,1,0:T(8,128)(2,1)}, u32[]{:S(2)}, u32[]{:S(2)}) collective-permute-start(bf16[2,2,640,128]{3,2,1,0:T(8,128)(2,1)} %collective-permute-done.2.b2_ref), channel_id=1, source_target_pairs={{0,2},{1,15},{2,0},{3,5},{4,6},{5,3},{6,4},{7,9},{8,10},{9,7},{10,... | collective-permute-start | bytes 1966088 | tf_op jit(solution)/shard_map/ppermute | solution.py:390
  52.3 5.2 %copy-start.1 = (bf16[3,2048,128]{2,1,0:T(8,128)(2,1)}, bf16[3,2048,128]{2,1,0:T(8,128)(2,1)S(1)}, u32[]{:S(2)}) copy-start(bf16[3,2048,128]{2,1,0:T(8,128)(2,1)S(1)} %collective-permute-done.4.w0_ref.w00_ref.w01_ref) | copy-start | bytes 4718596
  52.3 10.3 %collective-permute-start.5 = (bf16[3,2048,128]{2,1,0:T(8,128)(2,1)S(1)}, bf16[3,2048,128]{2,1,0:T(8,128)(2,1)S(1)}, u32[]{:S(2)}, u32[]{:S(2)}) collective-permute-start(bf16[3,2048,128]{2,1,0:T(8,128)(2,1)S(1)} %collective-permute-done.4.w0_ref.w00_ref.w01_ref), channel_id=1, source_target_pairs={{0,1},{1,0},{2,3},{3,2},{4,5},{5,4},{6,7},{7,6},{8,9},{9,8},{10,11... | collective-permute-start | bytes 4718600 | tf_op jit(solution)/shard_map/ppermute | solution.py:357
  58.8 20.3 %collective-permute-start.7 = (bf16[3,2048,128]{2,1,0:T(8,128)(2,1)}, bf16[3,2048,128]{2,1,0:T(8,128)(2,1)}, u32[]{:S(2)}, u32[]{:S(2)}) collective-permute-start(bf16[3,2048,128]{2,1,0:T(8,128)(2,1)} %pad_maximum_fusion.1.w0_ref), channel_id=1, source_target_pairs={{0,1},{1,0},{2,3},{3,2},{4,5},{5,4},{6,7},{7,6},{8,9},{9,8},{10,11... | collective-permute-start | bytes 4718600 | tf_op jit(solution)/shard_map/ppermute | solution.py:357
  60.7 11.9 %collective-permute-start.6 = (bf16[2,2,640,128]{3,2,1,0:T(8,128)(2,1)}, bf16[2,2,640,128]{3,2,1,0:T(8,128)(2,1)}, u32[]{:S(2)}, u32[]{:S(2)}) collective-permute-start(bf16[2,2,640,128]{3,2,1,0:T(8,128)(2,1)} %collective-permute-done.3.b3_ref), channel_id=1, source_target_pairs={{0,14},{1,3},{2,4},{3,1},{4,2},{5,7},{6,8},{7,5},{8,6},{9,11},{10,... | collective-permute-start | bytes 1966088 | tf_op jit(solution)/shard_map/ppermute | solution.py:390
  62.7 1.2 copy-start.2
  76.4 14.6 %collective-permute-start.8 = (bf16[4,584,128]{2,1,0:T(8,128)(2,1)}, bf16[4,584,128]{2,1,0:T(8,128)(2,1)S(1)}, u32[]{:S(2)}, u32[]{:S(2)}) collective-permute-start(bf16[4,584,128]{2,1,0:T(8,128)(2,1)} %get-tuple-element.47), channel_id=1, source_target_pairs={{0,256},{256,0},{1,257},{257,1},{2,258},{258,2},{3,259},{259,3},{4... | collective-permute-start | bytes 1794056 | tf_op jit(solution)/shard_map/ppermute | solution.py:357
  91.0 0.8 copy-start.11
  94.5 11.2 %collective-permute-start.9 = (bf16[2,512,128]{2,1,0:T(8,128)(2,1)}, bf16[2,512,128]{2,1,0:T(8,128)(2,1)S(1)}, u32[]{:S(2)}, u32[]{:S(2)}) collective-permute-start(bf16[2,512,128]{2,1,0:T(8,128)(2,1)} %get-tuple-element.51), channel_id=1, source_target_pairs={{0,1},{1,0},{2,3},{3,2},{4,5},{5,4},{6,7},{7,6},{8,9},{9,8},{10,11... | collective-permute-start | bytes 786440 | tf_op jit(solution)/shard_map/ppermute | solution.py:357
  99.8 18.6 %all-to-all-start = ((bf16[8,192,128]{2,1,0:T(8,128)(2,1)}), bf16[8,192,128]{2,1,0:T(8,128)(2,1)S(1)}, u32[]{:S(2)}, u32[]{:S(2)}) async-start(bf16[8,192,128]{2,1,0:T(8,128)(2,1)} %bitcast.57), calls=%async_computation | async-start | bytes 786432 | tf_op jit(solution)/shard_map/all_to_all | solution.py:443
  106.7 14.8 %copy-start.5 = (bf16[2,2,512,128]{3,2,1,0:T(8,128)(2,1)}, bf16[2,2,512,128]{3,2,1,0:T(8,128)(2,1)S(1)}, u32[]{:S(2)}) copy-start(bf16[2,2,512,128]{3,2,1,0:T(8,128)(2,1)S(1)} %get-tuple-element.58.near_ref) | copy-start | bytes 1572868
  106.7 13.6 %collective-permute-start.10 = (bf16[2,2,512,128]{3,2,1,0:T(8,128)(2,1)S(1)}, bf16[2,2,512,128]{3,2,1,0:T(8,128)(2,1)S(1)}, u32[]{:S(2)}, u32[]{:S(2)}) collective-permute-start(bf16[2,2,512,128]{3,2,1,0:T(8,128)(2,1)S(1)} %get-tuple-element.58.near_ref), channel_id=1, source_target_pairs={{0,16},{1,49},{16,0},{17,33},{32,48},{33,17},{48,32},{49,1},{2,18}... | collective-permute-start | bytes 1572872 | tf_op jit(solution)/shard_map/ppermute | solution.py:390
  112.4 36.4 %copy-start.4 = (bf16[4096,128]{1,0:T(8,128)(2,1)}, bf16[4096,128]{1,0:T(8,128)(2,1)S(1)}, u32[]{:S(2)}) copy-start(bf16[4096,128]{1,0:T(8,128)(2,1)S(1)} %slice_bitcast_fusion.w0_ref) | copy-start | bytes 3145732
  118.4 30.4 %copy-start.3 = (bf16[8,192,128]{2,1,0:T(8,128)(2,1)}, bf16[8,192,128]{2,1,0:T(8,128)(2,1)S(1)}, u32[]{:S(2)}) copy-start(bf16[8,192,128]{2,1,0:T(8,128)(2,1)S(1)} %all-to-all-done) | copy-start | bytes 1179652
  118.4 24.6 %collective-permute-start.13 = (bf16[4096,128]{1,0:T(8,128)(2,1)S(1)}, bf16[4096,128]{1,0:T(8,128)(2,1)}, u32[]{:S(2)}, u32[]{:S(2)}) collective-permute-start(bf16[4096,128]{1,0:T(8,128)(2,1)S(1)} %slice_bitcast_fusion.w0_ref), channel_id=1, source_target_pairs={{0,256},{256,0},{1,257},{257,1},{2,258},{258,2},{3,259},{259,3},{4... | collective-permute-start | bytes 3145736 | tf_op jit(solution)/shard_map/ppermute | solution.py:357
  120.3 28.5 %copy-start.6 = (bf16[2,2,512,128]{3,2,1,0:T(8,128)(2,1)}, bf16[2,2,512,128]{3,2,1,0:T(8,128)(2,1)S(1)}, u32[]{:S(2)}) copy-start(bf16[2,2,512,128]{3,2,1,0:T(8,128)(2,1)S(1)} %collective-permute-done.10.next_ref) | copy-start | bytes 1572868
  121.6 33.6 %collective-permute-start.11 = (bf16[2,2,2,512,128]{4,3,2,1,0:T(8,128)(2,1)}, bf16[2,2,2,512,128]{4,3,2,1,0:T(8,128)(2,1)}, u32[]{:S(2)}, u32[]{:S(2)}) collective-permute-start(bf16[2,2,2,512,128]{4,3,2,1,0:T(8,128)(2,1)} %pad_maximum_fusion.2), channel_id=1, source_target_pairs={{0,48},{1,17},{16,32},{17,1},{32,16},{33,49},{48,0},{49,33},{2,50}... | collective-permute-start | bytes 3145736 | tf_op jit(solution)/shard_map/ppermute | solution.py:390
  124.7 40.7 %collective-permute-start.12 = (bf16[4096,128]{1,0:T(8,128)(2,1)S(1)}, bf16[4096,128]{1,0:T(8,128)(2,1)S(1)}, u32[]{:S(2)}, u32[]{:S(2)}) collective-permute-start(bf16[4096,128]{1,0:T(8,128)(2,1)S(1)} %slice_bitcast_fusion.w0_ref), channel_id=1, source_target_pairs={{0,1},{1,0},{2,3},{3,2},{4,5},{5,4},{6,7},{7,6},{8,9},{9,8},{10,11... | collective-permute-start | bytes 3145736 | tf_op jit(solution)/shard_map/ppermute | solution.py:357
  143.0 34.9 %collective-permute-start.14 = (bf16[4096,128]{1,0:T(8,128)(2,1)}, bf16[4096,128]{1,0:T(8,128)(2,1)}, u32[]{:S(2)}, u32[]{:S(2)}) collective-permute-start(bf16[4096,128]{1,0:T(8,128)(2,1)} %collective-permute-done.13.w2_ref), channel_id=1, source_target_pairs={{0,1},{1,0},{2,3},{3,2},{4,5},{5,4},{6,7},{7,6},{8,9},{9,8},{10,11... | collective-permute-start | bytes 3145736 | tf_op jit(solution)/shard_map/ppermute | solution.py:357
  161.8 16.1 %all-to-all-start.1 = ((bf16[16,72,128]{2,1,0:T(8,128)(2,1)}), bf16[16,72,128]{2,1,0:T(8,128)(2,1)S(1)}, u32[]{:S(2)}, u32[]{:S(2)}) async-start(bf16[16,72,128]{2,1,0:T(8,128)(2,1)} %bitcast.52), calls=%async_computation.1 | async-start | bytes 589824 | tf_op jit(solution)/shard_map/all_to_all | solution.py:460
  165.4 12.5 %copy-start.10 = (bf16[4096,128]{1,0:T(8,128)(2,1)}, bf16[4096,128]{1,0:T(8,128)(2,1)S(1)}, u32[]{:S(2)}) copy-start(bf16[4096,128]{1,0:T(8,128)(2,1)S(1)} %collective-permute-done.12.w1_ref) | copy-start | bytes 3145732
  177.9 0.7 copy-start.9

commit v3 on v2

--- a/solution.py
+++ b/solution.py
@@ -104,7 +104,7 @@
     )(source, *blocks, gains, *weights)
 
 
-def late_kernel(source_ref, b4_ref, gain_ref, w00_ref, w01_ref, w10_ref, w11_ref, square_ref, kv_ref, q_ref, lhs_ref, squares_ref, send_ref):
+def late_kernel(source_ref, b4_ref, gain_ref, w00_ref, w01_ref, w10_ref, w11_ref, square_ref, kv_ref, q_ref, lhs_ref, squares_ref, send_ref, send_q_ref):
     square = square_ref[...]
     for k in range(2):
         square = normed(b4_ref.at[k], gain_ref[source_ref[6 + k]], lhs_ref, k, square)
@@ -114,16 +114,16 @@
     squares_ref[...] = squares
     upper = squares.astype(BF16)
     lower = (squares - upper.astype(F32)).astype(BF16)
-    for i in range(4):
-        send_ref[i, HALF + 64 :, :] = lower if i == 1 else upper
+    send_q_ref[256:264] = upper
+    send_q_ref[264:272] = lower
     lhs = columns([lhs_ref[k] for k in range(2)])
     for m, (one, two) in enumerate(((w00_ref, w01_ref), (w10_ref, w11_ref))):
         rows = [jnp.concatenate([one[i], two[i]], axis=0) for i in range(3)]
         both = kv_ref[m] + dot(lhs[:HALF], columns(rows[:2]), ((1,), (0,)))
         query = q_ref[m] + dot(lhs[HALF:], rows[2], ((1,), (0,)))
+        send_q_ref[m * 128 : (m + 1) * 128] = query.astype(BF16)
         for i in range(2):
-            send_ref[2 * m + i, :HALF, :] = both[:, i * 128 : (i + 1) * 128].astype(BF16)
-            send_ref[2 * m + i, HALF : HALF + 64, :] = query[i * 64 : (i + 1) * 64].astype(BF16)
+            send_ref[2 * m + i] = both[:, i * 128 : (i + 1) * 128].astype(BF16)
 
 
 def whole_spec(*shape):
@@ -149,76 +149,111 @@
             out_specs=[
                 whole_spec(2, ROWS_IN, 256),
                 whole_spec(8, 128),
-                whole_spec(4, HALF + 72, 128),
+                whole_spec(4, HALF, 128),
+                whole_spec(272, 128),
             ],
         ),
         out_shape=[
             jax.ShapeDtypeStruct((2, ROWS_IN, 256), BF16),
             jax.ShapeDtypeStruct((8, 128), F32),
-            jax.ShapeDtypeStruct((4, HALF + 72, 128), BF16),
+            jax.ShapeDtypeStruct((4, HALF, 128), BF16),
+            jax.ShapeDtypeStruct((272, 128), BF16),
         ],
         name="project_late",
     )(source, block, gains, weights[0], weights[0], weights[1], weights[1], square, kv, query)
 
 
-def near_kernel(source_ref, early_ref, late_ref, w0_ref, w1_ref, keep_ref, keep_q_ref):
+def rate_of(squares_ref, other_ref):
+    theirs = other_ref[256:264].astype(F32) + other_ref[264:272].astype(F32)
+    return lax.rsqrt((squares_ref[...] + theirs) * (1.0 / 4096) + EPS)
+
+
+def query_kernel(source_ref, early_ref, late_ref, w0_ref, w1_ref, squares_ref, other_ref, count_ref, q_ref):
+    core = source_ref[8]
+    column = row_to_column(rate_of(squares_ref, other_ref)[4:5])
+    lhs = columns([early_ref[k] for k in range(6)] + [late_ref[k] for k in range(2)])
+    for m, ref in enumerate((w0_ref, w1_ref)):
+        near = dot(lhs, rows_of(ref, 0, source_ref, range(8)), ((1,), (0,)))
+        total = near + other_ref[m * 128 : (m + 1) * 128].astype(F32)
+        value = (total * column).astype(BF16)
+        for z in range(4):
+            q_ref[z, core ^ m, :128] = value
+            q_ref[z, m, 128:] = count_ref[z]
+
+
+def finish_queries(source, early, late, weights, squares, other, counts):
+    last = lambda i, *_: (0, HALF // 128, 0)
+    weight = pl.BlockSpec((1, 2048, 128), lambda i, *_: (2, 0, 0))
+    return pl.pallas_call(
+        query_kernel,
+        grid_spec=pltpu.PrefetchScalarGridSpec(
+            num_scalar_prefetch=1,
+            grid=(1,),
+            in_specs=[
+                pl.BlockSpec((6, 128, 256), last),
+                pl.BlockSpec((2, 128, 256), last),
+                weight,
+                weight,
+                whole_spec(8, 128),
+                whole_spec(272, 128),
+                whole_spec(4, 64, 128),
+            ],
+            out_specs=whole_spec(4, 2, 192, 128),
+        ),
+        out_shape=jax.ShapeDtypeStruct((4, 2, 192, 128), BF16),
+        name="finish_queries",
+    )(source, early, late, *weights, squares, other, counts)
+
+
+def near_kernel(source_ref, early_ref, late_ref, w0_ref, w1_ref, keep_ref):
     lhs = columns([early_ref[k] for k in range(6)] + [late_ref[k] for k in range(2)])
     for m, ref in enumerate((w0_ref, w1_ref)):
         pair = columns([rows_of(ref, i, source_ref, range(8)) for i in range(2)])
-        both = dot(lhs[:HALF], pair, ((1,), (0,)))
+        both = dot(lhs, pair, ((1,), (0,)))
         keep_ref[m, 0] = both[:, :128]
         keep_ref[m, 1] = both[:, 128:]
-        keep_q_ref[m] = dot(lhs[HALF:], rows_of(ref, 2, source_ref, range(8)), ((1,), (0,)))
 
 
 def project_near(source, early, late, weights):
-    vmem = pl.BlockSpec(memory_space=pltpu.VMEM)
     return pl.pallas_call(
         near_kernel,
-        in_specs=[pl.BlockSpec(memory_space=pltpu.SMEM)] + [vmem] * 4,
-        out_specs=[vmem] * 2,
-        out_shape=[
-            jax.ShapeDtypeStruct((2, 2, HALF, 128), F32),
-            jax.ShapeDtypeStruct((2, 128, 128), F32),
-        ],
+        grid_spec=pltpu.PrefetchScalarGridSpec(
+            num_scalar_prefetch=1,
+            grid=(1,),
+            in_specs=[
+                whole_spec(6, HALF, 256),
+                whole_spec(2, HALF, 256),
+                whole_spec(2, 2048, 128),
+                whole_spec(2, 2048, 128),
+            ],
+            out_specs=whole_spec(2, 2, HALF, 128),
+        ),
+        out_shape=jax.ShapeDtypeStruct((2, 2, HALF, 128), F32),
         name="project_near",
     )(source, early, late, *weights)
 
 
-def finish_kernel(source_ref, keep_ref, keep_q_ref, squares_ref, other_ref, count_ref, own_ref, give_ref, q_ref):
-    core = source_ref[8]
-    ours = squares_ref[...]
-    theirs = other_ref[0, HALF + 64 :, :].astype(F32) + other_ref[1, HALF + 64 :, :].astype(F32)
-    rate = lax.rsqrt((ours + theirs) * (1.0 / 4096) + EPS)
-    for m, ref in enumerate((own_ref, give_ref)):
-        head = core ^ m
-        for k in range(4):
-            rows = slice(k * 128, (k + 1) * 128)
-            column = row_to_column(rate[k : k + 1])
+def finish_kernel(keep_ref, squares_ref, other_q_ref, other_ref, own_ref, give_ref):
+    rate = rate_of(squares_ref, other_q_ref)
+    for k in range(4):
+        rows = slice(k * 128, (k + 1) * 128)
+        column = row_to_column(rate[k : k + 1])
+        for m, ref in enumerate((own_ref, give_ref)):
             for i in range(2):
                 total = keep_ref[m, i, rows] + other_ref[2 * m + i, rows, :].astype(F32)
                 ref[i, rows] = (total * column).astype(BF16)
-        column = row_to_column(rate[4:5])
-        for i in range(2):
-            rows = slice(i * 64, (i + 1) * 64)
-            total = keep_q_ref[m, rows] + other_ref[2 * m + i, HALF : HALF + 64, :].astype(F32)
-            value = (total * column[rows]).astype(BF16)
-            for z in range(4):
-                q_ref[z, head, rows] = value
-        for z in range(4):
-            q_ref[z, m, 128:] = count_ref[z]
-
-
-def finish(source, keep, keep_q, squares, other, counts):
+
+
+def finish(keep, squares, other_q, other):
     vmem = pl.BlockSpec(memory_space=pltpu.VMEM)
     half = jax.ShapeDtypeStruct((2, HALF, 128), BF16)
     return pl.pallas_call(
         finish_kernel,
-        in_specs=[pl.BlockSpec(memory_space=pltpu.SMEM)] + [vmem] * 5,
-        out_specs=[vmem] * 3,
-        out_shape=[half, half, jax.ShapeDtypeStruct((4, 2, 192, 128), BF16)],
+        in_specs=[vmem] * 4,
+        out_specs=[vmem] * 2,
+        out_shape=[half, half],
         name="finish",
-    )(source, keep, keep_q, squares, other, counts)
+    )(keep, squares, other_q, other)
 
 
 def partial(order_ref, first, queries, blocks, count_ref, expo_ref):
@@ -407,11 +442,16 @@
 
     own = half_of(table, tokens, core)
     got = swap(half_of(table, tokens, 1 - core), "c")
-    across = swap(feature_rows(projections, 1 - section), "s")
+    away = feature_rows(after(projections, got), 1 - section)
+    across = swap(away, "s")
     chunk = jnp.where(core == 0, jnp.stack([own, got]), jnp.stack([got, own]))
     first = exchange(chunk, "y", 8, 0)
     second = exchange(jnp.stack([chunk, first]), "y", 8, 1)
-    mine = feature_rows(after(projections, first), section)
+    later = after(projections, first)
+    wo = later[1, 1]
+    wo_section = swap(wo, "s")
+    wo_beside = swap(wo, "c")
+    mine = feature_rows(later, section)
     beside = swap(mine, "c")
 
     gains = lax.dynamic_slice_in_dim(norm_gains, section * 2048, 2048, axis=1)
@@ -435,24 +475,22 @@
 
     far = (across, diagonal)
     early, square, kv, query = project_early(source, (chunk, first, second, third), gains, far)
-    late, squares, send = project_late(source, fourth, gains, far, square, kv, query)
+    late, squares, send, send_q = project_late(source, fourth, gains, far, square, kv, query)
+    other_q = swap(send_q, "s")
     other = swap(send, "s")
-    keep, keep_q = project_near(source, early, late, (mine, beside))
-    near, give, queries = finish(source, keep, keep_q, squares, other, counts)
+    beside = (mine, beside)
+    queries = finish_queries(source, early, late, beside, squares, other_q, counts)
     queries = queries.reshape(8, 192, 128)
     queries = lax.all_to_all(queries, ("zh", "c"), 0, 0)
+    keep = project_near(source, early, late, beside)
+    near, give = finish(keep, squares, other_q, other)
+    wo_diagonal = swap(wo_section, "c")
     near = jnp.stack([near, swap(give, "c")])
     following = exchange(near, "x", 4, 0)
-    following = after(following, queries)
     beyond = exchange(jnp.stack([near, following]), "x", 4, 1)
     queries = queries.reshape(4, 2, 192, 128)
     counts = queries[:, :, 128:].reshape(4, 2, 2, 8, HALF).transpose(0, 3, 1, 2, 4)
     counts = counts.reshape(4, 8, 4, HALF)
-
-    wo = after(projections[1, 1], first)
-    wo_section = swap(after(wo, queries), "s")
-    wo_beside = swap(wo, "c")
-    wo_diagonal = swap(wo_section, "c")
 
     part, total = attend_near(order, queries, near, following, counts)
     parts = attend_far(order, queries, beyond, counts, part, total)

time: 210 us -> 213 us (1.014)
  Pallas kernels: 35 us -> 37.8 us
  waiting for transfers between devices: 65.5 us -> 67.7 us
    all_to_all x1, waiting for transfers between devices: 6 us -> 12.9 us  [step(): queries = lax.all_to_all(queries, ('zh', 'c'), 0, 0)]
    ppermute x9 -> x10, waiting for transfers between devices: 20.2 us -> 13.3 us  [swap(): return lax.ppermute(value, axis, [(0, 1), (1, 0)])]
    all_to_all x1, starting transfers between devices: 5.84 us -> 9.86 us  [step(): queries = lax.all_to_all(queries, ('zh', 'c'), 0, 0)]
    ppermute x6, starting transfers between devices: 15.3 us -> 11.6 us  [exchange(): return lax.ppermute(value, (axis, 'c'), pairs(size, turn))]
    pallas_call x2 -> x3, Pallas kernels: 7.9 us -> 10.7 us  [the longest x1 5.07 us: project_near(): pl.pallas_call(near_kernel, grid_spec=pltpu.PrefetchScalarGridSpec(num_sc...]
    ppermute x9 -> x10, starting transfers between devices: 37 us -> 34.3 us  [swap(): return lax.ppermute(value, axis, [(0, 1), (1, 0)])]
    ppermute x6, waiting for transfers between devices: 26.8 us -> 29 us  [exchange(): return lax.ppermute(value, (axis, 'c'), pairs(size, turn))]
  transfers between devices with their start and end apart: 17 -> 18, of which waited for: 9 -> 11; matrix products, arithmetic and copies ran while one was open for 8% -> 7% of each run, Pallas kernels for 13% -> 14%
where the time goes in v3:
time: 213 us; the launch traced here: 212 us
  waiting for transfers between devices  67.7 us (32%)
  starting transfers between devices  59.8 us (28%)
  Pallas kernels  37.8 us (18%)
  blocking collectives  22.3 us (10%)
  local copies, waits for them, and re-layouts  15.5 us (7%)
  other arithmetic  7.29 us (3%)
    ppermute x10, starting transfers between devices, swap(): return lax.ppermute(value, axis, [(0, 1), (1, 0)])  34.3 us
    ppermute x6, waiting for transfers between devices, exchange(): return lax.ppermute(value, (axis, 'c'), pairs(size, turn))  29 us
    all_to_all x1, blocking collectives, step(): out = lax.all_to_all(out, ('s', 'y', 'c'), 0, 0)  22.3 us
    ppermute x10, waiting for transfers between devices, swap(): return lax.ppermute(value, axis, [(0, 1), (1, 0)])  13.3 us
    all_to_all x1, waiting for transfers between devices, step(): queries = lax.all_to_all(queries, ('zh', 'c'), 0, 0)  12.9 us
    all_to_all x1, waiting for transfers between devices, step(): parts = lax.all_to_all(parts, ('s', 'zh', 'c'), 0, 0)  12.5 us
    ppermute x6, starting transfers between devices, exchange(): return lax.ppermute(value, (axis, 'c'), pairs(size, turn))  11.6 us
    all_to_all x1, starting transfers between devices, step(): queries = lax.all_to_all(queries, ('zh', 'c'), 0, 0)  9.86 us
  transfers between devices with their start and end apart: 18, of which 11 were waited for; matrix products, arithmetic and copies ran while one was open for 7% of the time, Pallas kernels for 14%

profile of v3, /device:TPU:1, one launch (start us, length us, event | category | flops | bytes accessed | tf_op | source)
XLA Modules:
  0.0 211.6 jit_solution(4983337576373055481)
XLA Ops:
  0.0 0.8 constant_dynamic-slice_fusion.3
  0.8 1.0 constant_dynamic-slice_fusion.4
  1.8 8.7 %collective-permute-start = (bf16[640,128]{1,0:T(8,128)(2,1)S(1)}, bf16[640,128]{1,0:T(8,128)(2,1)S(1)}, u32[]{:S(2)}, u32[]{:S(2)}) collective-permute-start(bf16[640,128]{1,0:T(8,128)(2,1)S(1)} %pad_maximum_fusion.6), channel_id=1, source_target_pairs={{0,1},{1,0},{2,3},{3,2},{4,5},{5,4},{6,7},{7,6},{8,9},{9,8},{10,11... | collective-permute-start | bytes 491528 | tf_op jit(solution)/shard_map/ppermute | solution.py:392
  10.6 0.8 convert_reduce_fusion
  11.3 0.6 constant_dynamic-slice_fusion
  12.1 1.1 dynamic-slice_bitcast_fusion.3
  13.1 1.3 dynamic-slice_bitcast_fusion.1
  14.5 1.9 collective-permute-start.1
  16.4 1.3 pad_maximum_fusion
  17.8 2.0 collective-permute-start.4
  19.9 3.7 %collective-permute-done.1.b1_ref = bf16[2,640,128]{2,1,0:T(8,128)(2,1)S(1)} collective-permute-done((bf16[2,640,128]{2,1,0:T(8,128)(2,1)S(1)}, bf16[2,640,128]{2,1,0:T(8,128)(2,1)S(1)}, u32[]{:S(2)}, u32[]{:S(2)}) %collective-permute-start.1) | collective-permute-done | bytes 327712 | tf_op jit(solution)/shard_map/ppermute | solution.py:425
  23.6 2.1 collective-permute-start.2
  25.7 0.5 fusion.1
  26.2 0.3 convolution_convert_fusion
  26.5 0.3 copy.19
  26.8 0.5 reshape.110
  27.4 8.1 %collective-permute-done.2.b2_ref = bf16[2,2,640,128]{3,2,1,0:T(8,128)(2,1)} collective-permute-done((bf16[2,2,640,128]{3,2,1,0:T(8,128)(2,1)S(1)}, bf16[2,2,640,128]{3,2,1,0:T(8,128)(2,1)}, u32[]{:S(2)}, u32[]{:S(2)}) %collective-permute-start.2) | collective-permute-done | bytes 655392 | tf_op jit(solution)/shard_map/ppermute | solution.py:425
  35.5 1.9 collective-permute-start.3
  37.5 0.7 reshape.111.count_ref
  38.3 0.7 add.128.order_ref
  38.9 0.6 pad_add_fusion.source_ref
  39.5 8.8 %collective-permute-done.3.b3_ref = bf16[2,2,640,128]{3,2,1,0:T(8,128)(2,1)} collective-permute-done((bf16[2,2,640,128]{3,2,1,0:T(8,128)(2,1)}, bf16[2,2,640,128]{3,2,1,0:T(8,128)(2,1)}, u32[]{:S(2)}, u32[]{:S(2)}) %collective-permute-start.3) | collective-permute-done | bytes 655392 | tf_op jit(solution)/shard_map/ppermute | solution.py:425
  48.3 7.6 %collective-permute-done.4.w0_ref.w00_ref.w01_ref = bf16[3,2048,128]{2,1,0:T(8,128)(2,1)S(1)} collective-permute-done((bf16[3,2048,128]{2,1,0:T(8,128)(2,1)}, bf16[3,2048,128]{2,1,0:T(8,128)(2,1)S(1)}, u32[]{:S(2)}, u32[]{:S(2)}) %collective-permute-start.4) | collective-permute-done | bytes 1572896 | tf_op jit(solution)/shard_map/ppermute | solution.py:392
  55.9 2.8 %collective-permute-start.5 = (bf16[3,2048,128]{2,1,0:T(8,128)(2,1)S(1)}, bf16[3,2048,128]{2,1,0:T(8,128)(2,1)S(1)}, u32[]{:S(2)}, u32[]{:S(2)}) collective-permute-start(bf16[3,2048,128]{2,1,0:T(8,128)(2,1)S(1)} %collective-permute-done.4.w0_ref.w00_ref.w01_ref), channel_id=1, source_target_pairs={{0,1},{1,0},{2,3},{3,2},{4,5},{5,4},{6,7},{7,6},{8,9},{9,8},{10,11... | collective-permute-start | bytes 4718600 | tf_op jit(solution)/shard_map/ppermute | solution.py:392
  58.7 1.1 dynamic-slice_bitcast_fusion.2
  59.8 1.3 dynamic-slice_bitcast_fusion
  61.1 1.3 pad_maximum_fusion.1.w0_ref
  62.4 1.9 collective-permute-start.7
  64.3 1.9 collective-permute-start.6
  66.3 1.2 copy-done.2
  67.5 5.3 %project_early.1 = (bf16[6,640,256]{2,1,0:T(8,128)(2,1)}, f32[640,128]{1,0:T(8,128)}, f32[2,512,256]{2,1,0:T(8,128)}, f32[2,128,128]{2,1,0:T(8,128)}) custom-call(s32[9]{0:T(128)} %pad_add_fusion.source_ref, bf16[2,640,128]{2,1,0:T(8,128)(2,1)} %copy-done.8, bf16[2,640,128]{2,1,0:T(8,128)(2,1)} %copy-done.7, ...), custom_call_target="tpu_custom_call" | custom-call | tf_op jit(solution)/shard_map/project_early/pallas_call | solution.py:93
  72.8 3.5 %collective-permute-done.6.b4_ref = bf16[2,2,640,128]{3,2,1,0:T(8,128)(2,1)} collective-permute-done((bf16[2,2,640,128]{3,2,1,0:T(8,128)(2,1)}, bf16[2,2,640,128]{3,2,1,0:T(8,128)(2,1)}, u32[]{:S(2)}, u32[]{:S(2)}) %collective-permute-start.6) | collective-permute-done | bytes 655392 | tf_op jit(solution)/shard_map/ppermute | solution.py:425
  76.3 3.8 %project_late.1 = (bf16[2,640,256]{2,1,0:T(8,128)(2,1)}, f32[8,128]{1,0:T(8,128)}, bf16[4,512,128]{2,1,0:T(8,128)(2,1)}, bf16[272,128]{1,0:T(8,128)(2,1)}) custom-call(s32[9]{0:T(128)} %pad_add_fusion.source_ref, bf16[2,2,640,128]{3,2,1,0:T(8,128)(2,1)} %collective-permute-done.6.b4_ref, f32[8,2,2,128]{3,2,1,0:T(2,128)} %bitcast.61, ...), custom_call_target="tpu_custom_call" | custom-call | tf_op jit(solution)/shard_map/project_late/pallas_call | solution.py:135
  80.0 1.9 collective-permute-start.9
  82.0 3.4 %collective-permute-start.8 = (bf16[272,128]{1,0:T(8,128)(2,1)}, bf16[272,128]{1,0:T(8,128)(2,1)S(1)}, u32[]{:S(2)}, u32[]{:S(2)}) collective-permute-start(bf16[272,128]{1,0:T(8,128)(2,1)} %get-tuple-element.42), channel_id=1, source_target_pairs={{0,256},{256,0},{1,257},{257,1},{2,258},{258,2},{3,259},{259,3},{4... | collective-permute-start | bytes 208904 | tf_op jit(solution)/shard_map/ppermute | solution.py:392
  85.3 5.1 %project_near.1.keep_ref = f32[2,2,512,128]{3,2,1,0:T(8,128)} custom-call(s32[9]{0:T(128)} %pad_add_fusion.source_ref, bf16[6,640,256]{2,1,0:T(8,128)(2,1)} %get-tuple-element.35.early_ref, bf16[2,640,256]{2,1,0:T(8,128)(2,1)} %get-tuple-element.39.late_ref, bf16[3,2048,128]{2,1,0:T(8,128)(2,1)} %pad_maximum_fusion.1.w0_ref, ...), custom_call_target="tpu_custom_call" | custom-call | tf_op jit(solution)/shard_map/project_near/pallas_call | solution.py:218
  90.4 4.1 %collective-permute-done.8.other_ref.other_q_ref = bf16[272,128]{1,0:T(8,128)(2,1)S(1)} collective-permute-done((bf16[272,128]{1,0:T(8,128)(2,1)}, bf16[272,128]{1,0:T(8,128)(2,1)S(1)}, u32[]{:S(2)}, u32[]{:S(2)}) %collective-permute-start.8) | collective-permute-done | bytes 69664 | tf_op jit(solution)/shard_map/ppermute | solution.py:392
  94.6 0.6 copy-done.12
  95.2 0.2 copy-done.11
  95.4 2.3 %finish.1 = (bf16[2,512,128]{2,1,0:T(8,128)(2,1)}, bf16[2,512,128]{2,1,0:T(8,128)(2,1)}) custom-call(f32[2,2,512,128]{3,2,1,0:T(8,128)} %project_near.1.keep_ref, f32[8,128]{1,0:T(8,128)} %get-tuple-element.41.squares_ref, bf16[272,128]{1,0:T(8,128)(2,1)} %copy-done.12, bf16[4,512,128]{2,1,0:T(8,128)(2,1)} %copy-done.11), custom_call_target="tpu_custom_call" | custom-call | tf_op jit(solution)/shard_map/finish/pallas_call | solution.py:250
  97.8 5.3 %collective-permute-start.10 = (bf16[2,512,128]{2,1,0:T(8,128)(2,1)}, bf16[2,512,128]{2,1,0:T(8,128)(2,1)S(1)}, u32[]{:S(2)}, u32[]{:S(2)}) collective-permute-start(bf16[2,512,128]{2,1,0:T(8,128)(2,1)} %get-tuple-element.46), channel_id=1, source_target_pairs={{0,1},{1,0},{2,3},{3,2},{4,5},{5,4},{6,7},{7,6},{8,9},{9,8},{10,11... | collective-permute-start | bytes 786440 | tf_op jit(solution)/shard_map/ppermute | solution.py:392
  103.1 1.4 collective-permute-done.10
  104.4 1.0 fusion.16
  105.5 1.9 collective-permute-start.11
  107.4 1.3 slice_bitcast_fusion.w0_ref
  108.7 3.0 %collective-permute-start.14 = (bf16[4096,128]{1,0:T(8,128)(2,1)S(1)}, bf16[4096,128]{1,0:T(8,128)(2,1)}, u32[]{:S(2)}, u32[]{:S(2)}) collective-permute-start(bf16[4096,128]{1,0:T(8,128)(2,1)S(1)} %slice_bitcast_fusion.w0_ref), channel_id=1, source_target_pairs={{0,256},{256,0},{1,257},{257,1},{2,258},{258,2},{3,259},{259,3},{4... | collective-permute-start | bytes 3145736 | tf_op jit(solution)/shard_map/ppermute | solution.py:392
  111.7 4.9 %collective-permute-done.11.next_ref = bf16[2,2,512,128]{3,2,1,0:T(8,128)(2,1)S(1)} collective-permute-done((bf16[2,2,512,128]{3,2,1,0:T(8,128)(2,1)S(1)}, bf16[2,2,512,128]{3,2,1,0:T(8,128)(2,1)S(1)}, u32[]{:S(2)}, u32[]{:S(2)}) %collective-permute-start.11) | collective-permute-done | bytes 524320 | tf_op jit(solution)/shard_map/ppermute | solution.py:425
  116.6 1.3 pad_maximum_fusion.2
  117.9 1.9 collective-permute-start.12
  119.8 3.3 %finish_queries.1 = bf16[4,2,192,128]{3,2,1,0:T(8,128)(2,1)} custom-call(s32[9]{0:T(128)} %pad_add_fusion.source_ref, bf16[6,640,256]{2,1,0:T(8,128)(2,1)} %get-tuple-element.35.early_ref, bf16[2,640,256]{2,1,0:T(8,128)(2,1)} %get-tuple-element.39.late_ref, bf16[3,2048,128]{2,1,0:T(8,128)(2,1)} %pad_maximum_fusion.1.w0_ref, ...), custom_call_target="tpu_custom_call" | custom-call | tf_op jit(solution)/shard_map/finish_queries/pallas_call | solution.py:187
  123.1 9.9 %all-to-all-start = ((bf16[8,192,128]{2,1,0:T(8,128)(2,1)}), bf16[8,192,128]{2,1,0:T(8,128)(2,1)S(1)}, u32[]{:S(2)}, u32[]{:S(2)}) async-start(bf16[8,192,128]{2,1,0:T(8,128)(2,1)} %bitcast.51), calls=%async_computation | async-start | bytes 786432 | tf_op jit(solution)/shard_map/all_to_all | solution.py:484
  132.9 1.9 collective-permute-start.13
  135.0 3.3 %collective-permute-start.15 = (bf16[4096,128]{1,0:T(8,128)(2,1)}, bf16[4096,128]{1,0:T(8,128)(2,1)}, u32[]{:S(2)}, u32[]{:S(2)}) collective-permute-start(bf16[4096,128]{1,0:T(8,128)(2,1)} %collective-permute-done.14.w2_ref), channel_id=1, source_target_pairs={{0,1},{1,0},{2,3},{3,2},{4,5},{5,4},{6,7},{7,6},{8,9},{9,8},{10,11... | collective-permute-start | bytes 3145736 | tf_op jit(solution)/shard_map/ppermute | solution.py:392
  138.4 12.9 %all-to-all-done = bf16[8,192,128]{2,1,0:T(8,128)(2,1)S(1)} async-done(((bf16[8,192,128]{2,1,0:T(8,128)(2,1)}), bf16[8,192,128]{2,1,0:T(8,128)(2,1)S(1)}, u32[]{:S(2)}, u32[]{:S(2)}) %all-to-all-start) | async-done | bytes 393248 | tf_op jit(solution)/shard_map/all_to_all | solution.py:484
  151.5 0.7 reshape.116.count_ref
  152.3 6.3 %attend_near.1 = (f32[1024,128]{1,0:T(8,128)}, f32[1024,128]{1,0:T(8,128)}) custom-call(s32[8]{0:T(128)} %add.128.order_ref, bf16[4,2,192,128]{3,2,1,0:T(8,128)(2,1)} %bitcast.47, bf16[2,2,512,128]{3,2,1,0:T(8,128)(2,1)} %copy-done.5, bf16[2,2,512,128]{3,2,1,0:T(8,128)(2,1)} %copy-done.6, bf16[4,8,4,512]{3,2,1,0:T(4,128)(2,1)} %reshape.116.count_ref), custom_call_target="tpu_custom_call" | custom-call | tf_op jit(solution)/shard_map/attend_near/pallas_call | solution.py:307
  158.6 1.0 copy-done.10
  159.6 6.6 %attend_far.1 = bf16[2,4,2,72,128]{4,3,2,1,0:T(8,128)(2,1)} custom-call(s32[8]{0:T(128)} %add.128.order_ref, bf16[4,2,192,128]{3,2,1,0:T(8,128)(2,1)} %bitcast.48, bf16[2,2,2,512,128]{4,3,2,1,0:T(8,128)(2,1)} %copy-done.10, bf16[4,8,4,512]{3,2,1,0:T(4,128)(2,1)} %reshape.116.count_ref, f32[1024,128]{1,0:T(8,128)} %get-tuple-element.47.part_ref, ...), custom_call_target="tpu_custom_call" | custom-call | tf_op jit(solution)/shard_map/attend_far/pallas_call | solution.py:322
  166.2 4.1 %all-to-all-start.1 = ((bf16[16,72,128]{2,1,0:T(8,128)(2,1)}), bf16[16,72,128]{2,1,0:T(8,128)(2,1)S(1)}, u32[]{:S(2)}, u32[]{:S(2)}) async-start(bf16[16,72,128]{2,1,0:T(8,128)(2,1)} %bitcast.53), calls=%async_computation.1 | async-start | bytes 589824 | tf_op jit(solution)/shard_map/all_to_all | solution.py:498
  170.3 12.5 %all-to-all-done.1 = bf16[16,72,128]{2,1,0:T(8,128)(2,1)S(1)} async-done(((bf16[16,72,128]{2,1,0:T(8,128)(2,1)}), bf16[16,72,128]{2,1,0:T(8,128)(2,1)S(1)}, u32[]{:S(2)}, u32[]{:S(2)}) %all-to-all-start.1) | async-done | bytes 294944 | tf_op jit(solution)/shard_map/all_to_all | solution.py:498
  182.8 0.7 copy-done.9
  183.5 5.2 %mix.1 = bf16[32,64,128]{2,1,0:T(8,128)(2,1)} custom-call(s32[1]{0:T(128)} %bitcast.place_ref, bf16[2,4,2,72,128]{4,3,2,1,0:T(8,128)(2,1)} %bitcast.54, bf16[4096,128]{1,0:T(8,128)(2,1)} %copy-done.4, bf16[4096,128]{1,0:T(8,128)(2,1)} %collective-permute-done.13.w1_ref, bf16[4096,128]{1,0:T(8,128)(2,1)} %collective-permute-done.14.w2_ref, ...), custom_call_target="tpu_custom_call" | custom-call | tf_op jit(solution)/shard_map/mix/pallas_call | solution.py:371
  188.7 22.3 %all_to_all.15 = bf16[32,64,128]{2,1,0:T(8,128)(2,1)S(1)} all-to-all(bf16[32,64,128]{2,1,0:T(8,128)(2,1)} %mix.1), channel_id=1, replica_groups=mesh['s'=2,'zh'=4,'x'=4,'y'=8,'c'=2] {'s','y','c'}, dimensions={0} | all-to-all | bytes 1048576 | tf_op jit(solution)/shard_map/all_to_all | solution.py:502
  210.9 0.7 reduce_sum.22
  (48 shorter events, 0.9 us)
Async XLA Ops:
  0.0 11.3 %copy-start = (f32[2,4096]{1,0:T(2,128)S(1)}, f32[2,4096]{1,0:T(2,128)}, u32[]{:S(2)}) copy-start(f32[2,4096]{1,0:T(2,128)} %param.11) | copy-start | bytes 98308
  1.8 10.2 %collective-permute-start = (bf16[640,128]{1,0:T(8,128)(2,1)S(1)}, bf16[640,128]{1,0:T(8,128)(2,1)S(1)}, u32[]{:S(2)}, u32[]{:S(2)}) collective-permute-start(bf16[640,128]{1,0:T(8,128)(2,1)S(1)} %pad_maximum_fusion.6), channel_id=1, source_target_pairs={{0,1},{1,0},{2,3},{3,2},{4,5},{5,4},{6,7},{7,6},{8,9},{9,8},{10,11... | collective-permute-start | bytes 491528 | tf_op jit(solution)/shard_map/ppermute | solution.py:392
  14.5 3.3 %copy-start.8 = (bf16[2,640,128]{2,1,0:T(8,128)(2,1)}, bf16[2,640,128]{2,1,0:T(8,128)(2,1)S(1)}, u32[]{:S(2)}) copy-start(bf16[2,640,128]{2,1,0:T(8,128)(2,1)S(1)} %maximum_select_fusion.1.b0_ref) | copy-start | bytes 983044
  14.5 9.0 %collective-permute-start.1 = (bf16[2,640,128]{2,1,0:T(8,128)(2,1)S(1)}, bf16[2,640,128]{2,1,0:T(8,128)(2,1)S(1)}, u32[]{:S(2)}, u32[]{:S(2)}) collective-permute-start(bf16[2,640,128]{2,1,0:T(8,128)(2,1)S(1)} %maximum_select_fusion.1.b0_ref), channel_id=1, source_target_pairs={{0,2},{1,15},{2,0},{3,5},{4,6},{5,3},{6,4},{7,9},{8,10},{9,7},{10,... | collective-permute-start | bytes 983048 | tf_op jit(solution)/shard_map/ppermute | solution.py:425
  17.8 7.9 %copy-start.13 = (s32[8,128]{1,0:T(8,128)S(1)}, s32[8,128]{1,0:T(8,128)}, u32[]{:S(2)}) copy-start(s32[8,128]{1,0:T(8,128)} %param.8) | copy-start | bytes 12292
  17.8 38.2 %collective-permute-start.4 = (bf16[3,2048,128]{2,1,0:T(8,128)(2,1)}, bf16[3,2048,128]{2,1,0:T(8,128)(2,1)S(1)}, u32[]{:S(2)}, u32[]{:S(2)}) collective-permute-start(bf16[3,2048,128]{2,1,0:T(8,128)(2,1)} %pad_maximum_fusion), channel_id=1, source_target_pairs={{0,256},{256,0},{1,257},{257,1},{2,258},{258,2},{3,259},{259,3},{4... | collective-permute-start | bytes 4718600 | tf_op jit(solution)/shard_map/ppermute | solution.py:392
  23.5 3.3 %copy-start.7 = (bf16[2,640,128]{2,1,0:T(8,128)(2,1)}, bf16[2,640,128]{2,1,0:T(8,128)(2,1)S(1)}, u32[]{:S(2)}) copy-start(bf16[2,640,128]{2,1,0:T(8,128)(2,1)S(1)} %collective-permute-done.1.b1_ref) | copy-start | bytes 983044
  23.6 13.8 %copy-start.14 = (s32[8]{0:T(128)S(1)}, s32[8]{0:T(128)}, u32[]{:S(2)}) copy-start(s32[8]{0:T(128)} %constant.129.clone) | copy-start | bytes 100
  23.6 11.9 %collective-permute-start.2 = (bf16[2,2,640,128]{3,2,1,0:T(8,128)(2,1)S(1)}, bf16[2,2,640,128]{3,2,1,0:T(8,128)(2,1)}, u32[]{:S(2)}, u32[]{:S(2)}) collective-permute-start(bf16[2,2,640,128]{3,2,1,0:T(8,128)(2,1)S(1)} %pad_maximum_fusion.3), channel_id=1, source_target_pairs={{0,14},{1,3},{2,4},{3,1},{4,2},{5,7},{6,8},{7,5},{8,6},{9,11},{10,... | collective-permute-start | bytes 1966088 | tf_op jit(solution)/shard_map/ppermute | solution.py:425
  35.5 12.8 %collective-permute-start.3 = (bf16[2,2,640,128]{3,2,1,0:T(8,128)(2,1)}, bf16[2,2,640,128]{3,2,1,0:T(8,128)(2,1)}, u32[]{:S(2)}, u32[]{:S(2)}) collective-permute-start(bf16[2,2,640,128]{3,2,1,0:T(8,128)(2,1)} %collective-permute-done.2.b2_ref), channel_id=1, source_target_pairs={{0,2},{1,15},{2,0},{3,5},{4,6},{5,3},{6,4},{7,9},{8,10},{9,7},{10,... | collective-permute-start | bytes 1966088 | tf_op jit(solution)/shard_map/ppermute | solution.py:425
  55.9 5.2 %copy-start.1 = (bf16[3,2048,128]{2,1,0:T(8,128)(2,1)}, bf16[3,2048,128]{2,1,0:T(8,128)(2,1)S(1)}, u32[]{:S(2)}) copy-start(bf16[3,2048,128]{2,1,0:T(8,128)(2,1)S(1)} %collective-permute-done.4.w0_ref.w00_ref.w01_ref) | copy-start | bytes 4718596
  55.9 10.3 %collective-permute-start.5 = (bf16[3,2048,128]{2,1,0:T(8,128)(2,1)S(1)}, bf16[3,2048,128]{2,1,0:T(8,128)(2,1)S(1)}, u32[]{:S(2)}, u32[]{:S(2)}) collective-permute-start(bf16[3,2048,128]{2,1,0:T(8,128)(2,1)S(1)} %collective-permute-done.4.w0_ref.w00_ref.w01_ref), channel_id=1, source_target_pairs={{0,1},{1,0},{2,3},{3,2},{4,5},{5,4},{6,7},{7,6},{8,9},{9,8},{10,11... | collective-permute-start | bytes 4718600 | tf_op jit(solution)/shard_map/ppermute | solution.py:392
  62.4 22.9 %collective-permute-start.7 = (bf16[3,2048,128]{2,1,0:T(8,128)(2,1)}, bf16[3,2048,128]{2,1,0:T(8,128)(2,1)}, u32[]{:S(2)}, u32[]{:S(2)}) collective-permute-start(bf16[3,2048,128]{2,1,0:T(8,128)(2,1)} %pad_maximum_fusion.1.w0_ref), channel_id=1, source_target_pairs={{0,1},{1,0},{2,3},{3,2},{4,5},{5,4},{6,7},{7,6},{8,9},{9,8},{10,11... | collective-permute-start | bytes 4718600 | tf_op jit(solution)/shard_map/ppermute | solution.py:392
  64.3 11.9 %collective-permute-start.6 = (bf16[2,2,640,128]{3,2,1,0:T(8,128)(2,1)}, bf16[2,2,640,128]{3,2,1,0:T(8,128)(2,1)}, u32[]{:S(2)}, u32[]{:S(2)}) collective-permute-start(bf16[2,2,640,128]{3,2,1,0:T(8,128)(2,1)} %collective-permute-done.3.b3_ref), channel_id=1, source_target_pairs={{0,14},{1,3},{2,4},{3,1},{4,2},{5,7},{6,8},{7,5},{8,6},{9,11},{10,... | collective-permute-start | bytes 1966088 | tf_op jit(solution)/shard_map/ppermute | solution.py:425
  66.2 1.2 copy-start.2
  80.0 14.5 %collective-permute-start.9 = (bf16[4,512,128]{2,1,0:T(8,128)(2,1)}, bf16[4,512,128]{2,1,0:T(8,128)(2,1)S(1)}, u32[]{:S(2)}, u32[]{:S(2)}) collective-permute-start(bf16[4,512,128]{2,1,0:T(8,128)(2,1)} %get-tuple-element.44), channel_id=1, source_target_pairs={{0,256},{256,0},{1,257},{257,1},{2,258},{258,2},{3,259},{259,3},{4... | collective-permute-start | bytes 1572872 | tf_op jit(solution)/shard_map/ppermute | solution.py:392
  82.0 12.6 %collective-permute-start.8 = (bf16[272,128]{1,0:T(8,128)(2,1)}, bf16[272,128]{1,0:T(8,128)(2,1)S(1)}, u32[]{:S(2)}, u32[]{:S(2)}) collective-permute-start(bf16[272,128]{1,0:T(8,128)(2,1)} %get-tuple-element.42), channel_id=1, source_target_pairs={{0,256},{256,0},{1,257},{257,1},{2,258},{258,2},{3,259},{259,3},{4... | collective-permute-start | bytes 208904 | tf_op jit(solution)/shard_map/ppermute | solution.py:392
  94.5 0.6 copy-start.12
  94.6 0.9 copy-start.11
  97.8 6.7 %collective-permute-start.10 = (bf16[2,512,128]{2,1,0:T(8,128)(2,1)}, bf16[2,512,128]{2,1,0:T(8,128)(2,1)S(1)}, u32[]{:S(2)}, u32[]{:S(2)}) collective-permute-start(bf16[2,512,128]{2,1,0:T(8,128)(2,1)} %get-tuple-element.46), channel_id=1, source_target_pairs={{0,1},{1,0},{2,3},{3,2},{4,5},{5,4},{6,7},{7,6},{8,9},{9,8},{10,11... | collective-permute-start | bytes 786440 | tf_op jit(solution)/shard_map/ppermute | solution.py:392
  105.5 12.4 %copy-start.5 = (bf16[2,2,512,128]{3,2,1,0:T(8,128)(2,1)}, bf16[2,2,512,128]{3,2,1,0:T(8,128)(2,1)S(1)}, u32[]{:S(2)}) copy-start(bf16[2,2,512,128]{3,2,1,0:T(8,128)(2,1)S(1)} %get-tuple-element.50.near_ref) | copy-start | bytes 1572868
  105.5 11.1 %collective-permute-start.11 = (bf16[2,2,512,128]{3,2,1,0:T(8,128)(2,1)S(1)}, bf16[2,2,512,128]{3,2,1,0:T(8,128)(2,1)S(1)}, u32[]{:S(2)}, u32[]{:S(2)}) collective-permute-start(bf16[2,2,512,128]{3,2,1,0:T(8,128)(2,1)S(1)} %get-tuple-element.50.near_ref), channel_id=1, source_target_pairs={{0,16},{1,49},{16,0},{17,33},{32,48},{33,17},{48,32},{49,1},{2,18}... | collective-permute-start | bytes 1572872 | tf_op jit(solution)/shard_map/ppermute | solution.py:425
  108.7 24.2 %copy-start.4 = (bf16[4096,128]{1,0:T(8,128)(2,1)}, bf16[4096,128]{1,0:T(8,128)(2,1)S(1)}, u32[]{:S(2)}) copy-start(bf16[4096,128]{1,0:T(8,128)(2,1)S(1)} %slice_bitcast_fusion.w0_ref) | copy-start | bytes 3145732
  108.7 26.3 %collective-permute-start.14 = (bf16[4096,128]{1,0:T(8,128)(2,1)S(1)}, bf16[4096,128]{1,0:T(8,128)(2,1)}, u32[]{:S(2)}, u32[]{:S(2)}) collective-permute-start(bf16[4096,128]{1,0:T(8,128)(2,1)S(1)} %slice_bitcast_fusion.w0_ref), channel_id=1, source_target_pairs={{0,256},{256,0},{1,257},{257,1},{2,258},{258,2},{3,259},{259,3},{4... | collective-permute-start | bytes 3145736 | tf_op jit(solution)/shard_map/ppermute | solution.py:392
  116.6 6.5 %copy-start.6 = (bf16[2,2,512,128]{3,2,1,0:T(8,128)(2,1)}, bf16[2,2,512,128]{3,2,1,0:T(8,128)(2,1)S(1)}, u32[]{:S(2)}) copy-start(bf16[2,2,512,128]{3,2,1,0:T(8,128)(2,1)S(1)} %collective-permute-done.11.next_ref) | copy-start | bytes 1572868
  117.9 40.7 %collective-permute-start.12 = (bf16[2,2,2,512,128]{4,3,2,1,0:T(8,128)(2,1)}, bf16[2,2,2,512,128]{4,3,2,1,0:T(8,128)(2,1)S(1)}, u32[]{:S(2)}, u32[]{:S(2)}) collective-permute-start(bf16[2,2,2,512,128]{4,3,2,1,0:T(8,128)(2,1)} %pad_maximum_fusion.2), channel_id=1, source_target_pairs={{0,48},{1,17},{16,32},{17,1},{32,16},{33,49},{48,0},{49,33},{2,50}... | collective-permute-start | bytes 3145736 | tf_op jit(solution)/shard_map/ppermute | solution.py:425
  123.1 28.2 %all-to-all-start = ((bf16[8,192,128]{2,1,0:T(8,128)(2,1)}), bf16[8,192,128]{2,1,0:T(8,128)(2,1)S(1)}, u32[]{:S(2)}, u32[]{:S(2)}) async-start(bf16[8,192,128]{2,1,0:T(8,128)(2,1)} %bitcast.51), calls=%async_computation | async-start | bytes 786432 | tf_op jit(solution)/shard_map/all_to_all | solution.py:484
  132.9 37.3 %collective-permute-start.13 = (bf16[4096,128]{1,0:T(8,128)(2,1)S(1)}, bf16[4096,128]{1,0:T(8,128)(2,1)}, u32[]{:S(2)}, u32[]{:S(2)}) collective-permute-start(bf16[4096,128]{1,0:T(8,128)(2,1)S(1)} %slice_bitcast_fusion.w0_ref), channel_id=1, source_target_pairs={{0,1},{1,0},{2,3},{3,2},{4,5},{5,4},{6,7},{7,6},{8,9},{9,8},{10,11... | collective-permute-start | bytes 3145736 | tf_op jit(solution)/shard_map/ppermute | solution.py:392
  135.0 35.2 %collective-permute-start.15 = (bf16[4096,128]{1,0:T(8,128)(2,1)}, bf16[4096,128]{1,0:T(8,128)(2,1)}, u32[]{:S(2)}, u32[]{:S(2)}) collective-permute-start(bf16[4096,128]{1,0:T(8,128)(2,1)} %collective-permute-done.14.w2_ref), channel_id=1, source_target_pairs={{0,1},{1,0},{2,3},{3,2},{4,5},{5,4},{6,7},{7,6},{8,9},{9,8},{10,11... | collective-permute-start | bytes 3145736 | tf_op jit(solution)/shard_map/ppermute | solution.py:392
  151.3 1.0 copy-start.3
  158.6 1.0 copy-start.10
  166.2 16.6 %all-to-all-start.1 = ((bf16[16,72,128]{2,1,0:T(8,128)(2,1)}), bf16[16,72,128]{2,1,0:T(8,128)(2,1)S(1)}, u32[]{:S(2)}, u32[]{:S(2)}) async-start(bf16[16,72,128]{2,1,0:T(8,128)(2,1)} %bitcast.53), calls=%async_computation.1 | async-start | bytes 589824 | tf_op jit(solution)/shard_map/all_to_all | solution.py:498
  182.8 0.7 copy-start.9

commit v4 on v3

--- a/solution.py
+++ b/solution.py
@@ -104,7 +104,7 @@
     )(source, *blocks, gains, *weights)
 
 
-def late_kernel(source_ref, b4_ref, gain_ref, w00_ref, w01_ref, w10_ref, w11_ref, square_ref, kv_ref, q_ref, lhs_ref, squares_ref, send_ref, send_q_ref):
+def late_kernel(source_ref, b4_ref, gain_ref, early_ref, w0_ref, w1_ref, square_ref, lhs_ref, squares_ref, send_ref, send_q_ref):
     square = square_ref[...]
     for k in range(2):
         square = normed(b4_ref.at[k], gain_ref[source_ref[6 + k]], lhs_ref, k, square)
@@ -113,14 +113,13 @@
     squares = jnp.concatenate(tail + [jnp.zeros((3, 128), F32)], axis=0)
     squares_ref[...] = squares
     upper = squares.astype(BF16)
-    lower = (squares - upper.astype(F32)).astype(BF16)
     send_q_ref[256:264] = upper
-    send_q_ref[264:272] = lower
-    lhs = columns([lhs_ref[k] for k in range(2)])
-    for m, (one, two) in enumerate(((w00_ref, w01_ref), (w10_ref, w11_ref))):
-        rows = [jnp.concatenate([one[i], two[i]], axis=0) for i in range(3)]
-        both = kv_ref[m] + dot(lhs[:HALF], columns(rows[:2]), ((1,), (0,)))
-        query = q_ref[m] + dot(lhs[HALF:], rows[2], ((1,), (0,)))
+    send_q_ref[264:272] = (squares - upper.astype(F32)).astype(BF16)
+    lhs = columns([early_ref[k] for k in range(6)] + [lhs_ref[k] for k in range(2)])
+    for m, ref in enumerate((w0_ref, w1_ref)):
+        pair = columns([rows_of(ref, i, source_ref, range(8)) for i in range(2)])
+        both = dot(lhs[:HALF], pair, ((1,), (0,)))
+        query = dot(lhs[HALF:], rows_of(ref, 2, source_ref, range(8)), ((1,), (0,)))
         send_q_ref[m * 128 : (m + 1) * 128] = query.astype(BF16)
         for i in range(2):
             send_ref[2 * m + i] = both[:, i * 128 : (i + 1) * 128].astype(BF16)
@@ -130,8 +129,13 @@
     return pl.BlockSpec(shape, lambda i, *_: (0,) * len(shape))
 
 
-def project_late(source, block, gains, weights, square, kv, query):
-    picked = [pl.BlockSpec((3, 256, 128), lambda i, s, k=k: (0, s[6 + k], 0)) for k in range(2)]
+def picked_specs(depth, first):
+    return [
+        pl.BlockSpec((depth, 256, 128), lambda i, s, k=k: (first, s[6 + k], 0)) for k in range(2)
+    ]
+
+
+def project_late(source, block, gains, early, weights, square):
     return pl.pallas_call(
         late_kernel,
         grid_spec=pltpu.PrefetchScalarGridSpec(
@@ -140,11 +144,10 @@
             in_specs=[
                 whole_spec(2, 2, ROWS_IN, 128),
                 whole_spec(8, 2, 2, 128),
-                *picked,
-                *picked,
+                whole_spec(6, ROWS_IN, 256),
+                whole_spec(3, 2048, 128),
+                whole_spec(3, 2048, 128),
                 whole_spec(ROWS_IN, 128),
-                whole_spec(2, HALF, 256),
-                whole_spec(2, 128, 128),
             ],
             out_specs=[
                 whole_spec(2, ROWS_IN, 256),
@@ -160,7 +163,7 @@
             jax.ShapeDtypeStruct((272, 128), BF16),
         ],
         name="project_late",
-    )(source, block, gains, weights[0], weights[0], weights[1], weights[1], square, kv, query)
+    )(source, block, gains, early, *weights, square)
 
 
 def rate_of(squares_ref, other_ref):
@@ -168,12 +171,13 @@
     return lax.rsqrt((squares_ref[...] + theirs) * (1.0 / 4096) + EPS)
 
 
-def query_kernel(source_ref, early_ref, late_ref, w0_ref, w1_ref, squares_ref, other_ref, count_ref, q_ref):
+def query_kernel(source_ref, late_ref, w00_ref, w01_ref, w10_ref, w11_ref, near_ref, squares_ref, other_ref, count_ref, q_ref):
     core = source_ref[8]
     column = row_to_column(rate_of(squares_ref, other_ref)[4:5])
-    lhs = columns([early_ref[k] for k in range(6)] + [late_ref[k] for k in range(2)])
-    for m, ref in enumerate((w0_ref, w1_ref)):
-        near = dot(lhs, rows_of(ref, 0, source_ref, range(8)), ((1,), (0,)))
+    lhs = columns([late_ref[k] for k in range(2)])
+    for m, (one, two) in enumerate(((w00_ref, w01_ref), (w10_ref, w11_ref))):
+        rows = jnp.concatenate([one[0], two[0]], axis=0)
+        near = near_ref[m] + dot(lhs, rows, ((1,), (0,)))
         total = near + other_ref[m * 128 : (m + 1) * 128].astype(F32)
         value = (total * column).astype(BF16)
         for z in range(4):
@@ -181,19 +185,18 @@
             q_ref[z, m, 128:] = count_ref[z]
 
 
-def finish_queries(source, early, late, weights, squares, other, counts):
-    last = lambda i, *_: (0, HALF // 128, 0)
-    weight = pl.BlockSpec((1, 2048, 128), lambda i, *_: (2, 0, 0))
+def finish_queries(source, late, weights, near, squares, other, counts):
+    picked = picked_specs(1, 2)
     return pl.pallas_call(
         query_kernel,
         grid_spec=pltpu.PrefetchScalarGridSpec(
             num_scalar_prefetch=1,
             grid=(1,),
             in_specs=[
-                pl.BlockSpec((6, 128, 256), last),
-                pl.BlockSpec((2, 128, 256), last),
-                weight,
-                weight,
+                pl.BlockSpec((2, 128, 256), lambda i, *_: (0, HALF // 128, 0)),
+                *picked,
+                *picked,
+                whole_spec(2, 128, 128),
                 whole_spec(8, 128),
                 whole_spec(272, 128),
                 whole_spec(4, 64, 128),
@@ -202,35 +205,31 @@
         ),
         out_shape=jax.ShapeDtypeStruct((4, 2, 192, 128), BF16),
         name="finish_queries",
-    )(source, early, late, *weights, squares, other, counts)
-
-
-def near_kernel(source_ref, early_ref, late_ref, w0_ref, w1_ref, keep_ref):
-    lhs = columns([early_ref[k] for k in range(6)] + [late_ref[k] for k in range(2)])
-    for m, ref in enumerate((w0_ref, w1_ref)):
-        pair = columns([rows_of(ref, i, source_ref, range(8)) for i in range(2)])
-        both = dot(lhs, pair, ((1,), (0,)))
+    )(source, late, weights[0], weights[0], weights[1], weights[1], near, squares, other, counts)
+
+
+def near_kernel(source_ref, late_ref, w00_ref, w01_ref, w10_ref, w11_ref, kv_ref, keep_ref):
+    lhs = columns([late_ref[k] for k in range(2)])
+    for m, (one, two) in enumerate(((w00_ref, w01_ref), (w10_ref, w11_ref))):
+        rows = [jnp.concatenate([one[i], two[i]], axis=0) for i in range(2)]
+        both = kv_ref[m] + dot(lhs, columns(rows), ((1,), (0,)))
         keep_ref[m, 0] = both[:, :128]
         keep_ref[m, 1] = both[:, 128:]
 
 
-def project_near(source, early, late, weights):
+def project_near(source, late, weights, kv):
+    picked = picked_specs(2, 0)
     return pl.pallas_call(
         near_kernel,
         grid_spec=pltpu.PrefetchScalarGridSpec(
             num_scalar_prefetch=1,
             grid=(1,),
-            in_specs=[
-                whole_spec(6, HALF, 256),
-                whole_spec(2, HALF, 256),
-                whole_spec(2, 2048, 128),
-                whole_spec(2, 2048, 128),
-            ],
+            in_specs=[whole_spec(2, HALF, 256), *picked, *picked, whole_spec(2, HALF, 256)],
             out_specs=whole_spec(2, 2, HALF, 128),
         ),
         out_shape=jax.ShapeDtypeStruct((2, 2, HALF, 128), F32),
         name="project_near",
-    )(source, early, late, *weights)
+    )(source, late, weights[0], weights[0], weights[1], weights[1], kv)
 
 
 def finish_kernel(keep_ref, squares_ref, other_q_ref, other_ref, own_ref, give_ref):
@@ -436,6 +435,14 @@
     return jnp.concatenate([encoder[0], decoder[0]], axis=0)
 
 
+def block_order(column, core):
+    sign = 1 - 2 * ((column + core) % 2)
+    offsets = jnp.array([0, 0, 1, 1, -1, -1, -2, -2], jnp.int32)
+    origin = (column + sign * offsets) % 4
+    half = (core + jnp.arange(8)) % 2
+    return (2 * origin + half).astype(jnp.int32)
+
+
 def step(tokens, nb_ids, nb_index, table, norm_gains, projections):
     core, section, here = lax.axis_index("c"), lax.axis_index("s"), lax.axis_index("y")
     column = lax.axis_index("x")
@@ -462,28 +469,23 @@
     sign = 1 - 2 * ((here + core) % 2)
     offsets = after(jnp.array([0, 1, -1, -2, 2, 3, -3, -4], jnp.int32), first)
     source = jnp.concatenate([(here + sign * offsets) % 8, core.reshape(1)]).astype(jnp.int32)
-    sign = 1 - 2 * ((column + core) % 2)
-    origin = (column + sign * offsets[:4]) % 4
-    order = (2 * origin[:, None] + jnp.stack([core, 1 - core])[None]).reshape(8).astype(jnp.int32)
-
     third = exchange(second, "y", 8, 0)
-    third, gains, counts, source, order = lax.optimization_barrier(
-        (third, gains, counts, source, order)
-    )
+    third, gains, counts, source = lax.optimization_barrier((third, gains, counts, source))
     fourth = exchange(third, "y", 8, 1)
-    diagonal = swap(after(across, third), "c")
-
+    beside = (mine, beside)
+    early, square, kv, query = project_early(source, (chunk, first, second, third), gains, beside)
+    across = after(across, square)
+    diagonal = swap(across, "c")
     far = (across, diagonal)
-    early, square, kv, query = project_early(source, (chunk, first, second, third), gains, far)
-    late, squares, send, send_q = project_late(source, fourth, gains, far, square, kv, query)
+    late, squares, send, send_q = project_late(source, fourth, gains, early, far, square)
     other_q = swap(send_q, "s")
     other = swap(send, "s")
-    beside = (mine, beside)
-    queries = finish_queries(source, early, late, beside, squares, other_q, counts)
+    queries = finish_queries(source, late, beside, query, squares, other_q, counts)
     queries = queries.reshape(8, 192, 128)
     queries = lax.all_to_all(queries, ("zh", "c"), 0, 0)
-    keep = project_near(source, early, late, beside)
+    keep = project_near(source, late, beside, kv)
     near, give = finish(keep, squares, other_q, other)
+    order = block_order(column, core)
     wo_diagonal = swap(wo_section, "c")
     near = jnp.stack([near, swap(give, "c")])
     following = exchange(near, "x", 4, 0)

time: 213 us -> 217 us (1.019)
  local copies, waits for them, and re-layouts: 15.5 us -> 18.1 us
    ppermute x6, waiting for transfers between devices: 29 us -> 35.7 us  [exchange(): return lax.ppermute(value, (axis, 'c'), pairs(size, turn))]
    all_to_all x1, waiting for transfers between devices: 12.9 us -> 8.32 us  [step(): queries = lax.all_to_all(queries, ('zh', 'c'), 0, 0)]
    ppermute x10, waiting for transfers between devices: 13.3 us -> 9.29 us  [swap(): return lax.ppermute(value, axis, [(0, 1), (1, 0)])]
    ppermute x10, starting transfers between devices: 34.3 us -> 37 us  [swap(): return lax.ppermute(value, axis, [(0, 1), (1, 0)])]
    unnamed x30 -> x36, local copies, waits for them, and re-layouts: 3.83 us -> 5.18 us
  transfers between devices with their start and end apart: 18 -> 18, of which waited for: 11 -> 10; matrix products, arithmetic and copies ran while one was open for 7% -> 7% of each run, Pallas kernels for 14% -> 11%
where the time goes in v4:
time: 217 us; the launch traced here: 215 us
  waiting for transfers between devices  65.8 us (30%)
  starting transfers between devices  61.3 us (28%)
  Pallas kernels  37.8 us (17%)
  blocking collectives  23.3 us (11%)
  local copies, waits for them, and re-layouts  18.1 us (8%)
  other arithmetic  7.37 us (3%)
    ppermute x10, starting transfers between devices, swap(): return lax.ppermute(value, axis, [(0, 1), (1, 0)])  37 us
    ppermute x6, waiting for transfers between devices, exchange(): return lax.ppermute(value, (axis, 'c'), pairs(size, turn))  35.7 us
    all_to_all x1, blocking collectives, step(): out = lax.all_to_all(out, ('s', 'y', 'c'), 0, 0)  23.3 us
    all_to_all x1, waiting for transfers between devices, step(): parts = lax.all_to_all(parts, ('s', 'zh', 'c'), 0, 0)  12.5 us
    ppermute x6, starting transfers between devices, exchange(): return lax.ppermute(value, (axis, 'c'), pairs(size, turn))  11.5 us
    ppermute x10, waiting for transfers between devices, swap(): return lax.ppermute(value, axis, [(0, 1), (1, 0)])  9.29 us
    all_to_all x1, starting transfers between devices, step(): queries = lax.all_to_all(queries, ('zh', 'c'), 0, 0)  8.65 us
    all_to_all x1, waiting for transfers between devices, step(): queries = lax.all_to_all(queries, ('zh', 'c'), 0, 0)  8.32 us
  transfers between devices with their start and end apart: 18, of which 10 were waited for; matrix products, arithmetic and copies ran while one was open for 7% of the time, Pallas kernels for 11%

profile of v4, /device:TPU:1, one launch (start us, length us, event | category | flops | bytes accessed | tf_op | source)
XLA Modules:
  0.0 214.9 jit_solution(8417597235904290438)
XLA Ops:
  0.0 0.8 constant_dynamic-slice_fusion.3
  0.8 1.0 constant_dynamic-slice_fusion.4
  1.8 8.7 %collective-permute-start = (bf16[640,128]{1,0:T(8,128)(2,1)S(1)}, bf16[640,128]{1,0:T(8,128)(2,1)S(1)}, u32[]{:S(2)}, u32[]{:S(2)}) collective-permute-start(bf16[640,128]{1,0:T(8,128)(2,1)S(1)} %pad_maximum_fusion.6), channel_id=1, source_target_pairs={{0,1},{1,0},{2,3},{3,2},{4,5},{5,4},{6,7},{7,6},{8,9},{9,8},{10,11... | collective-permute-start | bytes 491528 | tf_op jit(solution)/shard_map/ppermute | solution.py:391
  10.6 0.6 constant_dynamic-slice_fusion
  11.2 0.8 convert_reduce_fusion
  12.0 1.1 dynamic-slice_bitcast_fusion.2
  13.1 1.3 dynamic-slice_bitcast_fusion
  14.4 1.9 collective-permute-start.1
  16.4 1.4 pad_maximum_fusion.1
  17.7 1.9 collective-permute-start.6
  19.7 3.7 %collective-permute-done.1.b1_ref = bf16[2,640,128]{2,1,0:T(8,128)(2,1)S(1)} collective-permute-done((bf16[2,640,128]{2,1,0:T(8,128)(2,1)S(1)}, bf16[2,640,128]{2,1,0:T(8,128)(2,1)S(1)}, u32[]{:S(2)}, u32[]{:S(2)}) %collective-permute-start.1) | collective-permute-done | bytes 327712 | tf_op jit(solution)/shard_map/ppermute | solution.py:424
  23.5 1.2 dynamic-slice_bitcast_fusion.3
  24.7 1.3 dynamic-slice_bitcast_fusion.1
  26.1 1.9 collective-permute-start.5
  28.1 1.0 pad_maximum_fusion.3
  29.0 1.9 collective-permute-start.2
  31.0 0.5 fusion.1
  31.8 1.0 copy.20
  32.8 1.6 reshape.103
  34.4 6.5 %collective-permute-done.2.b2_ref = bf16[2,2,640,128]{3,2,1,0:T(8,128)(2,1)} collective-permute-done((bf16[2,2,640,128]{3,2,1,0:T(8,128)(2,1)}, bf16[2,2,640,128]{3,2,1,0:T(8,128)(2,1)}, u32[]{:S(2)}, u32[]{:S(2)}) %collective-permute-start.2) | collective-permute-done | bytes 655392 | tf_op jit(solution)/shard_map/ppermute | solution.py:424
  41.0 1.9 collective-permute-start.3
  43.0 0.7 reshape.104.count_ref
  43.7 0.6 pad_add_fusion.source_ref
  44.3 9.5 %collective-permute-done.3.b3_ref = bf16[2,2,640,128]{3,2,1,0:T(8,128)(2,1)} collective-permute-done((bf16[2,2,640,128]{3,2,1,0:T(8,128)(2,1)}, bf16[2,2,640,128]{3,2,1,0:T(8,128)(2,1)}, u32[]{:S(2)}, u32[]{:S(2)}) %collective-permute-start.3) | collective-permute-done | bytes 655392 | tf_op jit(solution)/shard_map/ppermute | solution.py:424
  53.8 1.2 copy-done.2
  55.0 5.2 %project_early.1 = (bf16[6,640,256]{2,1,0:T(8,128)(2,1)}, f32[640,128]{1,0:T(8,128)}, f32[2,512,256]{2,1,0:T(8,128)}, f32[2,128,128]{2,1,0:T(8,128)}) custom-call(s32[9]{0:T(128)} %pad_add_fusion.source_ref, bf16[2,640,128]{2,1,0:T(8,128)(2,1)} %copy-done.9, bf16[2,640,128]{2,1,0:T(8,128)(2,1)} %copy-done.8, ...), custom_call_target="tpu_custom_call" | custom-call | tf_op jit(solution)/shard_map/project_early/pallas_call | solution.py:93
  60.2 4.4 %collective-permute-start.7 = (bf16[3,2048,128]{2,1,0:T(8,128)(2,1)}, bf16[3,2048,128]{2,1,0:T(8,128)(2,1)S(1)}, u32[]{:S(2)}, u32[]{:S(2)}) collective-permute-start(bf16[3,2048,128]{2,1,0:T(8,128)(2,1)} %collective-permute-done.6.w0_ref), channel_id=1, source_target_pairs={{0,1},{1,0},{2,3},{3,2},{4,5},{5,4},{6,7},{7,6},{8,9},{9,8},{10,11... | collective-permute-start | bytes 4718600 | tf_op jit(solution)/shard_map/ppermute | solution.py:391
  64.6 1.9 collective-permute-start.4
  66.5 9.9 %collective-permute-done.4.b4_ref = bf16[2,2,640,128]{3,2,1,0:T(8,128)(2,1)S(1)} collective-permute-done((bf16[2,2,640,128]{3,2,1,0:T(8,128)(2,1)}, bf16[2,2,640,128]{3,2,1,0:T(8,128)(2,1)S(1)}, u32[]{:S(2)}, u32[]{:S(2)}) %collective-permute-start.4) | collective-permute-done | bytes 655392 | tf_op jit(solution)/shard_map/ppermute | solution.py:424
  76.4 0.8 copy-done.12
  77.3 0.6 copy-done.7
  77.9 5.7 %project_late.1 = (bf16[2,640,256]{2,1,0:T(8,128)(2,1)}, f32[8,128]{1,0:T(8,128)}, bf16[4,512,128]{2,1,0:T(8,128)(2,1)}, bf16[272,128]{1,0:T(8,128)(2,1)}) custom-call(s32[9]{0:T(128)} %pad_add_fusion.source_ref, bf16[2,2,640,128]{3,2,1,0:T(8,128)(2,1)} %copy-done.12, f32[8,2,2,128]{3,2,1,0:T(2,128)} %bitcast.60, ...), custom_call_target="tpu_custom_call" | custom-call | tf_op jit(solution)/shard_map/project_late/pallas_call | solution.py:139
  83.6 1.9 collective-permute-start.9
  85.5 3.4 %collective-permute-start.8 = (bf16[272,128]{1,0:T(8,128)(2,1)}, bf16[272,128]{1,0:T(8,128)(2,1)S(1)}, u32[]{:S(2)}, u32[]{:S(2)}) collective-permute-start(bf16[272,128]{1,0:T(8,128)(2,1)} %get-tuple-element.39), channel_id=1, source_target_pairs={{0,256},{256,0},{1,257},{257,1},{2,258},{258,2},{3,259},{259,3},{4... | collective-permute-start | bytes 208904 | tf_op jit(solution)/shard_map/ppermute | solution.py:391
  88.9 3.7 %project_near.1.keep_ref = f32[2,2,512,128]{3,2,1,0:T(8,128)} custom-call(s32[9]{0:T(128)} %pad_add_fusion.source_ref, bf16[2,640,256]{2,1,0:T(8,128)(2,1)} %get-tuple-element.36.late_ref, bf16[3,2048,128]{2,1,0:T(8,128)(2,1)} %copy-done.1, bf16[3,2048,128]{2,1,0:T(8,128)(2,1)} %copy-done.1, bf16[3,2048,128]{2,1,0:T(8,128)(2,1)} %copy-done.2, ...), custom_call_target="tpu_custom_call" | custom-call | tf_op jit(solution)/shard_map/project_near/pallas_call | solution.py:222
  92.5 6.0 %collective-permute-done.8.other_ref.other_q_ref = bf16[272,128]{1,0:T(8,128)(2,1)S(1)} collective-permute-done((bf16[272,128]{1,0:T(8,128)(2,1)}, bf16[272,128]{1,0:T(8,128)(2,1)S(1)}, u32[]{:S(2)}, u32[]{:S(2)}) %collective-permute-start.8) | collective-permute-done | bytes 69664 | tf_op jit(solution)/shard_map/ppermute | solution.py:391
  98.6 0.6 copy-done.14
  99.4 2.3 %finish.1 = (bf16[2,512,128]{2,1,0:T(8,128)(2,1)}, bf16[2,512,128]{2,1,0:T(8,128)(2,1)}) custom-call(f32[2,2,512,128]{3,2,1,0:T(8,128)} %project_near.1.keep_ref, f32[8,128]{1,0:T(8,128)} %get-tuple-element.38.squares_ref, bf16[272,128]{1,0:T(8,128)(2,1)} %copy-done.14, bf16[4,512,128]{2,1,0:T(8,128)(2,1)} %copy-done.13), custom_call_target="tpu_custom_call" | custom-call | tf_op jit(solution)/shard_map/finish/pallas_call | solution.py:249
  101.7 4.8 %collective-permute-start.10 = (bf16[2,512,128]{2,1,0:T(8,128)(2,1)}, bf16[2,512,128]{2,1,0:T(8,128)(2,1)S(1)}, u32[]{:S(2)}, u32[]{:S(2)}) collective-permute-start(bf16[2,512,128]{2,1,0:T(8,128)(2,1)} %get-tuple-element.44), channel_id=1, source_target_pairs={{0,1},{1,0},{2,3},{3,2},{4,5},{5,4},{6,7},{7,6},{8,9},{9,8},{10,11... | collective-permute-start | bytes 786440 | tf_op jit(solution)/shard_map/ppermute | solution.py:391
  106.5 1.4 collective-permute-done.10
  107.9 1.0 fusion.18
  108.9 1.9 collective-permute-start.11
  110.9 1.3 slice_bitcast_fusion.w0_ref
  112.2 1.9 collective-permute-start.14
  114.1 6.0 %collective-permute-done.11.next_ref = bf16[2,2,512,128]{3,2,1,0:T(8,128)(2,1)S(1)} collective-permute-done((bf16[2,2,512,128]{3,2,1,0:T(8,128)(2,1)S(1)}, bf16[2,2,512,128]{3,2,1,0:T(8,128)(2,1)S(1)}, u32[]{:S(2)}, u32[]{:S(2)}) %collective-permute-start.11) | collective-permute-done | bytes 524320 | tf_op jit(solution)/shard_map/ppermute | solution.py:424
  120.1 1.1 pad_maximum_fusion.2
  121.2 1.9 collective-permute-start.12
  123.1 3.0 %finish_queries.1 = bf16[4,2,192,128]{3,2,1,0:T(8,128)(2,1)} custom-call(s32[9]{0:T(128)} %pad_add_fusion.source_ref, bf16[2,640,256]{2,1,0:T(8,128)(2,1)} %get-tuple-element.36.late_ref, bf16[3,2048,128]{2,1,0:T(8,128)(2,1)} %copy-done.1, bf16[3,2048,128]{2,1,0:T(8,128)(2,1)} %copy-done.1, bf16[3,2048,128]{2,1,0:T(8,128)(2,1)} %copy-done.2, ...), custom_call_target="tpu_custom_call" | custom-call | tf_op jit(solution)/shard_map/finish_queries/pallas_call | solution.py:190
  126.1 8.6 %all-to-all-start = ((bf16[8,192,128]{2,1,0:T(8,128)(2,1)}), bf16[8,192,128]{2,1,0:T(8,128)(2,1)S(1)}, u32[]{:S(2)}, u32[]{:S(2)}) async-start(bf16[8,192,128]{2,1,0:T(8,128)(2,1)} %bitcast.50), calls=%async_computation | async-start | bytes 786432 | tf_op jit(solution)/shard_map/all_to_all | solution.py:485
  134.7 1.9 collective-permute-start.13
  136.6 1.9 collective-permute-done.14.w2_ref
  138.5 6.1 %collective-permute-start.15 = (bf16[4096,128]{1,0:T(8,128)(2,1)}, bf16[4096,128]{1,0:T(8,128)(2,1)}, u32[]{:S(2)}, u32[]{:S(2)}) collective-permute-start(bf16[4096,128]{1,0:T(8,128)(2,1)} %collective-permute-done.14.w2_ref), channel_id=1, source_target_pairs={{0,1},{1,0},{2,3},{3,2},{4,5},{5,4},{6,7},{7,6},{8,9},{9,8},{10,11... | collective-permute-start | bytes 3145736 | tf_op jit(solution)/shard_map/ppermute | solution.py:391
  144.6 0.5 fusion.13.order_ref
  145.1 8.3 %all-to-all-done = bf16[8,192,128]{2,1,0:T(8,128)(2,1)S(1)} async-done(((bf16[8,192,128]{2,1,0:T(8,128)(2,1)}), bf16[8,192,128]{2,1,0:T(8,128)(2,1)S(1)}, u32[]{:S(2)}, u32[]{:S(2)}) %all-to-all-start) | async-done | bytes 393248 | tf_op jit(solution)/shard_map/all_to_all | solution.py:485
  153.7 0.7 reshape.109.count_ref
  154.4 6.3 %attend_near.1 = (f32[1024,128]{1,0:T(8,128)}, f32[1024,128]{1,0:T(8,128)}) custom-call(s32[8]{0:T(128)} %fusion.13.order_ref, bf16[4,2,192,128]{3,2,1,0:T(8,128)(2,1)} %bitcast.46, bf16[2,2,512,128]{3,2,1,0:T(8,128)(2,1)} %copy-done.5, bf16[2,2,512,128]{3,2,1,0:T(8,128)(2,1)} %copy-done.6, bf16[4,8,4,512]{3,2,1,0:T(4,128)(2,1)} %reshape.109.count_ref), custom_call_target="tpu_custom_call" | custom-call | tf_op jit(solution)/shard_map/attend_near/pallas_call | solution.py:306
  160.7 1.0 copy-done.11
  161.7 6.6 %attend_far.1 = bf16[2,4,2,72,128]{4,3,2,1,0:T(8,128)(2,1)} custom-call(s32[8]{0:T(128)} %fusion.13.order_ref, bf16[4,2,192,128]{3,2,1,0:T(8,128)(2,1)} %bitcast.47, bf16[2,2,2,512,128]{4,3,2,1,0:T(8,128)(2,1)} %copy-done.11, bf16[4,8,4,512]{3,2,1,0:T(4,128)(2,1)} %reshape.109.count_ref, f32[1024,128]{1,0:T(8,128)} %get-tuple-element.45.part_ref, ...), custom_call_target="tpu_custom_call" | custom-call | tf_op jit(solution)/shard_map/attend_far/pallas_call | solution.py:321
  168.3 4.2 %all-to-all-start.1 = ((bf16[16,72,128]{2,1,0:T(8,128)(2,1)}), bf16[16,72,128]{2,1,0:T(8,128)(2,1)S(1)}, u32[]{:S(2)}, u32[]{:S(2)}) async-start(bf16[16,72,128]{2,1,0:T(8,128)(2,1)} %bitcast.52), calls=%async_computation.1 | async-start | bytes 589824 | tf_op jit(solution)/shard_map/all_to_all | solution.py:500
  172.5 12.5 %all-to-all-done.1 = bf16[16,72,128]{2,1,0:T(8,128)(2,1)S(1)} async-done(((bf16[16,72,128]{2,1,0:T(8,128)(2,1)}), bf16[16,72,128]{2,1,0:T(8,128)(2,1)S(1)}, u32[]{:S(2)}, u32[]{:S(2)}) %all-to-all-start.1) | async-done | bytes 294944 | tf_op jit(solution)/shard_map/all_to_all | solution.py:500
  185.0 0.7 copy-done.10
  185.7 5.1 %mix.1 = bf16[32,64,128]{2,1,0:T(8,128)(2,1)} custom-call(s32[1]{0:T(128)} %bitcast.place_ref, bf16[2,4,2,72,128]{4,3,2,1,0:T(8,128)(2,1)} %bitcast.53, bf16[4096,128]{1,0:T(8,128)(2,1)} %copy-done.4, bf16[4096,128]{1,0:T(8,128)(2,1)} %collective-permute-done.13.w1_ref, bf16[4096,128]{1,0:T(8,128)(2,1)} %collective-permute-done.14.w2_ref, ...), custom_call_target="tpu_custom_call" | custom-call | tf_op jit(solution)/shard_map/mix/pallas_call | solution.py:370
  190.8 23.3 %all_to_all.15 = bf16[32,64,128]{2,1,0:T(8,128)(2,1)S(1)} all-to-all(bf16[32,64,128]{2,1,0:T(8,128)(2,1)} %mix.1), channel_id=1, replica_groups=mesh['s'=2,'zh'=4,'x'=4,'y'=8,'c'=2] {'s','y','c'}, dimensions={0} | all-to-all | bytes 1048576 | tf_op jit(solution)/shard_map/all_to_all | solution.py:504
  214.1 0.7 reduce_sum.22
  (51 shorter events, 1.1 us)
Async XLA Ops:
  0.0 10.6 %copy-start = (f32[2,4096]{1,0:T(2,128)S(1)}, f32[2,4096]{1,0:T(2,128)}, u32[]{:S(2)}) copy-start(f32[2,4096]{1,0:T(2,128)} %param.12) | copy-start | bytes 98308
  1.8 10.2 %collective-permute-start = (bf16[640,128]{1,0:T(8,128)(2,1)S(1)}, bf16[640,128]{1,0:T(8,128)(2,1)S(1)}, u32[]{:S(2)}, u32[]{:S(2)}) collective-permute-start(bf16[640,128]{1,0:T(8,128)(2,1)S(1)} %pad_maximum_fusion.6), channel_id=1, source_target_pairs={{0,1},{1,0},{2,3},{3,2},{4,5},{5,4},{6,7},{7,6},{8,9},{9,8},{10,11... | collective-permute-start | bytes 491528 | tf_op jit(solution)/shard_map/ppermute | solution.py:391
  14.4 5.2 %copy-start.9 = (bf16[2,640,128]{2,1,0:T(8,128)(2,1)}, bf16[2,640,128]{2,1,0:T(8,128)(2,1)S(1)}, u32[]{:S(2)}) copy-start(bf16[2,640,128]{2,1,0:T(8,128)(2,1)S(1)} %maximum_select_fusion.1.b0_ref) | copy-start | bytes 983044
  14.4 9.0 %collective-permute-start.1 = (bf16[2,640,128]{2,1,0:T(8,128)(2,1)S(1)}, bf16[2,640,128]{2,1,0:T(8,128)(2,1)S(1)}, u32[]{:S(2)}, u32[]{:S(2)}) collective-permute-start(bf16[2,640,128]{2,1,0:T(8,128)(2,1)S(1)} %maximum_select_fusion.1.b0_ref), channel_id=1, source_target_pairs={{0,2},{1,15},{2,0},{3,5},{4,6},{5,3},{6,4},{7,9},{8,10},{9,7},{10,... | collective-permute-start | bytes 983048 | tf_op jit(solution)/shard_map/ppermute | solution.py:424
  17.7 42.4 %collective-permute-start.6 = (bf16[3,2048,128]{2,1,0:T(8,128)(2,1)}, bf16[3,2048,128]{2,1,0:T(8,128)(2,1)}, u32[]{:S(2)}, u32[]{:S(2)}) collective-permute-start(bf16[3,2048,128]{2,1,0:T(8,128)(2,1)} %pad_maximum_fusion.1), channel_id=1, source_target_pairs={{0,256},{256,0},{1,257},{257,1},{2,258},{258,2},{3,259},{259,3},{4... | collective-permute-start | bytes 4718600 | tf_op jit(solution)/shard_map/ppermute | solution.py:391
  23.5 4.6 %copy-start.8 = (bf16[2,640,128]{2,1,0:T(8,128)(2,1)}, bf16[2,640,128]{2,1,0:T(8,128)(2,1)S(1)}, u32[]{:S(2)}) copy-start(bf16[2,640,128]{2,1,0:T(8,128)(2,1)S(1)} %collective-permute-done.1.b1_ref) | copy-start | bytes 983044
  26.0 5.0 %copy-start.15 = (s32[8,128]{1,0:T(8,128)S(1)}, s32[8,128]{1,0:T(8,128)}, u32[]{:S(2)}) copy-start(s32[8,128]{1,0:T(8,128)} %param.9) | copy-start | bytes 12292
  26.1 6.7 %copy-start.1 = (bf16[3,2048,128]{2,1,0:T(8,128)(2,1)}, bf16[3,2048,128]{2,1,0:T(8,128)(2,1)S(1)}, u32[]{:S(2)}) copy-start(bf16[3,2048,128]{2,1,0:T(8,128)(2,1)S(1)} %pad_maximum_fusion.w0_ref.w00_ref.w01_ref) | copy-start | bytes 4718596
  26.1 27.7 %collective-permute-start.5 = (bf16[3,2048,128]{2,1,0:T(8,128)(2,1)S(1)}, bf16[3,2048,128]{2,1,0:T(8,128)(2,1)S(1)}, u32[]{:S(2)}, u32[]{:S(2)}) collective-permute-start(bf16[3,2048,128]{2,1,0:T(8,128)(2,1)S(1)} %pad_maximum_fusion.w0_ref.w00_ref.w01_ref), channel_id=1, source_target_pairs={{0,1},{1,0},{2,3},{3,2},{4,5},{5,4},{6,7},{7,6},{8,9},{9,8},{10,11... | collective-permute-start | bytes 4718600 | tf_op jit(solution)/shard_map/ppermute | solution.py:391
  29.0 11.9 %collective-permute-start.2 = (bf16[2,2,640,128]{3,2,1,0:T(8,128)(2,1)}, bf16[2,2,640,128]{3,2,1,0:T(8,128)(2,1)}, u32[]{:S(2)}, u32[]{:S(2)}) collective-permute-start(bf16[2,2,640,128]{3,2,1,0:T(8,128)(2,1)} %pad_maximum_fusion.3), channel_id=1, source_target_pairs={{0,14},{1,3},{2,4},{3,1},{4,2},{5,7},{6,8},{7,5},{8,6},{9,11},{10,... | collective-permute-start | bytes 1966088 | tf_op jit(solution)/shard_map/ppermute | solution.py:424
  31.0 12.7 %copy-start.17 = (s32[8]{0:T(128)S(1)}, s32[8]{0:T(128)}, u32[]{:S(2)}) copy-start(s32[8]{0:T(128)} %constant.133.clone) | copy-start | bytes 100
  41.0 12.8 %collective-permute-start.3 = (bf16[2,2,640,128]{3,2,1,0:T(8,128)(2,1)}, bf16[2,2,640,128]{3,2,1,0:T(8,128)(2,1)}, u32[]{:S(2)}, u32[]{:S(2)}) collective-permute-start(bf16[2,2,640,128]{3,2,1,0:T(8,128)(2,1)} %collective-permute-done.2.b2_ref), channel_id=1, source_target_pairs={{0,2},{1,15},{2,0},{3,5},{4,6},{5,3},{6,4},{7,9},{8,10},{9,7},{10,... | collective-permute-start | bytes 1966088 | tf_op jit(solution)/shard_map/ppermute | solution.py:424
  53.8 1.2 copy-start.2
  60.2 16.2 %collective-permute-start.7 = (bf16[3,2048,128]{2,1,0:T(8,128)(2,1)}, bf16[3,2048,128]{2,1,0:T(8,128)(2,1)S(1)}, u32[]{:S(2)}, u32[]{:S(2)}) collective-permute-start(bf16[3,2048,128]{2,1,0:T(8,128)(2,1)} %collective-permute-done.6.w0_ref), channel_id=1, source_target_pairs={{0,1},{1,0},{2,3},{3,2},{4,5},{5,4},{6,7},{7,6},{8,9},{9,8},{10,11... | collective-permute-start | bytes 4718600 | tf_op jit(solution)/shard_map/ppermute | solution.py:391
  64.6 11.8 %collective-permute-start.4 = (bf16[2,2,640,128]{3,2,1,0:T(8,128)(2,1)}, bf16[2,2,640,128]{3,2,1,0:T(8,128)(2,1)S(1)}, u32[]{:S(2)}, u32[]{:S(2)}) collective-permute-start(bf16[2,2,640,128]{3,2,1,0:T(8,128)(2,1)} %collective-permute-done.3.b3_ref), channel_id=1, source_target_pairs={{0,14},{1,3},{2,4},{3,1},{4,2},{5,7},{6,8},{7,5},{8,6},{9,11},{10,... | collective-permute-start | bytes 1966088 | tf_op jit(solution)/shard_map/ppermute | solution.py:424
  76.4 0.8 copy-start.12
  76.4 1.4 copy-start.7
  83.6 15.0 %collective-permute-start.9 = (bf16[4,512,128]{2,1,0:T(8,128)(2,1)}, bf16[4,512,128]{2,1,0:T(8,128)(2,1)S(1)}, u32[]{:S(2)}, u32[]{:S(2)}) collective-permute-start(bf16[4,512,128]{2,1,0:T(8,128)(2,1)} %get-tuple-element.42), channel_id=1, source_target_pairs={{0,256},{256,0},{1,257},{257,1},{2,258},{258,2},{3,259},{259,3},{4... | collective-permute-start | bytes 1572872 | tf_op jit(solution)/shard_map/ppermute | solution.py:391
  85.5 13.1 %collective-permute-start.8 = (bf16[272,128]{1,0:T(8,128)(2,1)}, bf16[272,128]{1,0:T(8,128)(2,1)S(1)}, u32[]{:S(2)}, u32[]{:S(2)}) collective-permute-start(bf16[272,128]{1,0:T(8,128)(2,1)} %get-tuple-element.39), channel_id=1, source_target_pairs={{0,256},{256,0},{1,257},{257,1},{2,258},{258,2},{3,259},{259,3},{4... | collective-permute-start | bytes 208904 | tf_op jit(solution)/shard_map/ppermute | solution.py:391
  98.6 0.6 copy-start.14
  98.6 0.8 copy-start.13
  101.7 6.2 %collective-permute-start.10 = (bf16[2,512,128]{2,1,0:T(8,128)(2,1)}, bf16[2,512,128]{2,1,0:T(8,128)(2,1)S(1)}, u32[]{:S(2)}, u32[]{:S(2)}) collective-permute-start(bf16[2,512,128]{2,1,0:T(8,128)(2,1)} %get-tuple-element.44), channel_id=1, source_target_pairs={{0,1},{1,0},{2,3},{3,2},{4,5},{5,4},{6,7},{7,6},{8,9},{9,8},{10,11... | collective-permute-start | bytes 786440 | tf_op jit(solution)/shard_map/ppermute | solution.py:391
  108.9 12.3 %copy-start.5 = (bf16[2,2,512,128]{3,2,1,0:T(8,128)(2,1)}, bf16[2,2,512,128]{3,2,1,0:T(8,128)(2,1)S(1)}, u32[]{:S(2)}) copy-start(bf16[2,2,512,128]{3,2,1,0:T(8,128)(2,1)S(1)} %get-tuple-element.48.near_ref) | copy-start | bytes 1572868
  108.9 11.1 %collective-permute-start.11 = (bf16[2,2,512,128]{3,2,1,0:T(8,128)(2,1)S(1)}, bf16[2,2,512,128]{3,2,1,0:T(8,128)(2,1)S(1)}, u32[]{:S(2)}, u32[]{:S(2)}) collective-permute-start(bf16[2,2,512,128]{3,2,1,0:T(8,128)(2,1)S(1)} %get-tuple-element.48.near_ref), channel_id=1, source_target_pairs={{0,16},{1,49},{16,0},{17,33},{32,48},{33,17},{48,32},{49,1},{2,18}... | collective-permute-start | bytes 1572872 | tf_op jit(solution)/shard_map/ppermute | solution.py:424
  112.2 22.6 %copy-start.4 = (bf16[4096,128]{1,0:T(8,128)(2,1)}, bf16[4096,128]{1,0:T(8,128)(2,1)S(1)}, u32[]{:S(2)}) copy-start(bf16[4096,128]{1,0:T(8,128)(2,1)S(1)} %slice_bitcast_fusion.w0_ref) | copy-start | bytes 3145732
  112.2 26.3 %collective-permute-start.14 = (bf16[4096,128]{1,0:T(8,128)(2,1)S(1)}, bf16[4096,128]{1,0:T(8,128)(2,1)}, u32[]{:S(2)}, u32[]{:S(2)}) collective-permute-start(bf16[4096,128]{1,0:T(8,128)(2,1)S(1)} %slice_bitcast_fusion.w0_ref), channel_id=1, source_target_pairs={{0,256},{256,0},{1,257},{257,1},{2,258},{258,2},{3,259},{259,3},{4... | collective-permute-start | bytes 3145736 | tf_op jit(solution)/shard_map/ppermute | solution.py:391
  120.1 6.0 %copy-start.6 = (bf16[2,2,512,128]{3,2,1,0:T(8,128)(2,1)}, bf16[2,2,512,128]{3,2,1,0:T(8,128)(2,1)S(1)}, u32[]{:S(2)}) copy-start(bf16[2,2,512,128]{3,2,1,0:T(8,128)(2,1)S(1)} %collective-permute-done.11.next_ref) | copy-start | bytes 1572868
  121.2 39.5 %collective-permute-start.12 = (bf16[2,2,2,512,128]{4,3,2,1,0:T(8,128)(2,1)}, bf16[2,2,2,512,128]{4,3,2,1,0:T(8,128)(2,1)S(1)}, u32[]{:S(2)}, u32[]{:S(2)}) collective-permute-start(bf16[2,2,2,512,128]{4,3,2,1,0:T(8,128)(2,1)} %pad_maximum_fusion.2), channel_id=1, source_target_pairs={{0,48},{1,17},{16,32},{17,1},{32,16},{33,49},{48,0},{49,33},{2,50}... | collective-permute-start | bytes 3145736 | tf_op jit(solution)/shard_map/ppermute | solution.py:424
  123.1 21.5 %copy-start.16 = (s32[8]{0:T(128)S(1)}, s32[8]{0:T(128)}, u32[]{:S(2)}) copy-start(s32[8]{0:T(128)} %constant.134.clone) | copy-start | bytes 100
  126.1 27.4 %all-to-all-start = ((bf16[8,192,128]{2,1,0:T(8,128)(2,1)}), bf16[8,192,128]{2,1,0:T(8,128)(2,1)S(1)}, u32[]{:S(2)}, u32[]{:S(2)}) async-start(bf16[8,192,128]{2,1,0:T(8,128)(2,1)} %bitcast.50), calls=%async_computation | async-start | bytes 786432 | tf_op jit(solution)/shard_map/all_to_all | solution.py:485
  134.7 37.7 %collective-permute-start.13 = (bf16[4096,128]{1,0:T(8,128)(2,1)S(1)}, bf16[4096,128]{1,0:T(8,128)(2,1)}, u32[]{:S(2)}, u32[]{:S(2)}) collective-permute-start(bf16[4096,128]{1,0:T(8,128)(2,1)S(1)} %slice_bitcast_fusion.w0_ref), channel_id=1, source_target_pairs={{0,1},{1,0},{2,3},{3,2},{4,5},{5,4},{6,7},{7,6},{8,9},{9,8},{10,11... | collective-permute-start | bytes 3145736 | tf_op jit(solution)/shard_map/ppermute | solution.py:391
  138.5 34.0 %collective-permute-start.15 = (bf16[4096,128]{1,0:T(8,128)(2,1)}, bf16[4096,128]{1,0:T(8,128)(2,1)}, u32[]{:S(2)}, u32[]{:S(2)}) collective-permute-start(bf16[4096,128]{1,0:T(8,128)(2,1)} %collective-permute-done.14.w2_ref), channel_id=1, source_target_pairs={{0,1},{1,0},{2,3},{3,2},{4,5},{5,4},{6,7},{7,6},{8,9},{9,8},{10,11... | collective-permute-start | bytes 3145736 | tf_op jit(solution)/shard_map/ppermute | solution.py:391
  153.5 0.9 copy-start.3
  160.7 1.0 copy-start.11
  168.3 16.7 %all-to-all-start.1 = ((bf16[16,72,128]{2,1,0:T(8,128)(2,1)}), bf16[16,72,128]{2,1,0:T(8,128)(2,1)S(1)}, u32[]{:S(2)}, u32[]{:S(2)}) async-start(bf16[16,72,128]{2,1,0:T(8,128)(2,1)} %bitcast.52), calls=%async_computation.1 | async-start | bytes 589824 | tf_op jit(solution)/shard_map/all_to_all | solution.py:500
  185.0 0.7 copy-start.10

commit v5 on v4

--- a/solution.py
+++ b/solution.py
@@ -273,18 +273,17 @@
     return dot(weights, values, ((1,), (0,))), total
 
 
-def near_attend_kernel(order_ref, q_ref, near_ref, next_ref, count_ref, part_ref, total_ref, expo_ref):
+def near_attend_kernel(order_ref, q_ref, near_ref, up_ref, down_ref, count_ref, part_ref, total_ref, expo_ref):
     queries = jnp.concatenate([q_ref[0, 0], q_ref[0, 1]], axis=0)
-    blocks = [near_ref.at[0], near_ref.at[1], next_ref.at[0], next_ref.at[1]]
+    blocks = [ref.at[i] for ref in (near_ref, up_ref, down_ref) for i in range(2)]
     part, total = partial(order_ref, 0, queries, blocks, count_ref, expo_ref)
     part_ref[...] = part
     total_ref[...] = jnp.broadcast_to(total, (4 * SPAN, 128))
 
 
-def far_attend_kernel(order_ref, q_ref, far_ref, count_ref, part_ref, total_ref, out_ref, expo_ref):
+def far_attend_kernel(order_ref, q_ref, first_ref, second_ref, count_ref, part_ref, total_ref, out_ref, expo_ref):
     queries = jnp.concatenate([q_ref[0, 0], q_ref[0, 1]], axis=0)
-    blocks = [far_ref.at[k, i] for k in range(2) for i in range(2)]
-    part, total = partial(order_ref, 4, queries, blocks, count_ref, expo_ref)
+    part, total = partial(order_ref, 6, queries, [first_ref, second_ref], count_ref, expo_ref)
     before = total_ref[:, 0:1]
     both = total + before
     inverse = jnp.where(both > 0.0, 1.0 / both, 0.0)
@@ -301,41 +300,36 @@
 PART_SPEC = pl.BlockSpec((4 * SPAN, HEAD_DIM), lambda i, *_: (i, 0))
 
 
-def attend_near(order, queries, near, following, counts):
+def attend_near(order, queries, near, up, down, counts):
     block = pl.BlockSpec((2, 2, HALF, HEAD_DIM), lambda i, *_: (0, 0, 0, 0))
     return pl.pallas_call(
         near_attend_kernel,
         grid_spec=pltpu.PrefetchScalarGridSpec(
             num_scalar_prefetch=1,
             grid=(4,),
-            in_specs=[QUERY_SPEC, block, block, COUNT_SPEC],
+            in_specs=[QUERY_SPEC, block, block, block, COUNT_SPEC],
             out_specs=[PART_SPEC, PART_SPEC],
-            scratch_shapes=[pltpu.VMEM((4 * SPAN, 4 * HALF), F32)],
+            scratch_shapes=[pltpu.VMEM((4 * SPAN, 6 * HALF), F32)],
         ),
         out_shape=[jax.ShapeDtypeStruct((16 * SPAN, HEAD_DIM), F32)] * 2,
         name="attend_near",
-    )(order, queries, near, following, counts)
-
-
-def attend_far(order, queries, beyond, counts, part, total):
+    )(order, queries, near, up, down, counts)
+
+
+def attend_far(order, queries, first, second, counts, part, total):
+    half = pl.BlockSpec((2, HALF, HEAD_DIM), lambda i, *_: (0, 0, 0))
     return pl.pallas_call(
         far_attend_kernel,
         grid_spec=pltpu.PrefetchScalarGridSpec(
             num_scalar_prefetch=1,
             grid=(4,),
-            in_specs=[
-                QUERY_SPEC,
-                pl.BlockSpec((2, 2, 2, HALF, HEAD_DIM), lambda i, *_: (0, 0, 0, 0, 0)),
-                COUNT_SPEC,
-                PART_SPEC,
-                PART_SPEC,
-            ],
+            in_specs=[QUERY_SPEC, half, half, COUNT_SPEC, PART_SPEC, PART_SPEC],
             out_specs=pl.BlockSpec((2, 1, 2, ROWS, HEAD_DIM), lambda i, *_: (0, i, 0, 0, 0)),
-            scratch_shapes=[pltpu.VMEM((4 * SPAN, 4 * HALF), F32)],
+            scratch_shapes=[pltpu.VMEM((4 * SPAN, 2 * HALF), F32)],
         ),
         out_shape=jax.ShapeDtypeStruct((2, 4, 2, ROWS, HEAD_DIM), BF16),
         name="attend_far",
-    )(order, queries, beyond, counts, part, total)
+    )(order, queries, first, second, counts, part, total)
 
 
 def merge(parts):
@@ -436,9 +430,8 @@
 
 
 def block_order(column, core):
-    sign = 1 - 2 * ((column + core) % 2)
-    offsets = jnp.array([0, 0, 1, 1, -1, -1, -2, -2], jnp.int32)
-    origin = (column + sign * offsets) % 4
+    offsets = jnp.array([0, 0, -1, -1, 1, 1, 2, 2], jnp.int32)
+    origin = (column + offsets) % 4
     half = (core + jnp.arange(8)) % 2
     return (2 * origin + half).astype(jnp.int32)
 
@@ -488,14 +481,18 @@
     order = block_order(column, core)
     wo_diagonal = swap(wo_section, "c")
     near = jnp.stack([near, swap(give, "c")])
-    following = exchange(near, "x", 4, 0)
-    beyond = exchange(jnp.stack([near, following]), "x", 4, 1)
+    ahead = [(i, (i + 1) % 4) for i in range(4)]
+    back = [(i, (i - 1) % 4) for i in range(4)]
+    up = lax.ppermute(near, "x", ahead)
+    down = lax.ppermute(near, "x", back)
+    up_far = lax.ppermute(up[0], "x", ahead)
+    down_far = lax.ppermute(down[1], "x", back)
     queries = queries.reshape(4, 2, 192, 128)
     counts = queries[:, :, 128:].reshape(4, 2, 2, 8, HALF).transpose(0, 3, 1, 2, 4)
     counts = counts.reshape(4, 8, 4, HALF)
 
-    part, total = attend_near(order, queries, near, following, counts)
-    parts = attend_far(order, queries, beyond, counts, part, total)
+    part, total = attend_near(order, queries, near, up, down, counts)
+    parts = attend_far(order, queries, up_far, down_far, counts, part, total)
     parts = parts.reshape(16, ROWS, HEAD_DIM)
     parts = lax.all_to_all(parts, ("s", "zh", "c"), 0, 0)
     place = (section * 2 + core).astype(jnp.int32).reshape(1)

time: 217 us -> 229 us (1.055)
  waiting for transfers between devices: 65.8 us -> 73.4 us
  starting transfers between devices: 61.3 us -> 68 us
    ppermute x10, waiting for transfers between devices: 9.29 us -> 26.8 us  [swap(): return lax.ppermute(value, axis, [(0, 1), (1, 0)])]
    ppermute x0 -> x4, starting transfers between devices: none -> 13 us  [the longest x1 4.57 us: step(): down_far = lax.ppermute(down[1], 'x', back)]
    ppermute x6 -> x4, waiting for transfers between devices: 35.7 us -> 29.8 us  [exchange(): return lax.ppermute(value, (axis, 'c'), pairs(size, turn))]
    all_to_all x1, waiting for transfers between devices: 8.32 us -> 4.29 us  [step(): queries = lax.all_to_all(queries, ('zh', 'c'), 0, 0)]
    ppermute x6 -> x4, starting transfers between devices: 11.5 us -> 7.66 us  [exchange(): return lax.ppermute(value, (axis, 'c'), pairs(size, turn))]
    all_to_all x1, starting transfers between devices: 4.16 us -> 7.4 us  [step(): parts = lax.all_to_all(parts, ('s', 'zh', 'c'), 0, 0)]
    ppermute x10, starting transfers between devices: 37 us -> 33.8 us  [swap(): return lax.ppermute(value, axis, [(0, 1), (1, 0)])]
    all_to_all x1, starting transfers between devices: 8.65 us -> 6.21 us  [step(): queries = lax.all_to_all(queries, ('zh', 'c'), 0, 0)]
  transfers between devices with their start and end apart: 18 -> 20, of which waited for: 10 -> 8; matrix products, arithmetic and copies ran while one was open for 7% -> 7% of each run, Pallas kernels for 11% -> 12%
where the time goes in v5:
time: 229 us; the launch traced here: 227 us
  waiting for transfers between devices  73.4 us (32%)
  starting transfers between devices  68 us (30%)
  Pallas kernels  38 us (17%)
  blocking collectives  23.4 us (10%)
  local copies, waits for them, and re-layouts  17.1 us (7%)
  other arithmetic  6.16 us (3%)
    ppermute x10, starting transfers between devices, swap(): return lax.ppermute(value, axis, [(0, 1), (1, 0)])  33.8 us
    ppermute x4, waiting for transfers between devices, exchange(): return lax.ppermute(value, (axis, 'c'), pairs(size, turn))  29.8 us
    ppermute x10, waiting for transfers between devices, swap(): return lax.ppermute(value, axis, [(0, 1), (1, 0)])  26.8 us
    all_to_all x1, blocking collectives, step(): out = lax.all_to_all(out, ('s', 'y', 'c'), 0, 0)  23.4 us
    all_to_all x1, waiting for transfers between devices, step(): parts = lax.all_to_all(parts, ('s', 'zh', 'c'), 0, 0)  12.5 us
    ppermute x4, starting transfers between devices, exchange(): return lax.ppermute(value, (axis, 'c'), pairs(size, turn))  7.66 us
    pallas_call x1, Pallas kernels, attend_near(): pl.pallas_call(near_attend_kernel, grid_spec=pltpu.PrefetchScalarGridSpec...  7.59 us
    all_to_all x1, starting transfers between devices, step(): parts = lax.all_to_all(parts, ('s', 'zh', 'c'), 0, 0)  7.4 us
  transfers between devices with their start and end apart: 20, of which 8 were waited for; matrix products, arithmetic and copies ran while one was open for 7% of the time, Pallas kernels for 12%

profile of v5, /device:TPU:1, one launch (start us, length us, event | category | flops | bytes accessed | tf_op | source)
XLA Modules:
  0.0 227.3 jit_solution(791217694387905059)
XLA Ops:
  0.0 0.8 constant_dynamic-slice_fusion.3
  0.8 1.0 constant_dynamic-slice_fusion.4
  1.8 8.7 %collective-permute-start = (bf16[640,128]{1,0:T(8,128)(2,1)S(1)}, bf16[640,128]{1,0:T(8,128)(2,1)S(1)}, u32[]{:S(2)}, u32[]{:S(2)}) collective-permute-start(bf16[640,128]{1,0:T(8,128)(2,1)S(1)} %pad_maximum_fusion.5), channel_id=1, source_target_pairs={{0,1},{1,0},{2,3},{3,2},{4,5},{5,4},{6,7},{7,6},{8,9},{9,8},{10,11... | collective-permute-start | bytes 491528 | tf_op jit(solution)/shard_map/ppermute | solution.py:385
  10.6 0.6 constant_dynamic-slice_fusion
  11.2 0.8 convert_reduce_fusion
  12.0 1.1 dynamic-slice_bitcast_fusion.2
  13.1 1.3 dynamic-slice_bitcast_fusion
  14.4 1.9 collective-permute-start.1
  16.4 1.4 pad_maximum_fusion.1
  17.7 1.9 collective-permute-start.6
  19.7 3.8 %collective-permute-done.1.b1_ref = bf16[2,640,128]{2,1,0:T(8,128)(2,1)S(1)} collective-permute-done((bf16[2,640,128]{2,1,0:T(8,128)(2,1)S(1)}, bf16[2,640,128]{2,1,0:T(8,128)(2,1)S(1)}, u32[]{:S(2)}, u32[]{:S(2)}) %collective-permute-start.1) | collective-permute-done | bytes 327712 | tf_op jit(solution)/shard_map/ppermute | solution.py:418
  23.5 1.2 dynamic-slice_bitcast_fusion.3
  24.7 1.3 dynamic-slice_bitcast_fusion.1
  26.1 1.9 collective-permute-start.5
  28.1 1.0 pad_maximum_fusion.2
  29.0 1.9 collective-permute-start.2
  31.0 0.5 fusion.1
  31.5 0.3 convolution_convert_fusion
  31.8 1.0 copy.20
  32.8 1.6 reshape.103
  34.4 6.5 %collective-permute-done.2.b2_ref = bf16[2,2,640,128]{3,2,1,0:T(8,128)(2,1)} collective-permute-done((bf16[2,2,640,128]{3,2,1,0:T(8,128)(2,1)}, bf16[2,2,640,128]{3,2,1,0:T(8,128)(2,1)}, u32[]{:S(2)}, u32[]{:S(2)}) %collective-permute-start.2) | collective-permute-done | bytes 655392 | tf_op jit(solution)/shard_map/ppermute | solution.py:418
  41.0 1.9 collective-permute-start.3
  43.0 0.7 reshape.104.count_ref
  43.7 0.6 pad_add_fusion.source_ref
  44.3 9.6 %collective-permute-done.3.b3_ref = bf16[2,2,640,128]{3,2,1,0:T(8,128)(2,1)} collective-permute-done((bf16[2,2,640,128]{3,2,1,0:T(8,128)(2,1)}, bf16[2,2,640,128]{3,2,1,0:T(8,128)(2,1)}, u32[]{:S(2)}, u32[]{:S(2)}) %collective-permute-start.3) | collective-permute-done | bytes 655392 | tf_op jit(solution)/shard_map/ppermute | solution.py:418
  53.8 1.2 copy-done.2
  55.0 5.2 %project_early.1 = (bf16[6,640,256]{2,1,0:T(8,128)(2,1)}, f32[640,128]{1,0:T(8,128)}, f32[2,512,256]{2,1,0:T(8,128)}, f32[2,128,128]{2,1,0:T(8,128)}) custom-call(s32[9]{0:T(128)} %pad_add_fusion.source_ref, bf16[2,640,128]{2,1,0:T(8,128)(2,1)} %copy-done.8, bf16[2,640,128]{2,1,0:T(8,128)(2,1)} %copy-done.7, ...), custom_call_target="tpu_custom_call" | custom-call | tf_op jit(solution)/shard_map/project_early/pallas_call | solution.py:93
  60.2 4.4 %collective-permute-start.7 = (bf16[3,2048,128]{2,1,0:T(8,128)(2,1)}, bf16[3,2048,128]{2,1,0:T(8,128)(2,1)S(1)}, u32[]{:S(2)}, u32[]{:S(2)}) collective-permute-start(bf16[3,2048,128]{2,1,0:T(8,128)(2,1)} %collective-permute-done.6.w0_ref), channel_id=1, source_target_pairs={{0,1},{1,0},{2,3},{3,2},{4,5},{5,4},{6,7},{7,6},{8,9},{9,8},{10,11... | collective-permute-start | bytes 4718600 | tf_op jit(solution)/shard_map/ppermute | solution.py:385
  64.6 1.9 collective-permute-start.4
  66.5 9.9 %collective-permute-done.4.b4_ref = bf16[2,2,640,128]{3,2,1,0:T(8,128)(2,1)S(1)} collective-permute-done((bf16[2,2,640,128]{3,2,1,0:T(8,128)(2,1)}, bf16[2,2,640,128]{3,2,1,0:T(8,128)(2,1)S(1)}, u32[]{:S(2)}, u32[]{:S(2)}) %collective-permute-start.4) | collective-permute-done | bytes 655392 | tf_op jit(solution)/shard_map/ppermute | solution.py:418
  76.5 0.8 copy-done.12
  77.3 0.6 copy-done.6
  77.9 5.7 %project_late.1 = (bf16[2,640,256]{2,1,0:T(8,128)(2,1)}, f32[8,128]{1,0:T(8,128)}, bf16[4,512,128]{2,1,0:T(8,128)(2,1)}, bf16[272,128]{1,0:T(8,128)(2,1)}) custom-call(s32[9]{0:T(128)} %pad_add_fusion.source_ref, bf16[2,2,640,128]{3,2,1,0:T(8,128)(2,1)} %copy-done.12, f32[8,2,2,128]{3,2,1,0:T(2,128)} %bitcast.60, ...), custom_call_target="tpu_custom_call" | custom-call | tf_op jit(solution)/shard_map/project_late/pallas_call | solution.py:139
  83.6 2.0 collective-permute-start.9
  85.6 1.3 slice_bitcast_fusion.w0_ref
  86.9 3.4 %collective-permute-start.16 = (bf16[4096,128]{1,0:T(8,128)(2,1)S(1)}, bf16[4096,128]{1,0:T(8,128)(2,1)}, u32[]{:S(2)}, u32[]{:S(2)}) collective-permute-start(bf16[4096,128]{1,0:T(8,128)(2,1)S(1)} %slice_bitcast_fusion.w0_ref), channel_id=1, source_target_pairs={{0,256},{256,0},{1,257},{257,1},{2,258},{258,2},{3,259},{259,3},{4... | collective-permute-start | bytes 3145736 | tf_op jit(solution)/shard_map/ppermute | solution.py:385
  90.3 1.9 collective-permute-start.8
  92.2 3.6 %project_near.1.keep_ref = f32[2,2,512,128]{3,2,1,0:T(8,128)} custom-call(s32[9]{0:T(128)} %pad_add_fusion.source_ref, bf16[2,640,256]{2,1,0:T(8,128)(2,1)} %get-tuple-element.36.late_ref, bf16[3,2048,128]{2,1,0:T(8,128)(2,1)} %copy-done.1, bf16[3,2048,128]{2,1,0:T(8,128)(2,1)} %copy-done.1, bf16[3,2048,128]{2,1,0:T(8,128)(2,1)} %copy-done.2, ...), custom_call_target="tpu_custom_call" | custom-call | tf_op jit(solution)/shard_map/project_near/pallas_call | solution.py:222
  95.9 25.4 %collective-permute-done.8.other_ref.other_q_ref = bf16[272,128]{1,0:T(8,128)(2,1)S(1)} collective-permute-done((bf16[272,128]{1,0:T(8,128)(2,1)S(1)}, bf16[272,128]{1,0:T(8,128)(2,1)S(1)}, u32[]{:S(2)}, u32[]{:S(2)}) %collective-permute-start.8) | collective-permute-done | bytes 69664 | tf_op jit(solution)/shard_map/ppermute | solution.py:385
  121.3 0.6 copy-done.14
  121.9 0.2 copy-done.13
  122.1 2.3 %finish.1 = (bf16[2,512,128]{2,1,0:T(8,128)(2,1)}, bf16[2,512,128]{2,1,0:T(8,128)(2,1)}) custom-call(f32[2,2,512,128]{3,2,1,0:T(8,128)} %project_near.1.keep_ref, f32[8,128]{1,0:T(8,128)} %get-tuple-element.38.squares_ref, bf16[272,128]{1,0:T(8,128)(2,1)} %copy-done.14, bf16[4,512,128]{2,1,0:T(8,128)(2,1)} %copy-done.13), custom_call_target="tpu_custom_call" | custom-call | tf_op jit(solution)/shard_map/finish/pallas_call | solution.py:249
  124.4 4.7 %collective-permute-start.10 = (bf16[2,512,128]{2,1,0:T(8,128)(2,1)}, bf16[2,512,128]{2,1,0:T(8,128)(2,1)S(1)}, u32[]{:S(2)}, u32[]{:S(2)}) collective-permute-start(bf16[2,512,128]{2,1,0:T(8,128)(2,1)} %get-tuple-element.44), channel_id=1, source_target_pairs={{0,1},{1,0},{2,3},{3,2},{4,5},{5,4},{6,7},{7,6},{8,9},{9,8},{10,11... | collective-permute-start | bytes 786440 | tf_op jit(solution)/shard_map/ppermute | solution.py:385
  129.2 1.4 collective-permute-done.10
  130.5 1.0 pad_maximum_fusion.3.near_ref
  131.5 1.9 collective-permute-start.11
  133.5 4.6 %collective-permute-start.13 = (bf16[2,2,512,128]{3,2,1,0:T(8,128)(2,1)S(1)}, bf16[2,2,512,128]{3,2,1,0:T(8,128)(2,1)S(1)}, u32[]{:S(2)}, u32[]{:S(2)}) collective-permute-start(bf16[2,2,512,128]{3,2,1,0:T(8,128)(2,1)S(1)} %pad_maximum_fusion.3.near_ref), channel_id=1, source_target_pairs={{0,48},{16,0},{32,16},{48,32},{1,49},{17,1},{33,17},{49,33},{2,50}... | collective-permute-start | bytes 1572872 | tf_op jit(solution)/shard_map/ppermute | solution.py:487
  138.0 2.8 %collective-permute-start.15 = (bf16[4096,128]{1,0:T(8,128)(2,1)S(1)}, bf16[4096,128]{1,0:T(8,128)(2,1)}, u32[]{:S(2)}, u32[]{:S(2)}) collective-permute-start(bf16[4096,128]{1,0:T(8,128)(2,1)S(1)} %slice_bitcast_fusion.w0_ref), channel_id=1, source_target_pairs={{0,1},{1,0},{2,3},{3,2},{4,5},{5,4},{6,7},{7,6},{8,9},{9,8},{10,11... | collective-permute-start | bytes 3145736 | tf_op jit(solution)/shard_map/ppermute | solution.py:385
  140.9 1.9 collective-permute-start.17
  142.8 2.8 %finish_queries.1 = bf16[4,2,192,128]{3,2,1,0:T(8,128)(2,1)} custom-call(s32[9]{0:T(128)} %pad_add_fusion.source_ref, bf16[2,640,256]{2,1,0:T(8,128)(2,1)} %get-tuple-element.36.late_ref, bf16[3,2048,128]{2,1,0:T(8,128)(2,1)} %copy-done.1, bf16[3,2048,128]{2,1,0:T(8,128)(2,1)} %copy-done.1, bf16[3,2048,128]{2,1,0:T(8,128)(2,1)} %copy-done.2, ...), custom_call_target="tpu_custom_call" | custom-call | tf_op jit(solution)/shard_map/finish_queries/pallas_call | solution.py:190
  145.7 6.2 %all-to-all-start = ((bf16[8,192,128]{2,1,0:T(8,128)(2,1)}), bf16[8,192,128]{2,1,0:T(8,128)(2,1)S(1)}, u32[]{:S(2)}, u32[]{:S(2)}) async-start(bf16[8,192,128]{2,1,0:T(8,128)(2,1)} %bitcast.50), calls=%async_computation | async-start | bytes 786432 | tf_op jit(solution)/shard_map/all_to_all | solution.py:478
  151.9 1.9 collective-permute-start.12
  153.9 4.6 %collective-permute-start.14 = (bf16[2,512,128]{2,1,0:T(8,128)(2,1)S(1)}, bf16[2,512,128]{2,1,0:T(8,128)(2,1)}, u32[]{:S(2)}, u32[]{:S(2)}) collective-permute-start(bf16[2,512,128]{2,1,0:T(8,128)(2,1)S(1)} %slice_bitcast_fusion.1), channel_id=1, source_target_pairs={{0,48},{16,0},{32,16},{48,32},{1,49},{17,1},{33,17},{49,33},{2,50}... | collective-permute-start | bytes 786440 | tf_op jit(solution)/shard_map/ppermute | solution.py:489
  158.5 0.5 fusion.13.order_ref
  159.0 4.3 %all-to-all-done = bf16[8,192,128]{2,1,0:T(8,128)(2,1)S(1)} async-done(((bf16[8,192,128]{2,1,0:T(8,128)(2,1)}), bf16[8,192,128]{2,1,0:T(8,128)(2,1)S(1)}, u32[]{:S(2)}, u32[]{:S(2)}) %all-to-all-start) | async-done | bytes 393248 | tf_op jit(solution)/shard_map/all_to_all | solution.py:478
  163.5 0.7 reshape.109.count_ref
  164.2 7.6 %attend_near.1 = (f32[1024,128]{1,0:T(8,128)}, f32[1024,128]{1,0:T(8,128)}) custom-call(s32[8]{0:T(128)} %fusion.13.order_ref, bf16[4,2,192,128]{3,2,1,0:T(8,128)(2,1)} %bitcast.47, bf16[2,2,512,128]{3,2,1,0:T(8,128)(2,1)} %copy-done.5, bf16[2,2,512,128]{3,2,1,0:T(8,128)(2,1)} %copy-done.9, bf16[2,2,512,128]{3,2,1,0:T(8,128)(2,1)} %copy-done.10, ...), custom_call_target="tpu_custom_call" | custom-call | tf_op jit(solution)/shard_map/attend_near/pallas_call | solution.py:305
  171.8 5.6 %attend_far.1 = bf16[2,4,2,72,128]{4,3,2,1,0:T(8,128)(2,1)} custom-call(s32[8]{0:T(128)} %fusion.13.order_ref, bf16[4,2,192,128]{3,2,1,0:T(8,128)(2,1)} %bitcast.48, bf16[2,512,128]{2,1,0:T(8,128)(2,1)} %collective-permute-done.12.first_ref, bf16[2,512,128]{2,1,0:T(8,128)(2,1)} %collective-permute-done.14.second_ref, ...), custom_call_target="tpu_custom_call" | custom-call | tf_op jit(solution)/shard_map/attend_far/pallas_call | solution.py:321
  177.4 7.4 %all-to-all-start.1 = ((bf16[16,72,128]{2,1,0:T(8,128)(2,1)}), bf16[16,72,128]{2,1,0:T(8,128)(2,1)S(1)}, u32[]{:S(2)}, u32[]{:S(2)}) async-start(bf16[16,72,128]{2,1,0:T(8,128)(2,1)} %bitcast.52), calls=%async_computation.1 | async-start | bytes 589824 | tf_op jit(solution)/shard_map/all_to_all | solution.py:497
  184.8 12.5 %all-to-all-done.1 = bf16[16,72,128]{2,1,0:T(8,128)(2,1)S(1)} async-done(((bf16[16,72,128]{2,1,0:T(8,128)(2,1)}), bf16[16,72,128]{2,1,0:T(8,128)(2,1)S(1)}, u32[]{:S(2)}, u32[]{:S(2)}) %all-to-all-start.1) | async-done | bytes 294944 | tf_op jit(solution)/shard_map/all_to_all | solution.py:497
  197.4 0.7 copy-done.11
  198.1 5.1 %mix.1 = bf16[32,64,128]{2,1,0:T(8,128)(2,1)} custom-call(s32[1]{0:T(128)} %bitcast.place_ref, bf16[2,4,2,72,128]{4,3,2,1,0:T(8,128)(2,1)} %bitcast.53, bf16[4096,128]{1,0:T(8,128)(2,1)} %copy-done.4, bf16[4096,128]{1,0:T(8,128)(2,1)} %collective-permute-done.15.w1_ref, bf16[4096,128]{1,0:T(8,128)(2,1)} %collective-permute-done.16.w2_ref, ...), custom_call_target="tpu_custom_call" | custom-call | tf_op jit(solution)/shard_map/mix/pallas_call | solution.py:364
  203.2 23.4 %all_to_all.15 = bf16[32,64,128]{2,1,0:T(8,128)(2,1)S(1)} all-to-all(bf16[32,64,128]{2,1,0:T(8,128)(2,1)} %mix.1), channel_id=1, replica_groups=mesh['s'=2,'zh'=4,'x'=4,'y'=8,'c'=2] {'s','y','c'}, dimensions={0} | all-to-all | bytes 1048576 | tf_op jit(solution)/shard_map/all_to_all | solution.py:501
  226.6 0.7 reduce_sum.22
  (58 shorter events, 0.7 us)
Async XLA Ops:
  0.0 10.6 %copy-start = (f32[2,4096]{1,0:T(2,128)S(1)}, f32[2,4096]{1,0:T(2,128)}, u32[]{:S(2)}) copy-start(f32[2,4096]{1,0:T(2,128)} %param.12) | copy-start | bytes 98308
  1.8 10.2 %collective-permute-start = (bf16[640,128]{1,0:T(8,128)(2,1)S(1)}, bf16[640,128]{1,0:T(8,128)(2,1)S(1)}, u32[]{:S(2)}, u32[]{:S(2)}) collective-permute-start(bf16[640,128]{1,0:T(8,128)(2,1)S(1)} %pad_maximum_fusion.5), channel_id=1, source_target_pairs={{0,1},{1,0},{2,3},{3,2},{4,5},{5,4},{6,7},{7,6},{8,9},{9,8},{10,11... | collective-permute-start | bytes 491528 | tf_op jit(solution)/shard_map/ppermute | solution.py:385
  14.4 5.2 %copy-start.8 = (bf16[2,640,128]{2,1,0:T(8,128)(2,1)}, bf16[2,640,128]{2,1,0:T(8,128)(2,1)S(1)}, u32[]{:S(2)}) copy-start(bf16[2,640,128]{2,1,0:T(8,128)(2,1)S(1)} %maximum_select_fusion.1.b0_ref) | copy-start | bytes 983044
  14.4 9.0 %collective-permute-start.1 = (bf16[2,640,128]{2,1,0:T(8,128)(2,1)S(1)}, bf16[2,640,128]{2,1,0:T(8,128)(2,1)S(1)}, u32[]{:S(2)}, u32[]{:S(2)}) collective-permute-start(bf16[2,640,128]{2,1,0:T(8,128)(2,1)S(1)} %maximum_select_fusion.1.b0_ref), channel_id=1, source_target_pairs={{0,2},{1,15},{2,0},{3,5},{4,6},{5,3},{6,4},{7,9},{8,10},{9,7},{10,... | collective-permute-start | bytes 983048 | tf_op jit(solution)/shard_map/ppermute | solution.py:418
  17.7 42.5 %collective-permute-start.6 = (bf16[3,2048,128]{2,1,0:T(8,128)(2,1)}, bf16[3,2048,128]{2,1,0:T(8,128)(2,1)}, u32[]{:S(2)}, u32[]{:S(2)}) collective-permute-start(bf16[3,2048,128]{2,1,0:T(8,128)(2,1)} %pad_maximum_fusion.1), channel_id=1, source_target_pairs={{0,256},{256,0},{1,257},{257,1},{2,258},{258,2},{3,259},{259,3},{4... | collective-permute-start | bytes 4718600 | tf_op jit(solution)/shard_map/ppermute | solution.py:385
  23.5 4.6 %copy-start.7 = (bf16[2,640,128]{2,1,0:T(8,128)(2,1)}, bf16[2,640,128]{2,1,0:T(8,128)(2,1)S(1)}, u32[]{:S(2)}) copy-start(bf16[2,640,128]{2,1,0:T(8,128)(2,1)S(1)} %collective-permute-done.1.b1_ref) | copy-start | bytes 983044
  26.0 5.0 %copy-start.15 = (s32[8,128]{1,0:T(8,128)S(1)}, s32[8,128]{1,0:T(8,128)}, u32[]{:S(2)}) copy-start(s32[8,128]{1,0:T(8,128)} %param.9) | copy-start | bytes 12292
  26.1 6.7 %copy-start.1 = (bf16[3,2048,128]{2,1,0:T(8,128)(2,1)}, bf16[3,2048,128]{2,1,0:T(8,128)(2,1)S(1)}, u32[]{:S(2)}) copy-start(bf16[3,2048,128]{2,1,0:T(8,128)(2,1)S(1)} %pad_maximum_fusion.w0_ref.w00_ref.w01_ref) | copy-start | bytes 4718596
  26.1 27.7 %collective-permute-start.5 = (bf16[3,2048,128]{2,1,0:T(8,128)(2,1)S(1)}, bf16[3,2048,128]{2,1,0:T(8,128)(2,1)S(1)}, u32[]{:S(2)}, u32[]{:S(2)}) collective-permute-start(bf16[3,2048,128]{2,1,0:T(8,128)(2,1)S(1)} %pad_maximum_fusion.w0_ref.w00_ref.w01_ref), channel_id=1, source_target_pairs={{0,1},{1,0},{2,3},{3,2},{4,5},{5,4},{6,7},{7,6},{8,9},{9,8},{10,11... | collective-permute-start | bytes 4718600 | tf_op jit(solution)/shard_map/ppermute | solution.py:385
  29.0 11.9 %collective-permute-start.2 = (bf16[2,2,640,128]{3,2,1,0:T(8,128)(2,1)}, bf16[2,2,640,128]{3,2,1,0:T(8,128)(2,1)}, u32[]{:S(2)}, u32[]{:S(2)}) collective-permute-start(bf16[2,2,640,128]{3,2,1,0:T(8,128)(2,1)} %pad_maximum_fusion.2), channel_id=1, source_target_pairs={{0,14},{1,3},{2,4},{3,1},{4,2},{5,7},{6,8},{7,5},{8,6},{9,11},{10,... | collective-permute-start | bytes 1966088 | tf_op jit(solution)/shard_map/ppermute | solution.py:418
  31.0 12.7 %copy-start.17 = (s32[8]{0:T(128)S(1)}, s32[8]{0:T(128)}, u32[]{:S(2)}) copy-start(s32[8]{0:T(128)} %constant.129.clone) | copy-start | bytes 100
  41.0 12.8 %collective-permute-start.3 = (bf16[2,2,640,128]{3,2,1,0:T(8,128)(2,1)}, bf16[2,2,640,128]{3,2,1,0:T(8,128)(2,1)}, u32[]{:S(2)}, u32[]{:S(2)}) collective-permute-start(bf16[2,2,640,128]{3,2,1,0:T(8,128)(2,1)} %collective-permute-done.2.b2_ref), channel_id=1, source_target_pairs={{0,2},{1,15},{2,0},{3,5},{4,6},{5,3},{6,4},{7,9},{8,10},{9,7},{10,... | collective-permute-start | bytes 1966088 | tf_op jit(solution)/shard_map/ppermute | solution.py:418
  53.8 1.2 copy-start.2
  60.2 16.2 %collective-permute-start.7 = (bf16[3,2048,128]{2,1,0:T(8,128)(2,1)}, bf16[3,2048,128]{2,1,0:T(8,128)(2,1)S(1)}, u32[]{:S(2)}, u32[]{:S(2)}) collective-permute-start(bf16[3,2048,128]{2,1,0:T(8,128)(2,1)} %collective-permute-done.6.w0_ref), channel_id=1, source_target_pairs={{0,1},{1,0},{2,3},{3,2},{4,5},{5,4},{6,7},{7,6},{8,9},{9,8},{10,11... | collective-permute-start | bytes 4718600 | tf_op jit(solution)/shard_map/ppermute | solution.py:385
  64.6 11.8 %collective-permute-start.4 = (bf16[2,2,640,128]{3,2,1,0:T(8,128)(2,1)}, bf16[2,2,640,128]{3,2,1,0:T(8,128)(2,1)S(1)}, u32[]{:S(2)}, u32[]{:S(2)}) collective-permute-start(bf16[2,2,640,128]{3,2,1,0:T(8,128)(2,1)} %collective-permute-done.3.b3_ref), channel_id=1, source_target_pairs={{0,14},{1,3},{2,4},{3,1},{4,2},{5,7},{6,8},{7,5},{8,6},{9,11},{10,... | collective-permute-start | bytes 1966088 | tf_op jit(solution)/shard_map/ppermute | solution.py:418
  76.4 0.8 copy-start.12
  76.5 1.4 copy-start.6
  83.6 6.7 %copy-start.18 = (bf16[272,128]{1,0:T(8,128)(2,1)S(1)}, bf16[272,128]{1,0:T(8,128)(2,1)}, u32[]{:S(2)}) copy-start(bf16[272,128]{1,0:T(8,128)(2,1)} %get-tuple-element.39) | copy-start | bytes 208900
  83.6 37.7 %collective-permute-start.9 = (bf16[4,512,128]{2,1,0:T(8,128)(2,1)}, bf16[4,512,128]{2,1,0:T(8,128)(2,1)S(1)}, u32[]{:S(2)}, u32[]{:S(2)}) collective-permute-start(bf16[4,512,128]{2,1,0:T(8,128)(2,1)} %get-tuple-element.42), channel_id=1, source_target_pairs={{0,256},{256,0},{1,257},{257,1},{2,258},{258,2},{3,259},{259,3},{4... | collective-permute-start | bytes 1572872 | tf_op jit(solution)/shard_map/ppermute | solution.py:385
  86.9 51.1 %copy-start.4 = (bf16[4096,128]{1,0:T(8,128)(2,1)}, bf16[4096,128]{1,0:T(8,128)(2,1)S(1)}, u32[]{:S(2)}) copy-start(bf16[4096,128]{1,0:T(8,128)(2,1)S(1)} %slice_bitcast_fusion.w0_ref) | copy-start | bytes 3145732
  86.9 54.0 %collective-permute-start.16 = (bf16[4096,128]{1,0:T(8,128)(2,1)S(1)}, bf16[4096,128]{1,0:T(8,128)(2,1)}, u32[]{:S(2)}, u32[]{:S(2)}) collective-permute-start(bf16[4096,128]{1,0:T(8,128)(2,1)S(1)} %slice_bitcast_fusion.w0_ref), channel_id=1, source_target_pairs={{0,256},{256,0},{1,257},{257,1},{2,258},{258,2},{3,259},{259,3},{4... | collective-permute-start | bytes 3145736 | tf_op jit(solution)/shard_map/ppermute | solution.py:385
  90.3 31.0 %collective-permute-start.8 = (bf16[272,128]{1,0:T(8,128)(2,1)S(1)}, bf16[272,128]{1,0:T(8,128)(2,1)S(1)}, u32[]{:S(2)}, u32[]{:S(2)}) collective-permute-start(bf16[272,128]{1,0:T(8,128)(2,1)S(1)} %copy-done.18), channel_id=1, source_target_pairs={{0,256},{256,0},{1,257},{257,1},{2,258},{258,2},{3,259},{259,3},{4... | collective-permute-start | bytes 208904 | tf_op jit(solution)/shard_map/ppermute | solution.py:385
  121.3 0.6 copy-start.14
  121.3 0.8 copy-start.13
  124.4 6.1 %collective-permute-start.10 = (bf16[2,512,128]{2,1,0:T(8,128)(2,1)}, bf16[2,512,128]{2,1,0:T(8,128)(2,1)S(1)}, u32[]{:S(2)}, u32[]{:S(2)}) collective-permute-start(bf16[2,512,128]{2,1,0:T(8,128)(2,1)} %get-tuple-element.44), channel_id=1, source_target_pairs={{0,1},{1,0},{2,3},{3,2},{4,5},{5,4},{6,7},{7,6},{8,9},{9,8},{10,11... | collective-permute-start | bytes 786440 | tf_op jit(solution)/shard_map/ppermute | solution.py:385
  131.5 14.1 %copy-start.5 = (bf16[2,2,512,128]{3,2,1,0:T(8,128)(2,1)}, bf16[2,2,512,128]{3,2,1,0:T(8,128)(2,1)S(1)}, u32[]{:S(2)}) copy-start(bf16[2,2,512,128]{3,2,1,0:T(8,128)(2,1)S(1)} %pad_maximum_fusion.3.near_ref) | copy-start | bytes 1572868
  131.5 20.3 %collective-permute-start.11 = (bf16[2,2,512,128]{3,2,1,0:T(8,128)(2,1)S(1)}, bf16[2,2,512,128]{3,2,1,0:T(8,128)(2,1)S(1)}, u32[]{:S(2)}, u32[]{:S(2)}) collective-permute-start(bf16[2,2,512,128]{3,2,1,0:T(8,128)(2,1)S(1)} %pad_maximum_fusion.3.near_ref), channel_id=1, source_target_pairs={{0,16},{16,32},{32,48},{48,0},{1,17},{17,33},{33,49},{49,1},{2,18}... | collective-permute-start | bytes 1572872 | tf_op jit(solution)/shard_map/ppermute | solution.py:486
  133.5 20.4 %collective-permute-start.13 = (bf16[2,2,512,128]{3,2,1,0:T(8,128)(2,1)S(1)}, bf16[2,2,512,128]{3,2,1,0:T(8,128)(2,1)S(1)}, u32[]{:S(2)}, u32[]{:S(2)}) collective-permute-start(bf16[2,2,512,128]{3,2,1,0:T(8,128)(2,1)S(1)} %pad_maximum_fusion.3.near_ref), channel_id=1, source_target_pairs={{0,48},{16,0},{32,16},{48,32},{1,49},{17,1},{33,17},{49,33},{2,50}... | collective-permute-start | bytes 1572872 | tf_op jit(solution)/shard_map/ppermute | solution.py:487
  138.0 46.8 %collective-permute-start.15 = (bf16[4096,128]{1,0:T(8,128)(2,1)S(1)}, bf16[4096,128]{1,0:T(8,128)(2,1)}, u32[]{:S(2)}, u32[]{:S(2)}) collective-permute-start(bf16[4096,128]{1,0:T(8,128)(2,1)S(1)} %slice_bitcast_fusion.w0_ref), channel_id=1, source_target_pairs={{0,1},{1,0},{2,3},{3,2},{4,5},{5,4},{6,7},{7,6},{8,9},{9,8},{10,11... | collective-permute-start | bytes 3145736 | tf_op jit(solution)/shard_map/ppermute | solution.py:385
  140.9 43.9 %collective-permute-start.17 = (bf16[4096,128]{1,0:T(8,128)(2,1)}, bf16[4096,128]{1,0:T(8,128)(2,1)}, u32[]{:S(2)}, u32[]{:S(2)}) collective-permute-start(bf16[4096,128]{1,0:T(8,128)(2,1)} %collective-permute-done.16.w2_ref), channel_id=1, source_target_pairs={{0,1},{1,0},{2,3},{3,2},{4,5},{5,4},{6,7},{7,6},{8,9},{9,8},{10,11... | collective-permute-start | bytes 3145736 | tf_op jit(solution)/shard_map/ppermute | solution.py:385
  145.7 12.8 %copy-start.16 = (s32[8]{0:T(128)S(1)}, s32[8]{0:T(128)}, u32[]{:S(2)}) copy-start(s32[8]{0:T(128)} %constant.130.clone) | copy-start | bytes 100
  145.7 17.6 %all-to-all-start = ((bf16[8,192,128]{2,1,0:T(8,128)(2,1)}), bf16[8,192,128]{2,1,0:T(8,128)(2,1)S(1)}, u32[]{:S(2)}, u32[]{:S(2)}) async-start(bf16[8,192,128]{2,1,0:T(8,128)(2,1)} %bitcast.50), calls=%async_computation | async-start | bytes 786432 | tf_op jit(solution)/shard_map/all_to_all | solution.py:478
  151.9 12.3 %copy-start.9 = (bf16[2,2,512,128]{3,2,1,0:T(8,128)(2,1)}, bf16[2,2,512,128]{3,2,1,0:T(8,128)(2,1)S(1)}, u32[]{:S(2)}) copy-start(bf16[2,2,512,128]{3,2,1,0:T(8,128)(2,1)S(1)} %collective-permute-done.11.up_ref) | copy-start | bytes 1572868
  151.9 19.9 %collective-permute-start.12 = (bf16[2,512,128]{2,1,0:T(8,128)(2,1)S(1)}, bf16[2,512,128]{2,1,0:T(8,128)(2,1)}, u32[]{:S(2)}, u32[]{:S(2)}) collective-permute-start(bf16[2,512,128]{2,1,0:T(8,128)(2,1)S(1)} %slice_bitcast_fusion.2), channel_id=1, source_target_pairs={{0,16},{16,32},{32,48},{48,0},{1,17},{17,33},{33,49},{49,1},{2,18}... | collective-permute-start | bytes 786440 | tf_op jit(solution)/shard_map/ppermute | solution.py:488
  153.8 10.4 %copy-start.10 = (bf16[2,2,512,128]{3,2,1,0:T(8,128)(2,1)}, bf16[2,2,512,128]{3,2,1,0:T(8,128)(2,1)S(1)}, u32[]{:S(2)}) copy-start(bf16[2,2,512,128]{3,2,1,0:T(8,128)(2,1)S(1)} %collective-permute-done.13.down_ref) | copy-start | bytes 1572868
  153.9 17.9 %collective-permute-start.14 = (bf16[2,512,128]{2,1,0:T(8,128)(2,1)S(1)}, bf16[2,512,128]{2,1,0:T(8,128)(2,1)}, u32[]{:S(2)}, u32[]{:S(2)}) collective-permute-start(bf16[2,512,128]{2,1,0:T(8,128)(2,1)S(1)} %slice_bitcast_fusion.1), channel_id=1, source_target_pairs={{0,48},{16,0},{32,16},{48,32},{1,49},{17,1},{33,17},{49,33},{2,50}... | collective-permute-start | bytes 786440 | tf_op jit(solution)/shard_map/ppermute | solution.py:489
  163.3 0.9 copy-start.3
  177.4 20.0 %all-to-all-start.1 = ((bf16[16,72,128]{2,1,0:T(8,128)(2,1)}), bf16[16,72,128]{2,1,0:T(8,128)(2,1)S(1)}, u32[]{:S(2)}, u32[]{:S(2)}) async-start(bf16[16,72,128]{2,1,0:T(8,128)(2,1)} %bitcast.52), calls=%async_computation.1 | async-start | bytes 589824 | tf_op jit(solution)/shard_map/all_to_all | solution.py:497
  197.4 0.7 copy-start.11

commit v6 on v5

--- a/solution.py
+++ b/solution.py
@@ -281,9 +281,9 @@
     total_ref[...] = jnp.broadcast_to(total, (4 * SPAN, 128))
 
 
-def far_attend_kernel(order_ref, q_ref, first_ref, second_ref, count_ref, part_ref, total_ref, out_ref, expo_ref):
+def far_attend_kernel(order_ref, q_ref, far_ref, count_ref, part_ref, total_ref, out_ref, expo_ref):
     queries = jnp.concatenate([q_ref[0, 0], q_ref[0, 1]], axis=0)
-    part, total = partial(order_ref, 6, queries, [first_ref, second_ref], count_ref, expo_ref)
+    part, total = partial(order_ref, 6, queries, [far_ref.at[0], far_ref.at[1]], count_ref, expo_ref)
     before = total_ref[:, 0:1]
     both = total + before
     inverse = jnp.where(both > 0.0, 1.0 / both, 0.0)
@@ -316,20 +316,20 @@
     )(order, queries, near, up, down, counts)
 
 
-def attend_far(order, queries, first, second, counts, part, total):
-    half = pl.BlockSpec((2, HALF, HEAD_DIM), lambda i, *_: (0, 0, 0))
+def attend_far(order, queries, far, counts, part, total):
+    block = pl.BlockSpec((2, 2, HALF, HEAD_DIM), lambda i, *_: (0, 0, 0, 0))
     return pl.pallas_call(
         far_attend_kernel,
         grid_spec=pltpu.PrefetchScalarGridSpec(
             num_scalar_prefetch=1,
             grid=(4,),
-            in_specs=[QUERY_SPEC, half, half, COUNT_SPEC, PART_SPEC, PART_SPEC],
+            in_specs=[QUERY_SPEC, block, COUNT_SPEC, PART_SPEC, PART_SPEC],
             out_specs=pl.BlockSpec((2, 1, 2, ROWS, HEAD_DIM), lambda i, *_: (0, i, 0, 0, 0)),
             scratch_shapes=[pltpu.VMEM((4 * SPAN, 2 * HALF), F32)],
         ),
         out_shape=jax.ShapeDtypeStruct((2, 4, 2, ROWS, HEAD_DIM), BF16),
         name="attend_far",
-    )(order, queries, first, second, counts, part, total)
+    )(order, queries, far, counts, part, total)
 
 
 def merge(parts):
@@ -430,8 +430,9 @@
 
 
 def block_order(column, core):
-    offsets = jnp.array([0, 0, -1, -1, 1, 1, 2, 2], jnp.int32)
-    origin = (column + offsets) % 4
+    sign = 1 - 2 * ((column + core) % 2)
+    offsets = jnp.array([0, 0, 1, 1, -1, -1, -2, -2], jnp.int32)
+    origin = (column + sign * offsets) % 4
     half = (core + jnp.arange(8)) % 2
     return (2 * origin + half).astype(jnp.int32)
 
@@ -481,18 +482,15 @@
     order = block_order(column, core)
     wo_diagonal = swap(wo_section, "c")
     near = jnp.stack([near, swap(give, "c")])
-    ahead = [(i, (i + 1) % 4) for i in range(4)]
-    back = [(i, (i - 1) % 4) for i in range(4)]
-    up = lax.ppermute(near, "x", ahead)
-    down = lax.ppermute(near, "x", back)
-    up_far = lax.ppermute(up[0], "x", ahead)
-    down_far = lax.ppermute(down[1], "x", back)
+    following = exchange(near, "x", 4, 0)
+    preceding = exchange(near, "x", 4, 1)
+    beyond = exchange(following, "x", 4, 1)
     queries = queries.reshape(4, 2, 192, 128)
     counts = queries[:, :, 128:].reshape(4, 2, 2, 8, HALF).transpose(0, 3, 1, 2, 4)
     counts = counts.reshape(4, 8, 4, HALF)
 
-    part, total = attend_near(order, queries, near, up, down, counts)
-    parts = attend_far(order, queries, up_far, down_far, counts, part, total)
+    part, total = attend_near(order, queries, near, following, preceding, counts)
+    parts = attend_far(order, queries, beyond, counts, part, total)
     parts = parts.reshape(16, ROWS, HEAD_DIM)
     parts = lax.all_to_all(parts, ("s", "zh", "c"), 0, 0)
     place = (section * 2 + core).astype(jnp.int32).reshape(1)

time: 229 us -> 222 us (0.969)
  waiting for transfers between devices: 73.4 us -> 68.8 us
  starting transfers between devices: 68 us -> 65.5 us
    ppermute x4 -> x0, starting transfers between devices: 13 us -> none  [the longest x1 4.57 us: step(): down_far = lax.ppermute(down[1], 'x', back)]
    ppermute x4 -> x7, starting transfers between devices: 7.66 us -> 14.9 us  [exchange(): return lax.ppermute(value, (axis, 'c'), pairs(size, turn))]
    all_to_all x1, waiting for transfers between devices: 4.29 us -> 0.01 us  [step(): queries = lax.all_to_all(queries, ('zh', 'c'), 0, 0)]
    ppermute x4 -> x7, waiting for transfers between devices: 29.8 us -> 29.7 us  [exchange(): return lax.ppermute(value, (axis, 'c'), pairs(size, turn))]
  transfers between devices with their start and end apart: 20 -> 19, of which waited for: 8 -> 7; matrix products, arithmetic and copies ran while one was open for 7% -> 7% of each run, Pallas kernels for 12% -> 12%
where the time goes in v6:
time: 222 us; the launch traced here: 220 us
  waiting for transfers between devices  68.8 us (31%)
  starting transfers between devices  65.5 us (30%)
  Pallas kernels  38.1 us (17%)
  blocking collectives  23.3 us (10%)
  local copies, waits for them, and re-layouts  17.1 us (8%)
  other arithmetic  6.24 us (3%)
    ppermute x10, starting transfers between devices, swap(): return lax.ppermute(value, axis, [(0, 1), (1, 0)])  34.8 us
    ppermute x7, waiting for transfers between devices, exchange(): return lax.ppermute(value, (axis, 'c'), pairs(size, turn))  29.7 us
    ppermute x10, waiting for transfers between devices, swap(): return lax.ppermute(value, axis, [(0, 1), (1, 0)])  26.6 us
    all_to_all x1, blocking collectives, step(): out = lax.all_to_all(out, ('s', 'y', 'c'), 0, 0)  23.3 us
    ppermute x7, starting transfers between devices, exchange(): return lax.ppermute(value, (axis, 'c'), pairs(size, turn))  14.9 us
    all_to_all x1, waiting for transfers between devices, step(): parts = lax.all_to_all(parts, ('s', 'zh', 'c'), 0, 0)  12.5 us
    all_to_all x1, starting transfers between devices, step(): queries = lax.all_to_all(queries, ('zh', 'c'), 0, 0)  8.17 us
    all_to_all x1, starting transfers between devices, step(): parts = lax.all_to_all(parts, ('s', 'zh', 'c'), 0, 0)  7.71 us
  transfers between devices with their start and end apart: 19, of which 7 were waited for; matrix products, arithmetic and copies ran while one was open for 7% of the time, Pallas kernels for 12%

profile of v6, /device:TPU:1, one launch (start us, length us, event | category | flops | bytes accessed | tf_op | source)
XLA Modules:
  0.0 220.4 jit_solution(2107619471052255299)
XLA Ops:
  0.0 0.8 constant_dynamic-slice_fusion.3
  0.8 1.0 constant_dynamic-slice_fusion.4
  1.8 8.7 %collective-permute-start = (bf16[640,128]{1,0:T(8,128)(2,1)S(1)}, bf16[640,128]{1,0:T(8,128)(2,1)S(1)}, u32[]{:S(2)}, u32[]{:S(2)}) collective-permute-start(bf16[640,128]{1,0:T(8,128)(2,1)S(1)} %pad_maximum_fusion.5), channel_id=1, source_target_pairs={{0,1},{1,0},{2,3},{3,2},{4,5},{5,4},{6,7},{7,6},{8,9},{9,8},{10,11... | collective-permute-start | bytes 491528 | tf_op jit(solution)/shard_map/ppermute | solution.py:385
  10.6 0.6 constant_dynamic-slice_fusion
  11.2 0.8 convert_reduce_fusion
  12.0 1.1 dynamic-slice_bitcast_fusion.2
  13.1 1.3 dynamic-slice_bitcast_fusion
  14.4 1.9 collective-permute-start.1
  16.4 1.4 pad_maximum_fusion.1
  17.7 1.9 collective-permute-start.6
  19.7 3.7 %collective-permute-done.1.b1_ref = bf16[2,640,128]{2,1,0:T(8,128)(2,1)S(1)} collective-permute-done((bf16[2,640,128]{2,1,0:T(8,128)(2,1)S(1)}, bf16[2,640,128]{2,1,0:T(8,128)(2,1)S(1)}, u32[]{:S(2)}, u32[]{:S(2)}) %collective-permute-start.1) | collective-permute-done | bytes 327712 | tf_op jit(solution)/shard_map/ppermute | solution.py:418
  23.5 1.2 dynamic-slice_bitcast_fusion.3
  24.7 1.3 dynamic-slice_bitcast_fusion.1
  26.0 0.1 pad_maximum_fusion.w0_ref.w00_ref.w01_ref
  26.1 1.9 collective-permute-start.5
  28.1 1.0 pad_maximum_fusion.2
  29.0 1.9 collective-permute-start.2
  31.0 0.5 fusion.1
  31.5 0.3 convolution_convert_fusion
  31.8 1.0 copy.20
  32.8 1.6 reshape.103
  34.4 6.5 %collective-permute-done.2.b2_ref = bf16[2,2,640,128]{3,2,1,0:T(8,128)(2,1)} collective-permute-done((bf16[2,2,640,128]{3,2,1,0:T(8,128)(2,1)}, bf16[2,2,640,128]{3,2,1,0:T(8,128)(2,1)}, u32[]{:S(2)}, u32[]{:S(2)}) %collective-permute-start.2) | collective-permute-done | bytes 655392 | tf_op jit(solution)/shard_map/ppermute | solution.py:418
  41.0 1.9 collective-permute-start.3
  43.0 0.7 reshape.104.count_ref
  43.7 0.6 pad_add_fusion.source_ref
  44.3 9.5 %collective-permute-done.3.b3_ref = bf16[2,2,640,128]{3,2,1,0:T(8,128)(2,1)} collective-permute-done((bf16[2,2,640,128]{3,2,1,0:T(8,128)(2,1)}, bf16[2,2,640,128]{3,2,1,0:T(8,128)(2,1)}, u32[]{:S(2)}, u32[]{:S(2)}) %collective-permute-start.3) | collective-permute-done | bytes 655392 | tf_op jit(solution)/shard_map/ppermute | solution.py:418
  53.8 1.2 copy-done.2
  55.0 5.2 %project_early.1 = (bf16[6,640,256]{2,1,0:T(8,128)(2,1)}, f32[640,128]{1,0:T(8,128)}, f32[2,512,256]{2,1,0:T(8,128)}, f32[2,128,128]{2,1,0:T(8,128)}) custom-call(s32[9]{0:T(128)} %pad_add_fusion.source_ref, bf16[2,640,128]{2,1,0:T(8,128)(2,1)} %copy-done.8, bf16[2,640,128]{2,1,0:T(8,128)(2,1)} %copy-done.7, ...), custom_call_target="tpu_custom_call" | custom-call | tf_op jit(solution)/shard_map/project_early/pallas_call | solution.py:93
  60.2 4.4 %collective-permute-start.7 = (bf16[3,2048,128]{2,1,0:T(8,128)(2,1)}, bf16[3,2048,128]{2,1,0:T(8,128)(2,1)S(1)}, u32[]{:S(2)}, u32[]{:S(2)}) collective-permute-start(bf16[3,2048,128]{2,1,0:T(8,128)(2,1)} %collective-permute-done.6.w0_ref), channel_id=1, source_target_pairs={{0,1},{1,0},{2,3},{3,2},{4,5},{5,4},{6,7},{7,6},{8,9},{9,8},{10,11... | collective-permute-start | bytes 4718600 | tf_op jit(solution)/shard_map/ppermute | solution.py:385
  64.6 1.9 collective-permute-start.4
  66.5 9.9 %collective-permute-done.4.b4_ref = bf16[2,2,640,128]{3,2,1,0:T(8,128)(2,1)S(1)} collective-permute-done((bf16[2,2,640,128]{3,2,1,0:T(8,128)(2,1)}, bf16[2,2,640,128]{3,2,1,0:T(8,128)(2,1)S(1)}, u32[]{:S(2)}, u32[]{:S(2)}) %collective-permute-start.4) | collective-permute-done | bytes 655392 | tf_op jit(solution)/shard_map/ppermute | solution.py:418
  76.4 0.8 copy-done.11
  77.3 0.6 copy-done.6
  77.9 5.7 %project_late.1 = (bf16[2,640,256]{2,1,0:T(8,128)(2,1)}, f32[8,128]{1,0:T(8,128)}, bf16[4,512,128]{2,1,0:T(8,128)(2,1)}, bf16[272,128]{1,0:T(8,128)(2,1)}) custom-call(s32[9]{0:T(128)} %pad_add_fusion.source_ref, bf16[2,2,640,128]{3,2,1,0:T(8,128)(2,1)} %copy-done.11, f32[8,2,2,128]{3,2,1,0:T(2,128)} %bitcast.56, ...), custom_call_target="tpu_custom_call" | custom-call | tf_op jit(solution)/shard_map/project_late/pallas_call | solution.py:139
  83.6 2.0 collective-permute-start.9
  85.6 1.3 slice_bitcast_fusion.w0_ref
  86.9 3.4 %collective-permute-start.15 = (bf16[4096,128]{1,0:T(8,128)(2,1)S(1)}, bf16[4096,128]{1,0:T(8,128)(2,1)S(1)}, u32[]{:S(2)}, u32[]{:S(2)}) collective-permute-start(bf16[4096,128]{1,0:T(8,128)(2,1)S(1)} %slice_bitcast_fusion.w0_ref), channel_id=1, source_target_pairs={{0,256},{256,0},{1,257},{257,1},{2,258},{258,2},{3,259},{259,3},{4... | collective-permute-start | bytes 3145736 | tf_op jit(solution)/shard_map/ppermute | solution.py:385
  90.3 1.9 collective-permute-start.8
  92.2 3.7 %project_near.1.keep_ref = f32[2,2,512,128]{3,2,1,0:T(8,128)} custom-call(s32[9]{0:T(128)} %pad_add_fusion.source_ref, bf16[2,640,256]{2,1,0:T(8,128)(2,1)} %get-tuple-element.36.late_ref, bf16[3,2048,128]{2,1,0:T(8,128)(2,1)} %copy-done.1, bf16[3,2048,128]{2,1,0:T(8,128)(2,1)} %copy-done.1, bf16[3,2048,128]{2,1,0:T(8,128)(2,1)} %copy-done.2, ...), custom_call_target="tpu_custom_call" | custom-call | tf_op jit(solution)/shard_map/project_near/pallas_call | solution.py:222
  95.9 25.3 %collective-permute-done.8.other_ref.other_q_ref = bf16[272,128]{1,0:T(8,128)(2,1)S(1)} collective-permute-done((bf16[272,128]{1,0:T(8,128)(2,1)S(1)}, bf16[272,128]{1,0:T(8,128)(2,1)S(1)}, u32[]{:S(2)}, u32[]{:S(2)}) %collective-permute-start.8) | collective-permute-done | bytes 69664 | tf_op jit(solution)/shard_map/ppermute | solution.py:385
  121.2 0.6 copy-done.13
  121.8 0.2 copy-done.12
  122.0 2.4 %finish.1 = (bf16[2,512,128]{2,1,0:T(8,128)(2,1)}, bf16[2,512,128]{2,1,0:T(8,128)(2,1)}) custom-call(f32[2,2,512,128]{3,2,1,0:T(8,128)} %project_near.1.keep_ref, f32[8,128]{1,0:T(8,128)} %get-tuple-element.38.squares_ref, bf16[272,128]{1,0:T(8,128)(2,1)} %copy-done.13, bf16[4,512,128]{2,1,0:T(8,128)(2,1)} %copy-done.12), custom_call_target="tpu_custom_call" | custom-call | tf_op jit(solution)/shard_map/finish/pallas_call | solution.py:249
  124.4 4.8 %collective-permute-start.10 = (bf16[2,512,128]{2,1,0:T(8,128)(2,1)}, bf16[2,512,128]{2,1,0:T(8,128)(2,1)S(1)}, u32[]{:S(2)}, u32[]{:S(2)}) collective-permute-start(bf16[2,512,128]{2,1,0:T(8,128)(2,1)} %get-tuple-element.44), channel_id=1, source_target_pairs={{0,1},{1,0},{2,3},{3,2},{4,5},{5,4},{6,7},{7,6},{8,9},{9,8},{10,11... | collective-permute-start | bytes 786440 | tf_op jit(solution)/shard_map/ppermute | solution.py:385
  129.2 1.4 collective-permute-done.10
  130.6 1.0 pad_maximum_fusion.3.near_ref
  131.6 1.9 collective-permute-start.11
  133.5 2.9 %finish_queries.1 = bf16[4,2,192,128]{3,2,1,0:T(8,128)(2,1)} custom-call(s32[9]{0:T(128)} %pad_add_fusion.source_ref, bf16[2,640,256]{2,1,0:T(8,128)(2,1)} %get-tuple-element.36.late_ref, bf16[3,2048,128]{2,1,0:T(8,128)(2,1)} %copy-done.1, bf16[3,2048,128]{2,1,0:T(8,128)(2,1)} %copy-done.1, bf16[3,2048,128]{2,1,0:T(8,128)(2,1)} %copy-done.2, ...), custom_call_target="tpu_custom_call" | custom-call | tf_op jit(solution)/shard_map/finish_queries/pallas_call | solution.py:190
  136.4 8.2 %all-to-all-start = ((bf16[8,192,128]{2,1,0:T(8,128)(2,1)}), bf16[8,192,128]{2,1,0:T(8,128)(2,1)S(1)}, u32[]{:S(2)}, u32[]{:S(2)}) async-start(bf16[8,192,128]{2,1,0:T(8,128)(2,1)} %bitcast.46), calls=%async_computation | async-start | bytes 786432 | tf_op jit(solution)/shard_map/all_to_all | solution.py:479
  144.6 1.9 collective-permute-start.13
  146.5 3.4 %collective-permute-start.12 = (bf16[2,2,512,128]{3,2,1,0:T(8,128)(2,1)}, bf16[2,2,512,128]{3,2,1,0:T(8,128)(2,1)}, u32[]{:S(2)}, u32[]{:S(2)}) collective-permute-start(bf16[2,2,512,128]{3,2,1,0:T(8,128)(2,1)} %collective-permute-done.11.up_ref), channel_id=1, source_target_pairs={{0,48},{1,17},{16,32},{17,1},{32,16},{33,49},{48,0},{49,33},{2,50}... | collective-permute-start | bytes 1572872 | tf_op jit(solution)/shard_map/ppermute | solution.py:418
  149.9 3.7 %collective-permute-start.14 = (bf16[4096,128]{1,0:T(8,128)(2,1)S(1)}, bf16[4096,128]{1,0:T(8,128)(2,1)}, u32[]{:S(2)}, u32[]{:S(2)}) collective-permute-start(bf16[4096,128]{1,0:T(8,128)(2,1)S(1)} %slice_bitcast_fusion.w0_ref), channel_id=1, source_target_pairs={{0,1},{1,0},{2,3},{3,2},{4,5},{5,4},{6,7},{7,6},{8,9},{9,8},{10,11... | collective-permute-start | bytes 3145736 | tf_op jit(solution)/shard_map/ppermute | solution.py:385
  153.6 1.9 collective-permute-start.16
  155.6 0.5 fusion.13.order_ref
  156.2 0.1 copy.26
  156.3 0.7 reshape.109.count_ref
  157.0 7.6 %attend_near.1 = (f32[1024,128]{1,0:T(8,128)}, f32[1024,128]{1,0:T(8,128)}) custom-call(s32[8]{0:T(128)} %fusion.13.order_ref, bf16[4,2,192,128]{3,2,1,0:T(8,128)(2,1)} %bitcast.43, bf16[2,2,512,128]{3,2,1,0:T(8,128)(2,1)} %copy-done.5, bf16[2,2,512,128]{3,2,1,0:T(8,128)(2,1)} %collective-permute-done.11.up_ref, ...), custom_call_target="tpu_custom_call" | custom-call | tf_op jit(solution)/shard_map/attend_near/pallas_call | solution.py:305
  164.6 5.6 %attend_far.1 = bf16[2,4,2,72,128]{4,3,2,1,0:T(8,128)(2,1)} custom-call(s32[8]{0:T(128)} %fusion.13.order_ref, bf16[4,2,192,128]{3,2,1,0:T(8,128)(2,1)} %bitcast.44, bf16[2,2,512,128]{3,2,1,0:T(8,128)(2,1)} %collective-permute-done.12.far_ref, bf16[4,8,4,512]{3,2,1,0:T(4,128)(2,1)} %reshape.109.count_ref, f32[1024,128]{1,0:T(8,128)} %get-tuple-element.45.part_ref, ...), custom_call_target="tpu_custom_call" | custom-call | tf_op jit(solution)/shard_map/attend_far/pallas_call | solution.py:321
  170.2 7.7 %all-to-all-start.1 = ((bf16[16,72,128]{2,1,0:T(8,128)(2,1)}), bf16[16,72,128]{2,1,0:T(8,128)(2,1)S(1)}, u32[]{:S(2)}, u32[]{:S(2)}) async-start(bf16[16,72,128]{2,1,0:T(8,128)(2,1)} %bitcast.48), calls=%async_computation.1 | async-start | bytes 589824 | tf_op jit(solution)/shard_map/all_to_all | solution.py:495
  177.9 12.5 %all-to-all-done.1 = bf16[16,72,128]{2,1,0:T(8,128)(2,1)S(1)} async-done(((bf16[16,72,128]{2,1,0:T(8,128)(2,1)}), bf16[16,72,128]{2,1,0:T(8,128)(2,1)S(1)}, u32[]{:S(2)}, u32[]{:S(2)}) %all-to-all-start.1) | async-done | bytes 294944 | tf_op jit(solution)/shard_map/all_to_all | solution.py:495
  190.5 0.7 copy-done.9
  191.2 5.1 %mix.1 = bf16[32,64,128]{2,1,0:T(8,128)(2,1)} custom-call(s32[1]{0:T(128)} %bitcast.place_ref, bf16[2,4,2,72,128]{4,3,2,1,0:T(8,128)(2,1)} %bitcast.49, bf16[4096,128]{1,0:T(8,128)(2,1)} %copy-done.4, bf16[4096,128]{1,0:T(8,128)(2,1)} %collective-permute-done.14.w1_ref, bf16[4096,128]{1,0:T(8,128)(2,1)} %copy-done.10, ...), custom_call_target="tpu_custom_call" | custom-call | tf_op jit(solution)/shard_map/mix/pallas_call | solution.py:364
  196.3 23.3 %all_to_all.15 = bf16[32,64,128]{2,1,0:T(8,128)(2,1)S(1)} all-to-all(bf16[32,64,128]{2,1,0:T(8,128)(2,1)} %mix.1), channel_id=1, replica_groups=mesh['s'=2,'zh'=4,'x'=4,'y'=8,'c'=2] {'s','y','c'}, dimensions={0} | all-to-all | bytes 1048576 | tf_op jit(solution)/shard_map/all_to_all | solution.py:499
  219.6 0.7 reduce_sum.22
  (52 shorter events, 0.4 us)
Async XLA Ops:
  0.0 10.6 %copy-start = (f32[2,4096]{1,0:T(2,128)S(1)}, f32[2,4096]{1,0:T(2,128)}, u32[]{:S(2)}) copy-start(f32[2,4096]{1,0:T(2,128)} %param.12) | copy-start | bytes 98308
  1.8 10.2 %collective-permute-start = (bf16[640,128]{1,0:T(8,128)(2,1)S(1)}, bf16[640,128]{1,0:T(8,128)(2,1)S(1)}, u32[]{:S(2)}, u32[]{:S(2)}) collective-permute-start(bf16[640,128]{1,0:T(8,128)(2,1)S(1)} %pad_maximum_fusion.5), channel_id=1, source_target_pairs={{0,1},{1,0},{2,3},{3,2},{4,5},{5,4},{6,7},{7,6},{8,9},{9,8},{10,11... | collective-permute-start | bytes 491528 | tf_op jit(solution)/shard_map/ppermute | solution.py:385
  14.4 5.2 %copy-start.8 = (bf16[2,640,128]{2,1,0:T(8,128)(2,1)}, bf16[2,640,128]{2,1,0:T(8,128)(2,1)S(1)}, u32[]{:S(2)}) copy-start(bf16[2,640,128]{2,1,0:T(8,128)(2,1)S(1)} %maximum_select_fusion.1.b0_ref) | copy-start | bytes 983044
  14.4 9.0 %collective-permute-start.1 = (bf16[2,640,128]{2,1,0:T(8,128)(2,1)S(1)}, bf16[2,640,128]{2,1,0:T(8,128)(2,1)S(1)}, u32[]{:S(2)}, u32[]{:S(2)}) collective-permute-start(bf16[2,640,128]{2,1,0:T(8,128)(2,1)S(1)} %maximum_select_fusion.1.b0_ref), channel_id=1, source_target_pairs={{0,2},{1,15},{2,0},{3,5},{4,6},{5,3},{6,4},{7,9},{8,10},{9,7},{10,... | collective-permute-start | bytes 983048 | tf_op jit(solution)/shard_map/ppermute | solution.py:418
  17.7 42.4 %collective-permute-start.6 = (bf16[3,2048,128]{2,1,0:T(8,128)(2,1)}, bf16[3,2048,128]{2,1,0:T(8,128)(2,1)}, u32[]{:S(2)}, u32[]{:S(2)}) collective-permute-start(bf16[3,2048,128]{2,1,0:T(8,128)(2,1)} %pad_maximum_fusion.1), channel_id=1, source_target_pairs={{0,256},{256,0},{1,257},{257,1},{2,258},{258,2},{3,259},{259,3},{4... | collective-permute-start | bytes 4718600 | tf_op jit(solution)/shard_map/ppermute | solution.py:385
  23.5 4.6 %copy-start.7 = (bf16[2,640,128]{2,1,0:T(8,128)(2,1)}, bf16[2,640,128]{2,1,0:T(8,128)(2,1)S(1)}, u32[]{:S(2)}) copy-start(bf16[2,640,128]{2,1,0:T(8,128)(2,1)S(1)} %collective-permute-done.1.b1_ref) | copy-start | bytes 983044
  26.0 5.0 %copy-start.14 = (s32[8,128]{1,0:T(8,128)S(1)}, s32[8,128]{1,0:T(8,128)}, u32[]{:S(2)}) copy-start(s32[8,128]{1,0:T(8,128)} %param.9) | copy-start | bytes 12292
  26.1 6.7 %copy-start.1 = (bf16[3,2048,128]{2,1,0:T(8,128)(2,1)}, bf16[3,2048,128]{2,1,0:T(8,128)(2,1)S(1)}, u32[]{:S(2)}) copy-start(bf16[3,2048,128]{2,1,0:T(8,128)(2,1)S(1)} %pad_maximum_fusion.w0_ref.w00_ref.w01_ref) | copy-start | bytes 4718596
  26.1 27.7 %collective-permute-start.5 = (bf16[3,2048,128]{2,1,0:T(8,128)(2,1)S(1)}, bf16[3,2048,128]{2,1,0:T(8,128)(2,1)S(1)}, u32[]{:S(2)}, u32[]{:S(2)}) collective-permute-start(bf16[3,2048,128]{2,1,0:T(8,128)(2,1)S(1)} %pad_maximum_fusion.w0_ref.w00_ref.w01_ref), channel_id=1, source_target_pairs={{0,1},{1,0},{2,3},{3,2},{4,5},{5,4},{6,7},{7,6},{8,9},{9,8},{10,11... | collective-permute-start | bytes 4718600 | tf_op jit(solution)/shard_map/ppermute | solution.py:385
  29.0 11.9 %collective-permute-start.2 = (bf16[2,2,640,128]{3,2,1,0:T(8,128)(2,1)}, bf16[2,2,640,128]{3,2,1,0:T(8,128)(2,1)}, u32[]{:S(2)}, u32[]{:S(2)}) collective-permute-start(bf16[2,2,640,128]{3,2,1,0:T(8,128)(2,1)} %pad_maximum_fusion.2), channel_id=1, source_target_pairs={{0,14},{1,3},{2,4},{3,1},{4,2},{5,7},{6,8},{7,5},{8,6},{9,11},{10,... | collective-permute-start | bytes 1966088 | tf_op jit(solution)/shard_map/ppermute | solution.py:418
  31.0 12.7 %copy-start.16 = (s32[8]{0:T(128)S(1)}, s32[8]{0:T(128)}, u32[]{:S(2)}) copy-start(s32[8]{0:T(128)} %constant.133.clone) | copy-start | bytes 100
  41.0 12.8 %collective-permute-start.3 = (bf16[2,2,640,128]{3,2,1,0:T(8,128)(2,1)}, bf16[2,2,640,128]{3,2,1,0:T(8,128)(2,1)}, u32[]{:S(2)}, u32[]{:S(2)}) collective-permute-start(bf16[2,2,640,128]{3,2,1,0:T(8,128)(2,1)} %collective-permute-done.2.b2_ref), channel_id=1, source_target_pairs={{0,2},{1,15},{2,0},{3,5},{4,6},{5,3},{6,4},{7,9},{8,10},{9,7},{10,... | collective-permute-start | bytes 1966088 | tf_op jit(solution)/shard_map/ppermute | solution.py:418
  53.8 1.2 copy-start.2
  60.2 16.2 %collective-permute-start.7 = (bf16[3,2048,128]{2,1,0:T(8,128)(2,1)}, bf16[3,2048,128]{2,1,0:T(8,128)(2,1)S(1)}, u32[]{:S(2)}, u32[]{:S(2)}) collective-permute-start(bf16[3,2048,128]{2,1,0:T(8,128)(2,1)} %collective-permute-done.6.w0_ref), channel_id=1, source_target_pairs={{0,1},{1,0},{2,3},{3,2},{4,5},{5,4},{6,7},{7,6},{8,9},{9,8},{10,11... | collective-permute-start | bytes 4718600 | tf_op jit(solution)/shard_map/ppermute | solution.py:385
  64.6 11.8 %collective-permute-start.4 = (bf16[2,2,640,128]{3,2,1,0:T(8,128)(2,1)}, bf16[2,2,640,128]{3,2,1,0:T(8,128)(2,1)S(1)}, u32[]{:S(2)}, u32[]{:S(2)}) collective-permute-start(bf16[2,2,640,128]{3,2,1,0:T(8,128)(2,1)} %collective-permute-done.3.b3_ref), channel_id=1, source_target_pairs={{0,14},{1,3},{2,4},{3,1},{4,2},{5,7},{6,8},{7,5},{8,6},{9,11},{10,... | collective-permute-start | bytes 1966088 | tf_op jit(solution)/shard_map/ppermute | solution.py:418
  76.4 0.8 copy-start.11
  76.4 1.4 copy-start.6
  83.6 6.7 %copy-start.17 = (bf16[272,128]{1,0:T(8,128)(2,1)S(1)}, bf16[272,128]{1,0:T(8,128)(2,1)}, u32[]{:S(2)}) copy-start(bf16[272,128]{1,0:T(8,128)(2,1)} %get-tuple-element.39) | copy-start | bytes 208900
  83.6 37.6 %collective-permute-start.9 = (bf16[4,512,128]{2,1,0:T(8,128)(2,1)}, bf16[4,512,128]{2,1,0:T(8,128)(2,1)S(1)}, u32[]{:S(2)}, u32[]{:S(2)}) collective-permute-start(bf16[4,512,128]{2,1,0:T(8,128)(2,1)} %get-tuple-element.42), channel_id=1, source_target_pairs={{0,256},{256,0},{1,257},{257,1},{2,258},{258,2},{3,259},{259,3},{4... | collective-permute-start | bytes 1572872 | tf_op jit(solution)/shard_map/ppermute | solution.py:385
  86.9 63.0 %copy-start.4 = (bf16[4096,128]{1,0:T(8,128)(2,1)}, bf16[4096,128]{1,0:T(8,128)(2,1)S(1)}, u32[]{:S(2)}) copy-start(bf16[4096,128]{1,0:T(8,128)(2,1)S(1)} %slice_bitcast_fusion.w0_ref) | copy-start | bytes 3145732
  86.9 66.7 %collective-permute-start.15 = (bf16[4096,128]{1,0:T(8,128)(2,1)S(1)}, bf16[4096,128]{1,0:T(8,128)(2,1)S(1)}, u32[]{:S(2)}, u32[]{:S(2)}) collective-permute-start(bf16[4096,128]{1,0:T(8,128)(2,1)S(1)} %slice_bitcast_fusion.w0_ref), channel_id=1, source_target_pairs={{0,256},{256,0},{1,257},{257,1},{2,258},{258,2},{3,259},{259,3},{4... | collective-permute-start | bytes 3145736 | tf_op jit(solution)/shard_map/ppermute | solution.py:385
  90.3 30.9 %collective-permute-start.8 = (bf16[272,128]{1,0:T(8,128)(2,1)S(1)}, bf16[272,128]{1,0:T(8,128)(2,1)S(1)}, u32[]{:S(2)}, u32[]{:S(2)}) collective-permute-start(bf16[272,128]{1,0:T(8,128)(2,1)S(1)} %copy-done.17), channel_id=1, source_target_pairs={{0,256},{256,0},{1,257},{257,1},{2,258},{258,2},{3,259},{259,3},{4... | collective-permute-start | bytes 208904 | tf_op jit(solution)/shard_map/ppermute | solution.py:385
  121.2 0.6 copy-start.13
  121.2 0.8 copy-start.12
  124.4 6.2 %collective-permute-start.10 = (bf16[2,512,128]{2,1,0:T(8,128)(2,1)}, bf16[2,512,128]{2,1,0:T(8,128)(2,1)S(1)}, u32[]{:S(2)}, u32[]{:S(2)}) collective-permute-start(bf16[2,512,128]{2,1,0:T(8,128)(2,1)} %get-tuple-element.44), channel_id=1, source_target_pairs={{0,1},{1,0},{2,3},{3,2},{4,5},{5,4},{6,7},{7,6},{8,9},{9,8},{10,11... | collective-permute-start | bytes 786440 | tf_op jit(solution)/shard_map/ppermute | solution.py:385
  131.6 13.0 %copy-start.5 = (bf16[2,2,512,128]{3,2,1,0:T(8,128)(2,1)}, bf16[2,2,512,128]{3,2,1,0:T(8,128)(2,1)S(1)}, u32[]{:S(2)}) copy-start(bf16[2,2,512,128]{3,2,1,0:T(8,128)(2,1)S(1)} %pad_maximum_fusion.3.near_ref) | copy-start | bytes 1572868
  131.6 14.9 %collective-permute-start.11 = (bf16[2,2,512,128]{3,2,1,0:T(8,128)(2,1)S(1)}, bf16[2,2,512,128]{3,2,1,0:T(8,128)(2,1)}, u32[]{:S(2)}, u32[]{:S(2)}) collective-permute-start(bf16[2,2,512,128]{3,2,1,0:T(8,128)(2,1)S(1)} %pad_maximum_fusion.3.near_ref), channel_id=1, source_target_pairs={{0,16},{1,49},{16,0},{17,33},{32,48},{33,17},{48,32},{49,1},{2,18}... | collective-permute-start | bytes 1572872 | tf_op jit(solution)/shard_map/ppermute | solution.py:418
  133.5 22.1 %copy-start.15 = (s32[8]{0:T(128)S(1)}, s32[8]{0:T(128)}, u32[]{:S(2)}) copy-start(s32[8]{0:T(128)} %constant.134.clone) | copy-start | bytes 100
  136.4 19.7 %all-to-all-start = ((bf16[8,192,128]{2,1,0:T(8,128)(2,1)}), bf16[8,192,128]{2,1,0:T(8,128)(2,1)S(1)}, u32[]{:S(2)}, u32[]{:S(2)}) async-start(bf16[8,192,128]{2,1,0:T(8,128)(2,1)} %bitcast.46), calls=%async_computation | async-start | bytes 786432 | tf_op jit(solution)/shard_map/all_to_all | solution.py:479
  144.6 12.5 %collective-permute-start.13 = (bf16[2,2,512,128]{3,2,1,0:T(8,128)(2,1)S(1)}, bf16[2,2,512,128]{3,2,1,0:T(8,128)(2,1)}, u32[]{:S(2)}, u32[]{:S(2)}) collective-permute-start(bf16[2,2,512,128]{3,2,1,0:T(8,128)(2,1)S(1)} %pad_maximum_fusion.3.near_ref), channel_id=1, source_target_pairs={{0,48},{1,17},{16,32},{17,1},{32,16},{33,49},{48,0},{49,33},{2,50}... | collective-permute-start | bytes 1572872 | tf_op jit(solution)/shard_map/ppermute | solution.py:418
  146.5 18.1 %collective-permute-start.12 = (bf16[2,2,512,128]{3,2,1,0:T(8,128)(2,1)}, bf16[2,2,512,128]{3,2,1,0:T(8,128)(2,1)}, u32[]{:S(2)}, u32[]{:S(2)}) collective-permute-start(bf16[2,2,512,128]{3,2,1,0:T(8,128)(2,1)} %collective-permute-done.11.up_ref), channel_id=1, source_target_pairs={{0,48},{1,17},{16,32},{17,1},{32,16},{33,49},{48,0},{49,33},{2,50}... | collective-permute-start | bytes 1572872 | tf_op jit(solution)/shard_map/ppermute | solution.py:418
  149.9 28.0 %collective-permute-start.14 = (bf16[4096,128]{1,0:T(8,128)(2,1)S(1)}, bf16[4096,128]{1,0:T(8,128)(2,1)}, u32[]{:S(2)}, u32[]{:S(2)}) collective-permute-start(bf16[4096,128]{1,0:T(8,128)(2,1)S(1)} %slice_bitcast_fusion.w0_ref), channel_id=1, source_target_pairs={{0,1},{1,0},{2,3},{3,2},{4,5},{5,4},{6,7},{7,6},{8,9},{9,8},{10,11... | collective-permute-start | bytes 3145736 | tf_op jit(solution)/shard_map/ppermute | solution.py:385
  153.6 36.9 %copy-start.10 = (bf16[4096,128]{1,0:T(8,128)(2,1)}, bf16[4096,128]{1,0:T(8,128)(2,1)S(1)}, u32[]{:S(2)}) copy-start(bf16[4096,128]{1,0:T(8,128)(2,1)S(1)} %collective-permute-done.15.w2_ref) | copy-start | bytes 3145732
  153.6 24.3 %collective-permute-start.16 = (bf16[4096,128]{1,0:T(8,128)(2,1)S(1)}, bf16[4096,128]{1,0:T(8,128)(2,1)}, u32[]{:S(2)}, u32[]{:S(2)}) collective-permute-start(bf16[4096,128]{1,0:T(8,128)(2,1)S(1)} %collective-permute-done.15.w2_ref), channel_id=1, source_target_pairs={{0,1},{1,0},{2,3},{3,2},{4,5},{5,4},{6,7},{7,6},{8,9},{9,8},{10,11... | collective-permute-start | bytes 3145736 | tf_op jit(solution)/shard_map/ppermute | solution.py:385
  156.1 0.9 copy-start.3
  170.2 20.2 %all-to-all-start.1 = ((bf16[16,72,128]{2,1,0:T(8,128)(2,1)}), bf16[16,72,128]{2,1,0:T(8,128)(2,1)S(1)}, u32[]{:S(2)}, u32[]{:S(2)}) async-start(bf16[16,72,128]{2,1,0:T(8,128)(2,1)} %bitcast.48), calls=%async_computation.1 | async-start | bytes 589824 | tf_op jit(solution)/shard_map/all_to_all | solution.py:495
  190.5 0.7 copy-start.9
